TPU v7x, 128 devices: a whole 4x4x4 slice. The times are simulated.
128 devices in a mesh: dp: 8 (over z, core), expert: 16 (over x, y).
Axes of the slice: x: 4, y: 4, z: 4, core: 2. Of those that a mesh axis runs over, the one named last changes fastest.
Arguments:
- tokens: bfloat16 [4096, 2048], P(('dp', 'expert')), may hold values from -6 to 6
- norm_gain: float32 [2, 2048], replicated, may hold values from 0.5 to 1.5
- routes: int32 [2, 4096, 8], P(None, ('dp', 'expert')), may hold values from 0 to 127, all different within a row; in each aligned block of 32 rows (0 to 31, 32 to 63, ..., all dimensions but the last counted through in order) at most 3 rows name the same one
- gates: float32 [2, 4096, 8], P(None, ('dp', 'expert')), may hold values from 0.03 to 0.3
- placement: int32 [2, 128], replicated, may hold values from 0 to 127, each once within a row
- w_in: bfloat16 [2, 128, 2048, 1536], P(None, ('dp', 'expert')), may hold values from -0.125 to 0.125
- in_scale: float32 [2, 128, 16, 12], P(None, ('dp', 'expert')), may hold values from 0.5 to 2
- w_out: bfloat16 [2, 128, 768, 2048], P(None, ('dp', 'expert')), may hold values from -0.21875 to 0.21875
- out_scale: float32 [2, 128, 6, 16], P(None, ('dp', 'expert')), may hold values from 0.5 to 2
Outputs:
- stream: bfloat16 [4096, 2048], P(('dp', 'expert'))
Inputs may be any that keep to these rules, and one draw needn't show every extreme that they name: `routes`: each token names 8 different experts in each layer; among the tokens of one device in one layer no expert is named more than 3 times, a bound that some block reaches. `placement`: each layer's row is a permutation of the experts; device position p is p's index along dp+expert, dp slowest.
All inputs are finite; a program needn't handle non-finite values.
Results may differ from a plain program's by a relative error of at most 0.009.
Values may be sent and summed in bfloat16 or wider, within the bound.
No kernel may reach another device: no remote copies, remote signals or barrier semaphores. Data moves between devices by JAX's collectives and lax.ppermute only.
A program may use at most 128 MiB of HBM per device.

v0:
```python
import jax
import jax.numpy as jnp
from jax import lax
from jax.sharding import PartitionSpec as P

QBLK = 128


epsilon = 1e-06


def dequantize(quantized, scales, block_size):
    widened = jnp.repeat(jnp.repeat(scales, block_size, axis=0), block_size, axis=1)
    return (quantized.astype(jnp.float32) * widened).astype(jnp.bfloat16)


def shards(tokens, norm_gain, routes, gates, placement, w_in, in_scale, w_out, out_scale):
    tok_count = tokens.shape[0]
    width = tokens.shape[1]
    fanout = routes.shape[2]
    experts_all = placement.shape[1]
    capacity = max(2, 3 * tok_count * fanout // (2 * experts_all))
    hidden_width = w_out.shape[2]
    expert_ids = jnp.arange(experts_all, dtype=jnp.int32)
    slot_ids = jnp.arange(experts_all * capacity, dtype=jnp.int32)
    stream = tokens
    for layer_index in range(w_in.shape[0]):
        stream_f = stream.astype(jnp.float32)
        normed = (
            stream_f
            * lax.rsqrt(jnp.mean(stream_f * stream_f, axis=-1, keepdims=True) + epsilon)
            * norm_gain[layer_index]
        ).astype(jnp.bfloat16)
        in_weight = dequantize(w_in[layer_index, 0], in_scale[layer_index, 0], QBLK)
        out_weight = dequantize(w_out[layer_index, 0], out_scale[layer_index, 0], QBLK)
        matches = (placement[layer_index][:, None] == expert_ids[None, :]).astype(jnp.int32)
        holder = jnp.sum(matches * expert_ids[:, None], axis=0)
        chosen = routes[layer_index].reshape(-1)
        onehot = (chosen[:, None] == expert_ids[None, :]).astype(jnp.int32)
        ranks = jnp.sum((jnp.cumsum(onehot, axis=0) - 1) * onehot, axis=1)
        target = jnp.sum(onehot * holder[None, :], axis=1)
        slot_rows = target * capacity + ranks
        selector = (slot_rows[:, None] == slot_ids[None, :]).astype(jnp.bfloat16)
        spread = jnp.sum(
            selector.reshape(tok_count, fanout, -1).astype(jnp.float32), axis=1
        ).astype(jnp.bfloat16)
        outgoing = lax.dot_general(
            spread, normed, (((0,), (0,)), ((), ())), preferred_element_type=jnp.float32
        ).astype(jnp.bfloat16)
        outgoing = outgoing.reshape(experts_all, capacity, width)
        arrived = lax.all_to_all(
            outgoing, ("dp", "expert"), split_axis=0, concat_axis=0, tiled=True
        )
        arrived_shape = arrived.shape
        token_rows = arrived.reshape(-1, width)
        gate_up = jnp.dot(token_rows, in_weight, preferred_element_type=jnp.float32)
        hidden = (jax.nn.silu(gate_up[:, :hidden_width]) * gate_up[:, hidden_width:]).astype(
            jnp.bfloat16
        )
        answer = jnp.dot(hidden, out_weight, preferred_element_type=jnp.float32).astype(
            jnp.bfloat16
        )
        returned = lax.all_to_all(
            answer.reshape(arrived_shape), ("dp", "expert"), split_axis=0, concat_axis=0, tiled=True
        )
        back_rows = jnp.dot(
            selector, returned.reshape(-1, width), preferred_element_type=jnp.float32
        )
        back_rows = back_rows.reshape(tok_count, fanout, width)
        mixed = jnp.sum(back_rows * gates[layer_index][:, :, None], axis=1)
        stream = (stream_f + mixed).astype(jnp.bfloat16)
    return stream


def solution(mesh):
    return jax.shard_map(
        shards,
        mesh=mesh,
        in_specs=(
            P(("dp", "expert"), None),
            P(),
            P(None, ("dp", "expert"), None),
            P(None, ("dp", "expert"), None),
            P(),
            P(None, ("dp", "expert"), None, None),
            P(None, ("dp", "expert"), None, None),
            P(None, ("dp", "expert"), None, None),
            P(None, ("dp", "expert"), None, None),
        ),
        out_specs=P(("dp", "expert"), None),
        check_vma=False,
    )
```

profile of v0, /device:TPU:1, one launch (start us, length us, event | category | flops | bytes accessed | tf_op | source)
XLA Modules:
  0.0 202.2 jit_solution(1924677977317934338)
XLA Ops:
  8.6 11.5 %all-to-all-start = ((bf16[128,3,2048]{2,1,0:T(4,128)(2,1)}), bf16[128,3,2048]{2,1,0:T(4,128)(2,1)S(1)}, u32[]{:S(2)}, u32[]{:S(2)}) async-start(bf16[128,3,2048]{2,1,0:T(4,128)(2,1)} %reshape.229), calls=%async_computation | async-start | bytes 4194304 | tf_op jit(solution)/shard_map/all_to_all | solution.py:51
  20.1 10.2 %fusion.61 = (bf16[1,1,2048,1536]{3,2,1,0:T(8,128)(2,1)}, bf16[1,1,2048,1536]{3,2,1,0:T(8,128)(2,1)}) fusion(bf16[2,1,2048,1536]{3,2,1,0:T(8,128)(2,1)} %param.14), kind=kLoop, calls=%fused_computation.98 | loop fusion | bytes 25165824 | tf_op jit(solution)/shard_map/slice | solution.py:34
  30.5 8.6 %copy.46 = bf16[1,1,2048,1536]{2,3,1,0:T(8,128)(2,1)} copy(bf16[1,1,2048,1536]{3,2,1,0:T(8,128)(2,1)} %get-tuple-element.12) | data formatting | bytes 12582912
  39.2 7.7 %fusion.1 = bf16[2048,12,128]{0,2,1:T(8,128)(2,1)} fusion(bf16[2048,12,128]{0,2,1:T(8,128)(2,1)} %bitcast.100, f32[2048,12]{0,1:T(8,128)S(1)} %bitcast.108), kind=kLoop, calls=%fused_computation.3 | loop fusion | flops 9437184 | bytes 12681216 | tf_op jit(solution)/shard_map/convert_element_type | solution.py:14
  46.8 3.0 %all-to-all-done = bf16[128,3,2048]{2,1,0:T(4,128)(2,1)S(1)} async-done(((bf16[128,3,2048]{2,1,0:T(4,128)(2,1)}), bf16[128,3,2048]{2,1,0:T(4,128)(2,1)S(1)}, u32[]{:S(2)}, u32[]{:S(2)}) %all-to-all-start) | async-done | bytes 1572896 | tf_op jit(solution)/shard_map/all_to_all | solution.py:51
  49.9 2.5 %reshape.230 = bf16[384,2048]{1,0:T(8,128)(2,1)} reshape(bf16[128,3,2048]{2,1,0:T(4,128)(2,1)S(1)} %all-to-all-done) | data formatting | bytes 3145728 | tf_op jit(solution)/shard_map/reshape | solution.py:55
  52.4 5.2 %fusion.66 = f32[384,1536]{1,0:T(8,128)S(1)} fusion(bf16[384,2048]{1,0:T(8,128)(2,1)} %reshape.230, bf16[2048,1536]{0,1:T(8,128)(2,1)} %bitcast.102), kind=kOutput, calls=%fused_computation.103 | convolution fusion | flops 2415919104 | bytes 10223616 | tf_op jit(solution)/shard_map/dot_general | solution.py:56
  59.4 4.7 %fusion.15 = bf16[384,2048]{1,0:T(8,128)(2,1)S(1)} fusion(f32[96,8,16,128]{3,2,1,0:T(8,128)S(1)} %bitcast.104, bf16[2,1,768,2048]{3,2,1,0:T(8,128)(2,1)} %param.16, f32[384,1536]{1,0:T(8,128)S(1)} %fusion.66), kind=kOutput, calls=%fused_computation.15 | convolution fusion | flops 1215234048 | bytes 13369344 | tf_op jit(solution)/shard_map/dot_general | solution.py:60
  66.5 6.8 %all-to-all-start.1 = ((bf16[128,3,2048]{2,1,0:T(4,128)(2,1)}), bf16[128,3,2048]{2,1,0:T(4,128)(2,1)S(1)}, u32[]{:S(2)}, u32[]{:S(2)}) async-start(bf16[128,3,2048]{2,1,0:T(4,128)(2,1)} %reshape.234), calls=%async_computation.1 | async-start | bytes 4194304 | tf_op jit(solution)/shard_map/all_to_all | solution.py:63
  74.6 28.4 %all-to-all-done.1 = bf16[128,3,2048]{2,1,0:T(4,128)(2,1)S(1)} async-done(((bf16[128,3,2048]{2,1,0:T(4,128)(2,1)}), bf16[128,3,2048]{2,1,0:T(4,128)(2,1)S(1)}, u32[]{:S(2)}, u32[]{:S(2)}) %all-to-all-start.1) | async-done | bytes 1572896 | tf_op jit(solution)/shard_map/all_to_all | solution.py:63
  103.1 2.5 %reshape.248 = bf16[384,2048,1]{1,0,2:T(8,128)(2,1)} reshape(bf16[128,3,2048]{2,1,0:T(4,128)(2,1)S(1)} %all-to-all-done.1) | data formatting | bytes 3145728 | tf_op jit(solution)/shard_map/reshape | solution.py:67
  105.6 2.4 %fusion.18 = f32[32,2048]{1,0:T(8,128)S(1)} fusion(bf16[384,2048,1]{1,0,2:T(8,128)(2,1)} %reshape.248, f32[32,8]{1,0:T(8,128)S(1)} %copy.36, s32[32,8]{1,0:T(8,128)S(1)} %add.56), kind=kOutput, calls=%fused_computation.20 | convolution fusion | flops 403734528 | bytes 1837056 | tf_op jit(solution)/shard_map/dot_general | solution.py:66
  108.8 2.4 %reshape.237 = bf16[128,3,2048]{2,1,0:T(4,128)(2,1)} reshape(bf16[384,2048]{1,0:T(8,128)(2,1)S(1)} %convolution_convert_fusion) | data formatting | bytes 3145728 | tf_op jit(solution)/shard_map/reshape | solution.py:50
  111.2 4.5 %all-to-all-start.2 = ((bf16[128,3,2048]{2,1,0:T(4,128)(2,1)}), bf16[128,3,2048]{2,1,0:T(4,128)(2,1)S(1)}, u32[]{:S(2)}, u32[]{:S(2)}) async-start(bf16[128,3,2048]{2,1,0:T(4,128)(2,1)} %reshape.237), calls=%async_computation.2 | async-start | bytes 4194304 | tf_op jit(solution)/shard_map/all_to_all | solution.py:51
  115.9 8.7 %copy.48 = bf16[1,1,2048,1536]{2,3,1,0:T(8,128)(2,1)} copy(bf16[1,1,2048,1536]{3,2,1,0:T(8,128)(2,1)} %get-tuple-element.11) | data formatting | bytes 12582912
  124.5 7.7 %fusion = bf16[2048,12,128]{0,2,1:T(8,128)(2,1)} fusion(bf16[2048,12,128]{0,2,1:T(8,128)(2,1)} %bitcast.101, f32[2048,12]{0,1:T(8,128)S(1)} %bitcast.109), kind=kLoop, calls=%fused_computation.1 | loop fusion | flops 9437184 | bytes 12681216 | tf_op jit(solution)/shard_map/convert_element_type | solution.py:14
  132.2 13.3 %all-to-all-done.2 = bf16[128,3,2048]{2,1,0:T(4,128)(2,1)S(1)} async-done(((bf16[128,3,2048]{2,1,0:T(4,128)(2,1)}), bf16[128,3,2048]{2,1,0:T(4,128)(2,1)S(1)}, u32[]{:S(2)}, u32[]{:S(2)}) %all-to-all-start.2) | async-done | bytes 1572896 | tf_op jit(solution)/shard_map/all_to_all | solution.py:51
  145.6 2.5 %reshape.238 = bf16[384,2048]{1,0:T(8,128)(2,1)} reshape(bf16[128,3,2048]{2,1,0:T(4,128)(2,1)S(1)} %all-to-all-done.2) | data formatting | bytes 3145728 | tf_op jit(solution)/shard_map/reshape | solution.py:55
  148.1 5.2 %fusion.67 = f32[384,1536]{1,0:T(8,128)S(1)} fusion(bf16[384,2048]{1,0:T(8,128)(2,1)} %reshape.238, bf16[2048,1536]{0,1:T(8,128)(2,1)} %bitcast.103), kind=kOutput, calls=%fused_computation.104 | convolution fusion | flops 2415919104 | bytes 10223616 | tf_op jit(solution)/shard_map/dot_general | solution.py:56
  155.1 4.7 %fusion.12 = bf16[384,2048]{1,0:T(8,128)(2,1)S(1)} fusion(f32[96,8,16,128]{3,2,1,0:T(8,128)S(1)} %bitcast.105, bf16[2,1,768,2048]{3,2,1,0:T(8,128)(2,1)} %param.16, f32[384,1536]{1,0:T(8,128)S(1)} %fusion.67), kind=kOutput, calls=%fused_computation.14 | convolution fusion | flops 1215234048 | bytes 13369344 | tf_op jit(solution)/shard_map/dot_general | solution.py:60
  162.2 4.5 %all-to-all-start.3 = ((bf16[128,3,2048]{2,1,0:T(4,128)(2,1)}), bf16[128,3,2048]{2,1,0:T(4,128)(2,1)S(1)}, u32[]{:S(2)}, u32[]{:S(2)}) async-start(bf16[128,3,2048]{2,1,0:T(4,128)(2,1)} %reshape.242), calls=%async_computation.3 | async-start | bytes 4194304 | tf_op jit(solution)/shard_map/all_to_all | solution.py:63
  166.8 29.8 %all-to-all-done.3 = bf16[128,3,2048]{2,1,0:T(4,128)(2,1)S(1)} async-done(((bf16[128,3,2048]{2,1,0:T(4,128)(2,1)}), bf16[128,3,2048]{2,1,0:T(4,128)(2,1)S(1)}, u32[]{:S(2)}, u32[]{:S(2)}) %all-to-all-start.3) | async-done | bytes 1572896 | tf_op jit(solution)/shard_map/all_to_all | solution.py:63
  196.6 2.5 %reshape.249 = bf16[384,2048,1]{1,0,2:T(8,128)(2,1)} reshape(bf16[128,3,2048]{2,1,0:T(4,128)(2,1)S(1)} %all-to-all-done.3) | data formatting | bytes 3145728 | tf_op jit(solution)/shard_map/reshape | solution.py:67
  199.1 2.4 %fusion.19 = f32[32,2048]{1,0:T(8,128)S(1)} fusion(bf16[384,2048,1]{1,0,2:T(8,128)(2,1)} %reshape.249, f32[32,8]{1,0:T(8,128)S(1)} %copy.43, s32[32,8]{1,0:T(8,128)S(1)} %add.61), kind=kOutput, calls=%fused_computation.21 | convolution fusion | flops 403734528 | bytes 1837056 | tf_op jit(solution)/shard_map/dot_general | solution.py:66
  (67 shorter events, 20.0 us)
Async XLA Ops:
  8.6 11.5 %copy-start.1 = (f32[2,1,16,12]{2,1,3,0:T(1,128)S(1)}, f32[2,1,16,12]{2,1,3,0:T(1,128)}, u32[]{:S(2)}) copy-start(f32[2,1,16,12]{2,1,3,0:T(1,128)} %param.15) | copy-start | bytes 4612
  8.6 41.3 %all-to-all-start = ((bf16[128,3,2048]{2,1,0:T(4,128)(2,1)}), bf16[128,3,2048]{2,1,0:T(4,128)(2,1)S(1)}, u32[]{:S(2)}, u32[]{:S(2)}) async-start(bf16[128,3,2048]{2,1,0:T(4,128)(2,1)} %reshape.229), calls=%async_computation | async-start | bytes 4194304 | tf_op jit(solution)/shard_map/all_to_all | solution.py:51
  30.5 8.6 %copy-start.3 = (f32[2,1,6,16]{3,1,2,0:T(1,128)S(1)}, f32[2,1,6,16]{3,1,2,0:T(1,128)}, u32[]{:S(2)}) copy-start(f32[2,1,6,16]{3,1,2,0:T(1,128)} %param.17) | copy-start | bytes 2308
  66.5 7.0 %copy-start.2 = (f32[2,32,8]{1,2,0:T(8,128)S(1)}, f32[2,32,8]{1,2,0:T(8,128)}, u32[]{:S(2)}) copy-start(f32[2,32,8]{1,2,0:T(8,128)} %param.12) | copy-start | bytes 6148
  66.5 36.5 %all-to-all-start.1 = ((bf16[128,3,2048]{2,1,0:T(4,128)(2,1)}), bf16[128,3,2048]{2,1,0:T(4,128)(2,1)S(1)}, u32[]{:S(2)}, u32[]{:S(2)}) async-start(bf16[128,3,2048]{2,1,0:T(4,128)(2,1)} %reshape.234), calls=%async_computation.1 | async-start | bytes 4194304 | tf_op jit(solution)/shard_map/all_to_all | solution.py:63
  105.6 2.5 %copy-start = (bf16[32,2048]{1,0:T(8,128)(2,1)S(1)}, bf16[32,2048]{1,0:T(8,128)(2,1)}, u32[]{:S(2)}) copy-start(bf16[32,2048]{1,0:T(8,128)(2,1)} %param.9) | copy-start | bytes 393220
  111.2 34.4 %all-to-all-start.2 = ((bf16[128,3,2048]{2,1,0:T(4,128)(2,1)}), bf16[128,3,2048]{2,1,0:T(4,128)(2,1)S(1)}, u32[]{:S(2)}, u32[]{:S(2)}) async-start(bf16[128,3,2048]{2,1,0:T(4,128)(2,1)} %reshape.237), calls=%async_computation.2 | async-start | bytes 4194304 | tf_op jit(solution)/shard_map/all_to_all | solution.py:51
  162.2 34.3 %all-to-all-start.3 = ((bf16[128,3,2048]{2,1,0:T(4,128)(2,1)}), bf16[128,3,2048]{2,1,0:T(4,128)(2,1)S(1)}, u32[]{:S(2)}, u32[]{:S(2)}) async-start(bf16[128,3,2048]{2,1,0:T(4,128)(2,1)} %reshape.242), calls=%async_computation.3 | async-start | bytes 4194304 | tf_op jit(solution)/shard_map/all_to_all | solution.py:63
where the time goes:
time: 203 us; the launch traced here: 202 us
  waiting for transfers between devices  74.6 us (37%)
  local copies, waits for them, and re-layouts  54.3 us (27%)
  starting transfers between devices  27.2 us (13%)
  matrix products  27 us (13%)
  other arithmetic  18.9 us (9%)
    all_to_all x2, waiting for transfers between devices, shards(): lax.all_to_all(answer.reshape(arrived_shape), ('dp', 'expert'), split_axi...  58.2 us
    unnamed x17, local copies, waits for them, and re-layouts  17.6 us
    all_to_all x2, waiting for transfers between devices, shards(): lax.all_to_all(outgoing, ('dp', 'expert'), split_axis=0, concat_axis=0, t...  16.4 us
    all_to_all x2, starting transfers between devices, shards(): lax.all_to_all(outgoing, ('dp', 'expert'), split_axis=0, concat_axis=0, t...  16 us
    convert_element_type x2, other arithmetic, dequantize(): return (quantized.astype(jnp.float32) * widened).astype(jnp.bfloat16)  15.4 us
    all_to_all x2, starting transfers between devices, shards(): lax.all_to_all(answer.reshape(arrived_shape), ('dp', 'expert'), split_axi...  11.2 us
    dot_general x2, matrix products, shards(): gate_up = jnp.dot(token_rows, in_weight, preferred_element_type=jnp.float32)  10.5 us
    slice x2, local copies, waits for them, and re-layouts, shards(): in_weight = dequantize(w_in[layer_index, 0], in_scale[layer_index, 0], QBLK)  10.2 us
  transfers between devices with their start and end apart: 4, of which 4 were waited for; matrix products, arithmetic and copies ran while one was open for 22% of the time, Pallas kernels for 0%

commit v1 on v0

v1 whole, which is shorter than its diff:
```python
import functools

import jax
import jax.numpy as jnp
from jax import lax
from jax.experimental import pallas as pl
from jax.experimental.pallas import tpu as pltpu
from jax.sharding import PartitionSpec as P

AXES = ("dp", "expert")
QBLK = 128
CAP = 3
PIECES = 8
GROUP = 32
EPS = 1e-06
MIB = 1 << 20


def fold_matrix():
    row = lax.broadcasted_iota(jnp.int32, (GROUP * PIECES, GROUP * PIECES), 0)
    col = lax.broadcasted_iota(jnp.int32, (GROUP * PIECES, GROUP * PIECES), 1)
    return jnp.where(col == (row & (PIECES - 1)) * GROUP + (row >> 3), 1.0, 0.0).astype(jnp.bfloat16)


def unfold_matrix():
    row = lax.broadcasted_iota(jnp.int32, (GROUP * PIECES, GROUP * PIECES), 0)
    col = lax.broadcasted_iota(jnp.int32, (GROUP * PIECES, GROUP * PIECES), 1)
    return jnp.where(col == (row & (GROUP - 1)) * PIECES + (row >> 5), 1.0, 0.0).astype(jnp.bfloat16)


def unfold_rows(slab_ref, rows_ref):
    piece = slab_ref.shape[1]
    span = GROUP * PIECES
    unfold = unfold_matrix()
    for b in range(slab_ref.shape[0] // span):
        block = jnp.dot(
            unfold, slab_ref[b * span : (b + 1) * span, :], preferred_element_type=jnp.float32
        ).astype(jnp.bfloat16)
        for p in range(PIECES):
            rows_ref[b * GROUP : (b + 1) * GROUP, p * piece : (p + 1) * piece] = block[
                p * GROUP : (p + 1) * GROUP
            ]


def fold_rows(stack_ref, slab_ref):
    span = GROUP * PIECES
    fold = fold_matrix()
    for b in range(slab_ref.shape[0] // span):
        slab_ref[b * span : (b + 1) * span, :] = jnp.dot(
            fold, stack_ref[b * span : (b + 1) * span, :], preferred_element_type=jnp.float32
        ).astype(jnp.bfloat16)


def stack_piece(stack_ref, values, p):
    span = GROUP * PIECES
    for b in range(values.shape[0] // GROUP):
        stack_ref[b * span + p * GROUP : b * span + (p + 1) * GROUP, :] = values[
            b * GROUP : (b + 1) * GROUP
        ]


def slot_tables(routes_t, place_row, gates_t):
    tokens = routes_t.shape[1]
    devices = place_row.shape[1]
    slots = devices * CAP
    home = lax.broadcasted_iota(jnp.int32, (devices, slots), 0)
    slot = lax.broadcasted_iota(jnp.int32, (devices, slots), 1)
    low = home * CAP
    widen = jnp.where((slot >= low) & (slot < low + CAP), 1.0, 0.0).astype(jnp.bfloat16)
    place = jnp.dot(
        jnp.broadcast_to(place_row.astype(jnp.float32), (8, devices)).astype(jnp.bfloat16),
        widen,
        preferred_element_type=jnp.float32,
    )[:1]
    rank_of = jnp.dot(
        jnp.broadcast_to(
            lax.broadcasted_iota(jnp.int32, (1, devices), 1).astype(jnp.float32), (8, devices)
        ).astype(jnp.bfloat16),
        widen,
        preferred_element_type=jnp.float32,
    )[:1]
    order = lax.broadcasted_iota(jnp.int32, (1, slots), 1).astype(jnp.float32) - rank_of * CAP
    chosen = jnp.transpose(routes_t.astype(jnp.float32))
    gate = None if gates_t is None else jnp.transpose(gates_t)
    taken = jnp.zeros((tokens, slots), jnp.float32)
    weight = jnp.zeros((tokens, slots), jnp.float32)
    for k in range(chosen.shape[1]):
        same = chosen[:, k : k + 1] == place
        taken = jnp.where(same, 1.0, taken)
        if gate is not None:
            weight = jnp.where(same, gate[:, k : k + 1], weight)
    later = lax.broadcasted_iota(jnp.int32, (tokens, tokens), 0)
    earlier = lax.broadcasted_iota(jnp.int32, (tokens, tokens), 1)
    before = jnp.where(earlier < later, 1.0, 0.0).astype(jnp.bfloat16)
    ranks = jnp.dot(before, taken.astype(jnp.bfloat16), preferred_element_type=jnp.float32)
    mine = ranks == order
    return jnp.where(mine, taken, 0.0), jnp.where(mine, weight, 0.0)


def normalise(stream_f, gain):
    scale = lax.rsqrt(jnp.mean(stream_f * stream_f, axis=-1, keepdims=True) + EPS)
    return (stream_f * scale * gain).astype(jnp.bfloat16)


def send_rows(select, normed, stack_ref, slab_ref):
    piece = slab_ref.shape[1]
    pick = jnp.transpose(select).astype(jnp.bfloat16)
    for p in range(PIECES):
        rows = jnp.dot(
            pick, normed[:, p * piece : (p + 1) * piece], preferred_element_type=jnp.float32
        ).astype(jnp.bfloat16)
        stack_piece(stack_ref, rows, p)
    fold_rows(stack_ref, slab_ref)


def mix(weight, slab_ref, rows_ref):
    unfold_rows(slab_ref, rows_ref)
    high = weight.astype(jnp.bfloat16)
    low = (weight - high.astype(jnp.float32)).astype(jnp.bfloat16)
    both = jnp.dot(
        jnp.concatenate([high, low], axis=0), rows_ref[...], preferred_element_type=jnp.float32
    )
    tokens = weight.shape[0]
    return both[:tokens] + both[tokens:]


def first_kernel(tokens_ref, gain_ref, routes_ref, place_ref, slab_ref, stack_ref):
    select, _ = slot_tables(routes_ref[0], place_ref[0:1, :], None)
    normed = normalise(tokens_ref[...].astype(jnp.float32), gain_ref[0:1, :])
    send_rows(select, normed, stack_ref, slab_ref)


def middle_kernel(
    layer, slab_in, stream_ref, gain_ref, routes_ref, gates_ref, place_ref,
    slab_ref, out_ref, rows_ref, stack_ref,
):
    _, weight = slot_tables(routes_ref[layer], place_ref[layer : layer + 1, :], gates_ref[layer])
    select, _ = slot_tables(routes_ref[layer + 1], place_ref[layer + 1 : layer + 2, :], None)
    mixed = mix(weight, slab_in, rows_ref)
    stream = (stream_ref[...].astype(jnp.float32) + mixed).astype(jnp.bfloat16)
    out_ref[...] = stream
    normed = normalise(stream.astype(jnp.float32), gain_ref[layer + 1 : layer + 2, :])
    send_rows(select, normed, stack_ref, slab_ref)


def last_kernel(
    layer, slab_in, stream_ref, routes_ref, gates_ref, place_ref, out_ref, rows_ref
):
    _, weight = slot_tables(routes_ref[layer], place_ref[layer : layer + 1, :], gates_ref[layer])
    mixed = mix(weight, slab_in, rows_ref)
    out_ref[...] = (stream_ref[...].astype(jnp.float32) + mixed).astype(jnp.bfloat16)


def dequant_kernel(scale_ref, w_ref, out_ref):
    layer, step = pl.program_id(0), pl.program_id(1)
    rows, cols = out_ref.shape[1], out_ref.shape[2]
    per_step = rows // QBLK
    for i in range(per_step):
        for j in range(cols // QBLK):
            scale = scale_ref[layer, step * per_step + i, j]
            at = (slice(i * QBLK, (i + 1) * QBLK), slice(j * QBLK, (j + 1) * QBLK))
            out_ref[(0,) + at] = (w_ref[(0, 0) + at].astype(jnp.float32) * scale).astype(
                jnp.bfloat16
            )


def dequant(weights, scales):
    layers, _, height, width = weights.shape
    block = 256
    return pl.pallas_call(
        dequant_kernel,
        grid=(layers, height // block),
        in_specs=[
            pl.BlockSpec(memory_space=pltpu.SMEM),
            pl.BlockSpec((1, 1, block, width), lambda l, i: (l, 0, i, 0)),
        ],
        out_specs=pl.BlockSpec((1, block, width), lambda l, i: (l, i, 0)),
        out_shape=jax.ShapeDtypeStruct((layers, height, width), jnp.bfloat16),
        cost_estimate=pl.CostEstimate(
            flops=weights.size, bytes_accessed=4 * weights.size, transcendentals=0
        ),
        name="dequant",
    )(scales[:, 0], weights)


def expert_kernel(
    layer, slab_in, win_hbm, wout_hbm, slab_ref, x_ref, win, wout, hid, stack_ref, sems
):
    width, gated = win.shape
    ff = gated // 2
    chunk = 256
    loads = []
    for n in range(ff // chunk):
        for half in range(2):
            cols = pl.ds(half * ff + n * chunk, chunk)
            loads.append(
                pltpu.make_async_copy(
                    win_hbm.at[layer, :, cols], win.at[:, cols], sems.at[len(loads)]
                )
            )
    for m in range(PIECES):
        cols = pl.ds(m * chunk, chunk)
        loads.append(
            pltpu.make_async_copy(
                wout_hbm.at[layer, :, cols], wout.at[:, cols], sems.at[len(loads)]
            )
        )
    for load in loads:
        load.start()
    unfold_rows(slab_in, x_ref)
    at = 0
    for n in range(ff // chunk):
        loads[at].wait()
        gate = jnp.dot(
            x_ref[...], win[:, n * chunk : (n + 1) * chunk], preferred_element_type=jnp.float32
        )
        loads[at + 1].wait()
        up = jnp.dot(
            x_ref[...],
            win[:, ff + n * chunk : ff + (n + 1) * chunk],
            preferred_element_type=jnp.float32,
        )
        at += 2
        hid[:, n * chunk : (n + 1) * chunk] = (gate / (1.0 + jnp.exp(-gate)) * up).astype(
            jnp.bfloat16
        )
    for m in range(PIECES):
        loads[at].wait()
        at += 1
        answer = jnp.dot(
            hid[...], wout[:, m * chunk : (m + 1) * chunk], preferred_element_type=jnp.float32
        ).astype(jnp.bfloat16)
        stack_piece(stack_ref, answer, m)
    fold_rows(stack_ref, slab_ref)


VM = pl.BlockSpec(memory_space=pltpu.VMEM)


def expert(layer, slab, in_weight, out_weight):
    rows, piece = slab.shape
    slots = rows // PIECES
    _, width, gated = in_weight.shape
    ff = gated // 2
    return pl.pallas_call(
        functools.partial(expert_kernel, layer),
        in_specs=[VM, pl.BlockSpec(memory_space=pl.ANY), pl.BlockSpec(memory_space=pl.ANY)],
        out_specs=VM,
        out_shape=jax.ShapeDtypeStruct(slab.shape, jnp.bfloat16),
        scratch_shapes=[
            pltpu.VMEM((slots, width), jnp.bfloat16),
            pltpu.VMEM((width, gated), jnp.bfloat16),
            pltpu.VMEM((ff, width), jnp.bfloat16),
            pltpu.VMEM((slots, ff), jnp.bfloat16),
            pltpu.VMEM(slab.shape, jnp.bfloat16),
            pltpu.SemaphoreType.DMA((2 * (ff // 256) + PIECES,)),
        ],
        compiler_params=pltpu.CompilerParams(vmem_limit_bytes=40 * MIB),
        cost_estimate=pl.CostEstimate(
            flops=6 * slots * width * ff,
            bytes_accessed=6 * width * ff + 4 * slots * width,
            transcendentals=slots * ff,
        ),
        name="expert",
    )(slab, in_weight, out_weight)


def exchange(slab, devices):
    split = slab.reshape(devices, slab.shape[0] // devices, slab.shape[1])
    moved = lax.all_to_all(split, AXES, split_axis=0, concat_axis=0, tiled=True)
    return moved.reshape(slab.shape)


def shards(tokens, norm_gain, routes, gates, placement, w_in, in_scale, w_out, out_scale):
    count, width = tokens.shape
    layers, devices = placement.shape
    slots = devices * CAP
    piece = width // PIECES
    routes_t = jnp.swapaxes(routes, 1, 2)
    gates_t = jnp.swapaxes(gates, 1, 2)
    slab_type = jax.ShapeDtypeStruct((slots * PIECES, piece), jnp.bfloat16)
    stream_type = jax.ShapeDtypeStruct((count, width), jnp.bfloat16)
    rows = pltpu.VMEM((slots, width), jnp.bfloat16)
    stack = pltpu.VMEM((slots * PIECES, piece), jnp.bfloat16)
    params = pltpu.CompilerParams(vmem_limit_bytes=24 * MIB)

    slab = pl.pallas_call(
        first_kernel,
        in_specs=[VM] * 4,
        out_specs=VM,
        out_shape=slab_type,
        scratch_shapes=[stack],
        compiler_params=params,
        name="first",
    )(tokens, norm_gain, routes_t, placement)
    in_weight = dequant(w_in, in_scale)
    out_weight = dequant(w_out, out_scale)
    stream = tokens
    for layer in range(layers):
        answers = expert(layer, exchange(slab, devices), in_weight, out_weight)
        back = exchange(answers, devices)
        if layer + 1 < layers:
            slab, stream = pl.pallas_call(
                functools.partial(middle_kernel, layer),
                in_specs=[VM] * 6,
                out_specs=(VM, VM),
                out_shape=(slab_type, stream_type),
                scratch_shapes=[rows, stack],
                compiler_params=params,
                name="middle",
            )(back, stream, norm_gain, routes_t, gates_t, placement)
        else:
            stream = pl.pallas_call(
                functools.partial(last_kernel, layer),
                in_specs=[VM] * 5,
                out_specs=VM,
                out_shape=stream_type,
                scratch_shapes=[rows],
                compiler_params=params,
                name="last",
            )(back, stream, routes_t, gates_t, placement)
    return stream


def solution(mesh):
    return jax.shard_map(
        shards,
        mesh=mesh,
        in_specs=(
            P(AXES, None),
            P(),
            P(None, AXES, None),
            P(None, AXES, None),
            P(),
            P(None, AXES, None, None),
            P(None, AXES, None, None),
            P(None, AXES, None, None),
            P(None, AXES, None, None),
        ),
        out_specs=P(AXES, None),
        check_vma=False,
    )
```

time: 203 us -> 163 us (0.80)
  blocking collectives: 0 us -> 90.6 us
  waiting for transfers between devices: 74.6 us -> 0.01 us
  Pallas kernels: 0 us -> 52.9 us
  local copies, waits for them, and re-layouts: 54.3 us -> 7.11 us
  matrix products: 27 us -> 0 us
  other arithmetic: 18.9 us -> 0 us
  starting transfers between devices: 27.2 us -> 11.5 us
    all_to_all x0 -> x3, blocking collectives: none -> 90.6 us  [exchange(): moved = lax.all_to_all(split, AXES, split_axis=0, concat_axis=0, tiled=True)]
    all_to_all x4 -> x1, waiting for transfers between devices: 74.6 us -> 0.01 us  [exchange(): moved = lax.all_to_all(split, AXES, split_axis=0, concat_axis=0, tiled=True)]
    pallas_call x0 -> x7, Pallas kernels: none -> 52.9 us  [the longest x2 23.4 us: dequant(): pl.pallas_call(dequant_kernel, grid=(layers, height // block), in_specs=[...]
    dot_general x8 -> x0, matrix products: 27 us -> none  [the longest x2 10.5 us: shards(): gate_up = jnp.dot(token_rows, in_weight, preferred_element_type=jnp.float32)]
    reshape x8 -> x0, local copies, waits for them, and re-layouts: 19.5 us -> none  [the longest x2 5.03 us: shards(): returned.reshape(-1, width)]
    convert_element_type x3 -> x0, other arithmetic: 16.1 us -> none  [the longest x2 15.4 us: dequantize(): return (quantized.astype(jnp.float32) * widened).astype(jnp.bfloat16)]
    all_to_all x4 -> x1, starting transfers between devices: 27.2 us -> 11.5 us  [exchange(): moved = lax.all_to_all(split, AXES, split_axis=0, concat_axis=0, tiled=True)]
    slice x7 -> x0, local copies, waits for them, and re-layouts: 11.9 us -> none  [the longest x2 10.2 us: shards(): in_weight = dequantize(w_in[layer_index, 0], in_scale[layer_index, 0], QBLK)]
  transfers between devices with their start and end apart: 4 -> 1, of which waited for: 4 -> 0; matrix products, arithmetic and copies ran while one was open for 22% -> 1% of each run, Pallas kernels for 0% -> 14%
where the time goes in v1:
time: 163 us; the launch traced here: 162 us
  blocking collectives  90.6 us (56%)
  Pallas kernels  52.9 us (32%)
  starting transfers between devices  11.5 us (7%)
  local copies, waits for them, and re-layouts  7.11 us (4%)
    all_to_all x3, blocking collectives, exchange(): moved = lax.all_to_all(split, AXES, split_axis=0, concat_axis=0, tiled=True)  90.6 us
    pallas_call x2, Pallas kernels, dequant(): pl.pallas_call(dequant_kernel, grid=(layers, height // block), in_specs=[...  23.4 us
    pallas_call x2, Pallas kernels, expert(): pl.pallas_call(functools.partial(expert_kernel, layer), in_specs=[VM, pl....  22.7 us
    all_to_all x1, starting transfers between devices, exchange(): moved = lax.all_to_all(split, AXES, split_axis=0, concat_axis=0, tiled=True)  11.5 us
    unnamed x26, local copies, waits for them, and re-layouts  6.51 us
  transfers between devices with their start and end apart: 1, of which 0 were waited for; matrix products, arithmetic and copies ran while one was open for 1% of the time, Pallas kernels for 14%

profile of v1, /device:TPU:1, one launch (start us, length us, event | category | flops | bytes accessed | tf_op | source)
XLA Modules:
  0.0 162.2 jit_solution(5183704805092113076)
XLA Ops:
  0.0 0.9 copy-done.1
  0.9 0.7 copy-done.3
  1.6 0.7 copy-done.5
  2.3 0.7 copy-done.8
  3.0 2.6 %first.1 = bf16[3072,256]{1,0:T(8,128)(2,1)} custom-call(bf16[32,2048]{1,0:T(8,128)(2,1)S(1)} %copy-done.1, f32[2,2048]{1,0:T(2,128)S(1)} %copy-done.5, s32[2,8,32]{2,1,0:T(8,128)S(1)} %bitcast.21, s32[2,128]{1,0:T(2,128)S(1)} %copy-done.8), custom_call_target="tpu_custom_call" | custom-call | tf_op jit(solution)/shard_map/first/pallas_call | solution.py:287
  5.6 11.5 %all-to-all-start = ((bf16[128,24,256]{2,1,0:T(8,128)(2,1)}), bf16[128,24,256]{2,1,0:T(8,128)(2,1)S(1)}, u32[]{:S(2)}, u32[]{:S(2)}) async-start(bf16[128,24,256]{2,1,0:T(8,128)(2,1)} %bitcast.1), calls=%async_computation | async-start | bytes 3145728 | tf_op jit(solution)/shard_map/all_to_all | solution.py:270
  17.1 0.6 copy.13.scale_ref
  17.7 0.7 copy.11
  18.4 7.4 %dequant.3.wout_hbm = bf16[2,768,2048]{2,1,0:T(8,128)(2,1)} custom-call(f32[2,6,16]{2,1,0:T(8,128)} %copy.13.scale_ref, bf16[2,1,768,2048]{3,2,1,0:T(8,128)(2,1)} %w_ref.3), custom_call_target="tpu_custom_call" | custom-call | flops 3145728 | bytes 12582912 | tf_op jit(solution)/shard_map/dequant/pallas_call | solution.py:170
  25.9 16.0 %dequant.2.win_hbm = bf16[2,2048,1536]{2,1,0:T(8,128)(2,1)} custom-call(f32[2,16,12]{2,1,0:T(8,128)} %bitcast.26, bf16[2,1,2048,1536]{3,2,1,0:T(8,128)(2,1)} %w_ref.2), custom_call_target="tpu_custom_call" | custom-call | flops 6291456 | bytes 25165824 | tf_op jit(solution)/shard_map/dequant/pallas_call | solution.py:170
  41.8 0.0 all-to-all-done
  41.8 2.8 %copy-done = bf16[2,768,2048]{2,1,0:T(8,128)(2,1)S(1)} copy-done((bf16[2,768,2048]{2,1,0:T(8,128)(2,1)S(1)}, bf16[2,768,2048]{2,1,0:T(8,128)(2,1)}, u32[]{:S(2)}) %copy-start) | copy-done | bytes 6291480
  44.6 11.3 %expert.2 = bf16[3072,256]{1,0:T(8,128)(2,1)S(1)} custom-call(bf16[3072,256]{1,0:T(8,128)(2,1)S(1)} %bitcast.16, bf16[2,2048,1536]{2,1,0:T(8,128)(2,1)} %dequant.2.win_hbm, bf16[2,768,2048]{2,1,0:T(8,128)(2,1)S(1)} %copy-done), custom_call_target="tpu_custom_call" | custom-call | flops 3623878656 | bytes 12582912 | tf_op jit(solution)/shard_map/expert/pallas_call | solution.py:245
  55.9 0.0 copy-start.2
  56.0 0.0 copy-start.4
  56.0 0.0 copy-start.6
  56.0 0.0 copy-start.7
  56.0 0.0 copy-start.9
  56.0 33.7 %all_to_all.20 = bf16[128,24,256]{2,1,0:T(8,128)(2,1)S(1)} all-to-all(bf16[128,24,256]{2,1,0:T(8,128)(2,1)S(1)} %bitcast.19), channel_id=1, replica_groups=mesh['dp'=8,'expert'=16] {'dp','expert'}, dimensions={0} | all-to-all | bytes 3145728 | tf_op jit(solution)/shard_map/all_to_all | solution.py:270
  89.8 2.4 %middle.1 = (bf16[3072,256]{1,0:T(8,128)(2,1)S(1)}, bf16[32,2048]{1,0:T(8,128)(2,1)S(1)}) custom-call(bf16[3072,256]{1,0:T(8,128)(2,1)S(1)} %bitcast.14, bf16[32,2048]{1,0:T(8,128)(2,1)S(1)} %copy-done.2, f32[2,2048]{1,0:T(2,128)S(1)} %copy-done.6, s32[2,8,32]{2,1,0:T(8,128)S(1)} %bitcast.22, f32[2,8,32]{2,1,0:T(8,128)S(1)} %bitcast.24, s32[2,128]{1,0:T(2,128)S(1)} %copy-done.9), custom_call_target="tpu_custom_call" | custom-call | tf_op jit(solution)/shard_map/middle/pallas_call | solution.py:303
  92.2 28.5 %all_to_all.21 = bf16[128,24,256]{2,1,0:T(8,128)(2,1)S(1)} all-to-all(bf16[128,24,256]{2,1,0:T(8,128)(2,1)S(1)} %bitcast.20), channel_id=1, replica_groups=mesh['dp'=8,'expert'=16] {'dp','expert'}, dimensions={0} | all-to-all | bytes 3145728 | tf_op jit(solution)/shard_map/all_to_all | solution.py:270
  120.6 11.3 %expert.3 = bf16[3072,256]{1,0:T(8,128)(2,1)S(1)} custom-call(bf16[3072,256]{1,0:T(8,128)(2,1)S(1)} %bitcast.17, bf16[2,2048,1536]{2,1,0:T(8,128)(2,1)} %dequant.2.win_hbm, bf16[2,768,2048]{2,1,0:T(8,128)(2,1)S(1)} %copy-done), custom_call_target="tpu_custom_call" | custom-call | flops 3623878656 | bytes 12582912 | tf_op jit(solution)/shard_map/expert/pallas_call | solution.py:245
  132.0 28.5 %all_to_all.22 = bf16[128,24,256]{2,1,0:T(8,128)(2,1)S(1)} all-to-all(bf16[128,24,256]{2,1,0:T(8,128)(2,1)S(1)} %bitcast.18), channel_id=1, replica_groups=mesh['dp'=8,'expert'=16] {'dp','expert'}, dimensions={0} | all-to-all | bytes 3145728 | tf_op jit(solution)/shard_map/all_to_all | solution.py:270
  160.4 1.8 %last.1 = bf16[32,2048]{1,0:T(8,128)(2,1)} custom-call(bf16[3072,256]{1,0:T(8,128)(2,1)S(1)} %bitcast.15, bf16[32,2048]{1,0:T(8,128)(2,1)S(1)} %get-tuple-element.8.stream_ref, s32[2,8,32]{2,1,0:T(8,128)S(1)} %bitcast.23, f32[2,8,32]{2,1,0:T(8,128)S(1)} %bitcast.25, s32[2,128]{1,0:T(2,128)S(1)} %copy-done.9), custom_call_target="tpu_custom_call" | custom-call | tf_op jit(solution)/shard_map/last/pallas_call | solution.py:313
  (15 shorter events, 0.0 us)
Async XLA Ops:
  0.0 0.9 copy-start.1
  0.9 0.7 copy-start.3
  1.6 0.7 copy-start.5
  2.3 0.7 copy-start.8
  5.6 11.5 %copy-start.11 = (f32[2,1,6,16]{3,1,2,0:T(1,128)S(1)}, f32[2,1,6,16]{3,1,2,0:T(1,128)}, u32[]{:S(2)}) copy-start(f32[2,1,6,16]{3,1,2,0:T(1,128)} %param.17) | copy-start | bytes 2308
  5.6 12.1 %copy-start.10 = (f32[2,1,16,12]{2,1,3,0:T(1,128)S(1)}, f32[2,1,16,12]{2,1,3,0:T(1,128)}, u32[]{:S(2)}) copy-start(f32[2,1,16,12]{2,1,3,0:T(1,128)} %param.15) | copy-start | bytes 4612
  5.6 36.2 %all-to-all-start = ((bf16[128,24,256]{2,1,0:T(8,128)(2,1)}), bf16[128,24,256]{2,1,0:T(8,128)(2,1)S(1)}, u32[]{:S(2)}, u32[]{:S(2)}) async-start(bf16[128,24,256]{2,1,0:T(8,128)(2,1)} %bitcast.1), calls=%async_computation | async-start | bytes 3145728 | tf_op jit(solution)/shard_map/all_to_all | solution.py:270
  41.8 2.8 %copy-start = (bf16[2,768,2048]{2,1,0:T(8,128)(2,1)S(1)}, bf16[2,768,2048]{2,1,0:T(8,128)(2,1)}, u32[]{:S(2)}) copy-start(bf16[2,768,2048]{2,1,0:T(8,128)(2,1)} %dequant.3.wout_hbm) | copy-start | bytes 18874372
  55.9 33.8 %copy-start.2 = (bf16[32,2048]{1,0:T(8,128)(2,1)S(1)}, bf16[32,2048]{1,0:T(8,128)(2,1)}, u32[]{:S(2)}) copy-start(bf16[32,2048]{1,0:T(8,128)(2,1)} %stream_ref.1) | copy-start | bytes 393220
  56.0 33.8 %copy-start.4 = (s32[2,32,8]{1,2,0:T(8,128)S(1)}, s32[2,32,8]{1,2,0:T(8,128)}, u32[]{:S(2)}) copy-start(s32[2,32,8]{1,2,0:T(8,128)} %param.11) | copy-start | bytes 6148
  56.0 33.8 %copy-start.6 = (f32[2,2048]{1,0:T(2,128)S(1)}, f32[2,2048]{1,0:T(2,128)}, u32[]{:S(2)}) copy-start(f32[2,2048]{1,0:T(2,128)} %gain_ref.3) | copy-start | bytes 49156
  56.0 33.8 %copy-start.7 = (f32[2,32,8]{1,2,0:T(8,128)S(1)}, f32[2,32,8]{1,2,0:T(8,128)}, u32[]{:S(2)}) copy-start(f32[2,32,8]{1,2,0:T(8,128)} %param.12) | copy-start | bytes 6148
  56.0 33.8 %copy-start.9 = (s32[2,128]{1,0:T(2,128)S(1)}, s32[2,128]{1,0:T(2,128)}, u32[]{:S(2)}) copy-start(s32[2,128]{1,0:T(2,128)} %place_ref.5) | copy-start | bytes 3076

commit v2 on v1

v2 whole, which is shorter than its diff:
```python
import functools

import jax
import jax.numpy as jnp
from jax import lax
from jax.experimental import pallas as pl
from jax.experimental.pallas import tpu as pltpu
from jax.sharding import PartitionSpec as P

AXES = ("dp", "expert")
QBLK = 128
CAP = 3
PIECES = 8
GROUP = 32
EPS = 1e-06
MIB = 1 << 20


def fold_matrix():
    row = lax.broadcasted_iota(jnp.int32, (GROUP * PIECES, GROUP * PIECES), 0)
    col = lax.broadcasted_iota(jnp.int32, (GROUP * PIECES, GROUP * PIECES), 1)
    return jnp.where(col == (row & (PIECES - 1)) * GROUP + (row >> 3), 1.0, 0.0).astype(jnp.bfloat16)


def unfold_matrix():
    row = lax.broadcasted_iota(jnp.int32, (GROUP * PIECES, GROUP * PIECES), 0)
    col = lax.broadcasted_iota(jnp.int32, (GROUP * PIECES, GROUP * PIECES), 1)
    return jnp.where(col == (row & (GROUP - 1)) * PIECES + (row >> 5), 1.0, 0.0).astype(jnp.bfloat16)


def unfold_rows(slab_ref, rows_ref):
    piece = slab_ref.shape[1]
    span = GROUP * PIECES
    unfold = unfold_matrix()
    for b in range(slab_ref.shape[0] // span):
        block = jnp.dot(
            unfold, slab_ref[b * span : (b + 1) * span, :], preferred_element_type=jnp.float32
        ).astype(jnp.bfloat16)
        for p in range(PIECES):
            rows_ref[b * GROUP : (b + 1) * GROUP, p * piece : (p + 1) * piece] = block[
                p * GROUP : (p + 1) * GROUP
            ]


def fold_rows(stack_ref, slab_ref):
    span = GROUP * PIECES
    fold = fold_matrix()
    for b in range(slab_ref.shape[0] // span):
        slab_ref[b * span : (b + 1) * span, :] = jnp.dot(
            fold, stack_ref[b * span : (b + 1) * span, :], preferred_element_type=jnp.float32
        ).astype(jnp.bfloat16)


def stack_piece(stack_ref, values, p):
    span = GROUP * PIECES
    for b in range(values.shape[0] // GROUP):
        stack_ref[b * span + p * GROUP : b * span + (p + 1) * GROUP, :] = values[
            b * GROUP : (b + 1) * GROUP
        ]


def slot_tables(routes_t, place_row, gates_t):
    tokens = routes_t.shape[1]
    devices = place_row.shape[1]
    slots = devices * CAP
    home = lax.broadcasted_iota(jnp.int32, (devices, slots), 0)
    slot = lax.broadcasted_iota(jnp.int32, (devices, slots), 1)
    low = home * CAP
    widen = jnp.where((slot >= low) & (slot < low + CAP), 1.0, 0.0).astype(jnp.bfloat16)
    place = jnp.dot(
        jnp.broadcast_to(place_row.astype(jnp.float32), (8, devices)).astype(jnp.bfloat16),
        widen,
        preferred_element_type=jnp.float32,
    )[:1]
    rank_of = jnp.dot(
        jnp.broadcast_to(
            lax.broadcasted_iota(jnp.int32, (1, devices), 1).astype(jnp.float32), (8, devices)
        ).astype(jnp.bfloat16),
        widen,
        preferred_element_type=jnp.float32,
    )[:1]
    order = lax.broadcasted_iota(jnp.int32, (1, slots), 1).astype(jnp.float32) - rank_of * CAP
    chosen = jnp.transpose(routes_t.astype(jnp.float32))
    gate = None if gates_t is None else jnp.transpose(gates_t)
    taken = jnp.zeros((tokens, slots), jnp.float32)
    weight = jnp.zeros((tokens, slots), jnp.float32)
    for k in range(chosen.shape[1]):
        same = chosen[:, k : k + 1] == place
        taken = jnp.where(same, 1.0, taken)
        if gate is not None:
            weight = jnp.where(same, gate[:, k : k + 1], weight)
    later = lax.broadcasted_iota(jnp.int32, (tokens, tokens), 0)
    earlier = lax.broadcasted_iota(jnp.int32, (tokens, tokens), 1)
    before = jnp.where(earlier < later, 1.0, 0.0).astype(jnp.bfloat16)
    ranks = jnp.dot(before, taken.astype(jnp.bfloat16), preferred_element_type=jnp.float32)
    mine = ranks == order
    return jnp.where(mine, taken, 0.0), jnp.where(mine, weight, 0.0)


def normalise(stream_f, gain):
    scale = lax.rsqrt(jnp.mean(stream_f * stream_f, axis=-1, keepdims=True) + EPS)
    return (stream_f * scale * gain).astype(jnp.bfloat16)


def send_rows(pick, normed, stack_ref, slab_ref):
    piece = slab_ref.shape[1]
    for p in range(PIECES):
        rows = jnp.dot(
            pick, normed[:, p * piece : (p + 1) * piece], preferred_element_type=jnp.float32
        ).astype(jnp.bfloat16)
        stack_piece(stack_ref, rows, p)
    fold_rows(stack_ref, slab_ref)


def mix(weight, slab_ref, rows_ref):
    unfold_rows(slab_ref, rows_ref)
    both = jnp.dot(weight, rows_ref[...], preferred_element_type=jnp.float32)
    tokens = weight.shape[0] // 2
    return both[:tokens] + both[tokens:]


def first_kernel(
    tokens_hbm, gain_hbm, routes_hbm, place_hbm, slab_ref,
    tokens_ref, gain_ref, routes_ref, place_ref, stack_ref, sems,
):
    loads = [
        pltpu.make_async_copy(src, dst, sems.at[i])
        for i, (src, dst) in enumerate(
            (
                (routes_hbm, routes_ref),
                (place_hbm, place_ref),
                (tokens_hbm, tokens_ref),
                (gain_hbm, gain_ref),
            )
        )
    ]
    for load in loads:
        load.start()
    loads[0].wait()
    loads[1].wait()
    select, _ = slot_tables(routes_ref[0], place_ref[0:1, :], None)
    pick = jnp.transpose(select).astype(jnp.bfloat16)
    loads[2].wait()
    loads[3].wait()
    normed = normalise(tokens_ref[...].astype(jnp.float32), gain_ref[0:1, :])
    send_rows(pick, normed, stack_ref, slab_ref)


def middle_kernel(
    layer, slab_in, stream_ref, gain_ref, weight_ref, pick_ref,
    slab_ref, out_ref, rows_ref, stack_ref,
):
    mixed = mix(weight_ref[...], slab_in, rows_ref)
    stream = (stream_ref[...].astype(jnp.float32) + mixed).astype(jnp.bfloat16)
    out_ref[...] = stream
    normed = normalise(stream.astype(jnp.float32), gain_ref[layer + 1 : layer + 2, :])
    send_rows(pick_ref[...], normed, stack_ref, slab_ref)


def last_kernel(slab_in, stream_ref, weight_ref, out_ref, rows_ref):
    mixed = mix(weight_ref[...], slab_in, rows_ref)
    out_ref[...] = (stream_ref[...].astype(jnp.float32) + mixed).astype(jnp.bfloat16)


def prepare_kernel(
    layer, in_scale, out_scale, w_in, w_out, routes_ref, gates_ref, place_ref,
    win_hbm, wout_hbm, weight_ref, *rest,
):
    pick_ref = rest[0] if len(rest) > 5 else None
    win, wout, load_sems, in_sems, out_sems = rest[-5:]
    rows = 2 * QBLK
    chunk = win_hbm.shape[2]
    loads = []
    for src, buf, scale, dst, sems in (
        (w_in, win, in_scale, win_hbm, in_sems),
        (w_out, wout, out_scale, wout_hbm, out_sems),
    ):
        for r in range(buf.shape[0] // rows):
            span = pl.ds(r * rows, rows)
            load = pltpu.make_async_copy(
                src.at[layer, 0, span, :], buf.at[span, :], load_sems.at[len(loads)]
            )
            load.start()
            loads.append((load, buf, scale, dst, sems, r))
    _, weight = slot_tables(routes_ref[layer], place_ref[layer : layer + 1, :], gates_ref[layer])
    high = weight.astype(jnp.bfloat16)
    low = (weight - high.astype(jnp.float32)).astype(jnp.bfloat16)
    weight_ref[...] = jnp.concatenate([high, low], axis=0)
    if pick_ref is not None:
        select, _ = slot_tables(
            routes_ref[layer + 1], place_ref[layer + 1 : layer + 2, :], None
        )
        pick_ref[...] = jnp.transpose(select).astype(jnp.bfloat16)
    stores = []
    for load, buf, scale, dst, sems, r in loads:
        load.wait()
        for i in range(rows // QBLK):
            for j in range(buf.shape[1] // QBLK):
                at = (
                    slice(r * rows + i * QBLK, r * rows + (i + 1) * QBLK),
                    slice(j * QBLK, (j + 1) * QBLK),
                )
                factor = scale[layer, r * (rows // QBLK) + i, j]
                buf[at] = (buf[at].astype(jnp.float32) * factor).astype(jnp.bfloat16)
        for c in range(dst.shape[0]):
            store = pltpu.make_async_copy(
                buf.at[pl.ds(r * rows, rows), pl.ds(c * chunk, chunk)],
                dst.at[c, pl.ds(r * rows, rows), :],
                sems.at[r, c],
            )
            store.start()
            stores.append(store)
    for store in stores:
        store.wait()


def expert_steps(slab_in, slab_ref, x_ref, hid, stack_ref, in_chunk, out_chunk, chunks):
    unfold_rows(slab_in, x_ref)
    chunk = slab_ref.shape[1]
    for n in range(chunks):
        gate = jnp.dot(x_ref[...], in_chunk(n), preferred_element_type=jnp.float32)
        up = jnp.dot(x_ref[...], in_chunk(chunks + n), preferred_element_type=jnp.float32)
        hid[:, n * chunk : (n + 1) * chunk] = (gate / (1.0 + jnp.exp(-gate)) * up).astype(
            jnp.bfloat16
        )
    for m in range(PIECES):
        answer = jnp.dot(hid[...], out_chunk(m), preferred_element_type=jnp.float32).astype(
            jnp.bfloat16
        )
        stack_piece(stack_ref, answer, m)
    fold_rows(stack_ref, slab_ref)


def expert_kernel(slab_in, win, wout, slab_ref, x_ref, hid, stack_ref):
    expert_steps(
        slab_in, slab_ref, x_ref, hid, stack_ref,
        lambda c: win[c], lambda c: wout[c], win.shape[0] // 2,
    )


def streamed_kernel(
    slab_in, win_hbm, wout_hbm, slab_ref, x_ref, hid, stack_ref, win, wout, in_sems, out_sems
):
    chunks = win.shape[0] // 2

    def in_load(c):
        return pltpu.make_async_copy(win_hbm.at[c], win.at[c], in_sems.at[c])

    def out_load(c):
        return pltpu.make_async_copy(wout_hbm.at[c], wout.at[c], out_sems.at[c])

    for n in range(chunks):
        in_load(n).start()
        in_load(chunks + n).start()
    for m in range(wout.shape[0]):
        out_load(m).start()

    def in_chunk(c):
        in_load(c).wait()
        return win[c]

    def out_chunk(c):
        out_load(c).wait()
        return wout[c]

    expert_steps(slab_in, slab_ref, x_ref, hid, stack_ref, in_chunk, out_chunk, chunks)


VM = pl.BlockSpec(memory_space=pltpu.VMEM)
SM = pl.BlockSpec(memory_space=pltpu.SMEM)
HB = pl.BlockSpec(memory_space=pltpu.HBM)


def prepare(layer, layers, weights, tables, slots, chunk):
    w_in, in_scale, w_out, out_scale = weights
    routes_t, gates_t, place = tables
    tokens = routes_t.shape[2]
    width, gated = w_in.shape[2:]
    ff = w_out.shape[2]
    outs = [
        pltpu.HBM((gated // chunk, width, chunk), jnp.bfloat16),
        pltpu.HBM((width // chunk, ff, chunk), jnp.bfloat16),
        jax.ShapeDtypeStruct((2 * tokens, slots), jnp.bfloat16),
    ]
    if layer + 1 < layers:
        outs.append(jax.ShapeDtypeStruct((slots, tokens), jnp.bfloat16))
    rows = 2 * QBLK
    size = width * gated + ff * width
    return pl.pallas_call(
        functools.partial(prepare_kernel, layer),
        in_specs=[SM, SM, HB, HB, VM, VM, VM],
        out_specs=[HB, HB] + [VM] * (len(outs) - 2),
        out_shape=outs,
        scratch_shapes=[
            pltpu.VMEM((width, gated), jnp.bfloat16),
            pltpu.VMEM((ff, width), jnp.bfloat16),
            pltpu.SemaphoreType.DMA(((width + ff) // rows,)),
            pltpu.SemaphoreType.DMA((width // rows, gated // chunk)),
            pltpu.SemaphoreType.DMA((ff // rows, width // chunk)),
        ],
        compiler_params=pltpu.CompilerParams(vmem_limit_bytes=24 * MIB),
        cost_estimate=pl.CostEstimate(flops=size, bytes_accessed=4 * size, transcendentals=0),
        name="prepare",
    )(in_scale[:, 0], out_scale[:, 0], w_in, w_out, routes_t, gates_t, place)


def expert(slab, win, wout, streamed):
    rows, piece = slab.shape
    slots = rows // PIECES
    width = win.shape[1]
    ff = wout.shape[1]
    scratch = [
        pltpu.VMEM((slots, width), jnp.bfloat16),
        pltpu.VMEM((slots, ff), jnp.bfloat16),
        pltpu.VMEM(slab.shape, jnp.bfloat16),
    ]
    if streamed:
        win, wout = hbm(win), hbm(wout)
        scratch += [
            pltpu.VMEM(win.shape, jnp.bfloat16),
            pltpu.VMEM(wout.shape, jnp.bfloat16),
            pltpu.SemaphoreType.DMA((win.shape[0],)),
            pltpu.SemaphoreType.DMA((wout.shape[0],)),
        ]
    return pl.pallas_call(
        streamed_kernel if streamed else expert_kernel,
        in_specs=[VM, HB, HB] if streamed else [VM] * 3,
        out_specs=VM,
        out_shape=jax.ShapeDtypeStruct(slab.shape, jnp.bfloat16),
        scratch_shapes=scratch,
        compiler_params=pltpu.CompilerParams(vmem_limit_bytes=(28 if streamed else 20) * MIB),
        cost_estimate=pl.CostEstimate(
            flops=6 * slots * width * ff,
            bytes_accessed=6 * width * ff + 4 * slots * width,
            transcendentals=slots * ff,
        ),
        name="expert",
    )(slab, win, wout)


def hbm(array):
    return pltpu.with_memory_space_constraint(array, pltpu.HBM)


def exchange(slab, devices):
    split = slab.reshape(devices, slab.shape[0] // devices, slab.shape[1])
    moved = lax.all_to_all(split, AXES, split_axis=0, concat_axis=0, tiled=True)
    return moved.reshape(slab.shape)


def shards(tokens, norm_gain, routes, gates, placement, w_in, in_scale, w_out, out_scale):
    count, width = tokens.shape
    layers, devices = placement.shape
    slots = devices * CAP
    piece = width // PIECES
    routes_t = jnp.swapaxes(routes, 1, 2)
    gates_t = jnp.swapaxes(gates, 1, 2)
    slab_type = jax.ShapeDtypeStruct((slots * PIECES, piece), jnp.bfloat16)
    stream_type = jax.ShapeDtypeStruct((count, width), jnp.bfloat16)
    rows = pltpu.VMEM((slots, width), jnp.bfloat16)
    stack = pltpu.VMEM((slots * PIECES, piece), jnp.bfloat16)
    params = pltpu.CompilerParams(vmem_limit_bytes=24 * MIB)

    small = (
        pltpu.VMEM((count, width), jnp.bfloat16),
        pltpu.VMEM(norm_gain.shape, jnp.float32),
        pltpu.VMEM(routes_t.shape, jnp.int32),
        pltpu.VMEM(placement.shape, jnp.int32),
    )
    slab = pl.pallas_call(
        first_kernel,
        in_specs=[HB] * 4,
        out_specs=VM,
        out_shape=slab_type,
        scratch_shapes=[*small, stack, pltpu.SemaphoreType.DMA((4,))],
        compiler_params=params,
        name="first",
    )(*[hbm(a) for a in (tokens, norm_gain, routes_t, placement)])
    weights = (hbm(w_in), in_scale, hbm(w_out), out_scale)
    stream = tokens
    prepared = [
        prepare(layer, layers, weights, (routes_t, gates_t, placement), slots, piece)
        for layer in range(layers)
    ]
    for layer in range(layers):
        win, wout, weight = prepared[layer][:3]
        arrived = exchange(slab, devices)
        if layer == 0:
            arrived, prepared = lax.optimization_barrier((arrived, prepared))
            win, wout, weight = prepared[0][:3]
        answers = expert(arrived, win, wout, layer == 0)
        back = exchange(answers, devices)
        if layer + 1 < layers:
            slab, stream = pl.pallas_call(
                functools.partial(middle_kernel, layer),
                in_specs=[VM] * 5,
                out_specs=(VM, VM),
                out_shape=(slab_type, stream_type),
                scratch_shapes=[rows, stack],
                compiler_params=params,
                name="middle",
            )(back, stream, norm_gain, weight, prepared[layer][3])
        else:
            stream = pl.pallas_call(
                last_kernel,
                in_specs=[VM] * 3,
                out_specs=VM,
                out_shape=stream_type,
                scratch_shapes=[rows],
                compiler_params=params,
                name="last",
            )(back, stream, weight)
    return stream


def solution(mesh):
    return jax.shard_map(
        shards,
        mesh=mesh,
        in_specs=(
            P(AXES, None),
            P(),
            P(None, AXES, None),
            P(None, AXES, None),
            P(),
            P(None, AXES, None, None),
            P(None, AXES, None, None),
            P(None, AXES, None, None),
            P(None, AXES, None, None),
        ),
        out_specs=P(AXES, None),
        check_vma=False,
    )
```

time: 163 us -> 145 us (0.89)
  Pallas kernels: 52.9 us -> 41.2 us
  local copies, waits for them, and re-layouts: 7.11 us -> 0.15 us
  waiting for transfers between devices: 0.01 us -> 5.86 us
  blocking collectives: 90.6 us -> 85.6 us
    pallas_call x7, Pallas kernels: 52.9 us -> 41.2 us  [the longest x2 18.1 us: prepare(): pl.pallas_call(functools.partial(prepare_kernel, layer), in_specs=[SM, SM...]
    unnamed x26 -> x20, local copies, waits for them, and re-layouts: 6.51 us -> 0.14 us
    all_to_all x1, waiting for transfers between devices: 0.01 us -> 5.86 us  [exchange(): moved = lax.all_to_all(split, AXES, split_axis=0, concat_axis=0, tiled=True)]
    all_to_all x3, blocking collectives: 90.6 us -> 85.6 us  [exchange(): moved = lax.all_to_all(split, AXES, split_axis=0, concat_axis=0, tiled=True)]
  transfers between devices with their start and end apart: 1 -> 1, of which waited for: 0 -> 1; matrix products, arithmetic and copies ran while one was open for 1% -> 0% of each run, Pallas kernels for 14% -> 13%
where the time goes in v2:
time: 145 us; the launch traced here: 144 us
  blocking collectives  85.6 us (59%)
  Pallas kernels  41.2 us (28%)
  starting transfers between devices  11.5 us (8%)
  waiting for transfers between devices  5.86 us (4%)
    all_to_all x3, blocking collectives, exchange(): moved = lax.all_to_all(split, AXES, split_axis=0, concat_axis=0, tiled=True)  85.6 us
    pallas_call x2, Pallas kernels, prepare(): pl.pallas_call(functools.partial(prepare_kernel, layer), in_specs=[SM, SM...  18.1 us
    pallas_call x2, Pallas kernels, expert(): pl.pallas_call(streamed_kernel if streamed else expert_kernel, in_specs=[...  16.1 us
    all_to_all x1, starting transfers between devices, exchange(): moved = lax.all_to_all(split, AXES, split_axis=0, concat_axis=0, tiled=True)  11.5 us
    all_to_all x1, waiting for transfers between devices, exchange(): moved = lax.all_to_all(split, AXES, split_axis=0, concat_axis=0, tiled=True)  5.86 us
    pallas_call x1, Pallas kernels, shards(): pl.pallas_call(first_kernel, in_specs=[HB] * 4, out_specs=VM, out_shape=s...  3.46 us
  transfers between devices with their start and end apart: 1, of which 1 were waited for; matrix products, arithmetic and copies ran while one was open for 0% of the time, Pallas kernels for 13%

profile of v2, /device:TPU:1, one launch (start us, length us, event | category | flops | bytes accessed | tf_op | source)
XLA Modules:
  0.0 144.4 jit_solution(7603589787783136583)
XLA Ops:
  0.0 3.5 %first.1 = bf16[3072,256]{1,0:T(8,128)(2,1)} custom-call(bf16[32,2048]{1,0:T(8,128)(2,1)} %stream_ref.1, f32[2,2048]{1,0:T(2,128)} %gain_ref.1, s32[2,8,32]{2,1,0:T(8,128)} %bitcast.23, s32[2,128]{1,0:T(2,128)} %place_ref.3), custom_call_target="tpu_custom_call" | custom-call | tf_op jit(solution)/shard_map/first/pallas_call | solution.py:370
  3.5 0.0 copy-start.8
  3.5 0.0 copy-start.7
  3.5 0.0 copy-start.1
  3.5 0.0 copy-start.3
  3.5 0.0 copy-start.4
  3.5 11.5 %all-to-all-start = ((bf16[128,24,256]{2,1,0:T(8,128)(2,1)}), bf16[128,24,256]{2,1,0:T(8,128)(2,1)S(1)}, u32[]{:S(2)}, u32[]{:S(2)}) async-start(bf16[128,24,256]{2,1,0:T(8,128)(2,1)} %bitcast.1), calls=%async_computation | async-start | bytes 3145728 | tf_op jit(solution)/shard_map/all_to_all | solution.py:347
  15.0 0.0 copy-done.8
  15.1 0.0 copy-done.7
  15.1 0.1 copy.11
  15.2 0.0 copy-done.4
  15.2 8.8 %prepare.3 = (bf16[6,2048,256]{2,1,0:T(8,128)(2,1)}, bf16[8,768,256]{2,1,0:T(8,128)(2,1)}, bf16[64,384]{1,0:T(8,128)(2,1)S(1)}) custom-call(f32[2,16,12]{2,1,0:T(8,128)S(1)} %bitcast.21, f32[2,6,16]{2,1,0:T(8,128)S(1)} %copy.13.out_scale, bf16[2,1,2048,1536]{3,2,1,0:T(8,128)(2,1)} %w_in.3, bf16[2,1,768,2048]{3,2,1,0:T(8,128)(2,1)} %w_out.3, ...), custom_call_target="tpu_custom_call" | custom-call | flops 4718592 | bytes 18874368 | tf_op jit(solution)/shard_map/prepare/pallas_call | solution.py:289
  24.0 9.3 %prepare.2 = (bf16[6,2048,256]{2,1,0:T(8,128)(2,1)}, bf16[8,768,256]{2,1,0:T(8,128)(2,1)}, bf16[64,384]{1,0:T(8,128)(2,1)S(1)}, bf16[384,32]{1,0:T(8,128)(2,1)S(1)}) custom-call(f32[2,16,12]{2,1,0:T(8,128)S(1)} %bitcast.22, f32[2,6,16]{2,1,0:T(8,128)S(1)} %copy.13.out_scale, bf16[2,1,2048,1536]{3,2,1,0:T(8,128)(2,1)} %w_in.3, ...), custom_call_target="tpu_custom_call" | custom-call | flops 4718592 | bytes 18874368 | tf_op jit(solution)/shard_map/prepare/pallas_call | solution.py:289
  33.3 5.9 %all-to-all-done = bf16[128,24,256]{2,1,0:T(8,128)(2,1)S(1)} async-done(((bf16[128,24,256]{2,1,0:T(8,128)(2,1)}), bf16[128,24,256]{2,1,0:T(8,128)(2,1)S(1)}, u32[]{:S(2)}, u32[]{:S(2)}) %all-to-all-start) | async-done | bytes 1572896 | tf_op jit(solution)/shard_map/all_to_all | solution.py:347
  39.2 11.4 %expert.2 = bf16[3072,256]{1,0:T(8,128)(2,1)S(1)} custom-call(bf16[3072,256]{1,0:T(8,128)(2,1)S(1)} %bitcast.16, bf16[6,2048,256]{2,1,0:T(8,128)(2,1)} %get-tuple-element.30.win_hbm, bf16[8,768,256]{2,1,0:T(8,128)(2,1)} %get-tuple-element.31.wout_hbm), custom_call_target="tpu_custom_call" | custom-call | flops 3623878656 | bytes 12582912 | tf_op jit(solution)/shard_map/expert/pallas_call | solution.py:325
  50.6 0.0 copy-start
  50.6 0.0 copy-start.2
  50.6 28.7 %all_to_all.20 = bf16[128,24,256]{2,1,0:T(8,128)(2,1)S(1)} all-to-all(bf16[128,24,256]{2,1,0:T(8,128)(2,1)S(1)} %bitcast.18), channel_id=1, replica_groups=mesh['dp'=8,'expert'=16] {'dp','expert'}, dimensions={0} | all-to-all | bytes 3145728 | tf_op jit(solution)/shard_map/all_to_all | solution.py:347
  79.3 2.0 %middle.1 = (bf16[3072,256]{1,0:T(8,128)(2,1)S(1)}, bf16[32,2048]{1,0:T(8,128)(2,1)S(1)}) custom-call(bf16[3072,256]{1,0:T(8,128)(2,1)S(1)} %bitcast.14, bf16[32,2048]{1,0:T(8,128)(2,1)S(1)} %copy-done, f32[2,2048]{1,0:T(2,128)S(1)} %copy-done.2, bf16[64,384]{1,0:T(8,128)(2,1)S(1)} %get-tuple-element.32.weight_ref, ...), custom_call_target="tpu_custom_call" | custom-call | tf_op jit(solution)/shard_map/middle/pallas_call | solution.py:394
  81.3 28.5 %all_to_all.21 = bf16[128,24,256]{2,1,0:T(8,128)(2,1)S(1)} all-to-all(bf16[128,24,256]{2,1,0:T(8,128)(2,1)S(1)} %bitcast.17), channel_id=1, replica_groups=mesh['dp'=8,'expert'=16] {'dp','expert'}, dimensions={0} | all-to-all | bytes 3145728 | tf_op jit(solution)/shard_map/all_to_all | solution.py:347
  109.8 0.0 copy-done.6
  109.8 4.7 %expert.3 = bf16[3072,256]{1,0:T(8,128)(2,1)S(1)} custom-call(bf16[3072,256]{1,0:T(8,128)(2,1)S(1)} %bitcast.19, bf16[6,2048,256]{2,1,0:T(8,128)(2,1)S(1)} %copy-done.5, bf16[8,768,256]{2,1,0:T(8,128)(2,1)S(1)} %copy-done.6), custom_call_target="tpu_custom_call" | custom-call | flops 3623878656 | bytes 12582912 | tf_op jit(solution)/shard_map/expert/pallas_call | solution.py:325
  114.5 28.5 %all_to_all.22 = bf16[128,24,256]{2,1,0:T(8,128)(2,1)S(1)} all-to-all(bf16[128,24,256]{2,1,0:T(8,128)(2,1)S(1)} %bitcast.20), channel_id=1, replica_groups=mesh['dp'=8,'expert'=16] {'dp','expert'}, dimensions={0} | all-to-all | bytes 3145728 | tf_op jit(solution)/shard_map/all_to_all | solution.py:347
  142.9 1.5 %last.1 = bf16[32,2048]{1,0:T(8,128)(2,1)} custom-call(bf16[3072,256]{1,0:T(8,128)(2,1)S(1)} %bitcast.15, bf16[32,2048]{1,0:T(8,128)(2,1)S(1)} %get-tuple-element.37.stream_ref, bf16[64,384]{1,0:T(8,128)(2,1)S(1)} %get-tuple-element.38.weight_ref), custom_call_target="tpu_custom_call" | custom-call | tf_op jit(solution)/shard_map/last/pallas_call | solution.py:404
  (9 shorter events, 0.0 us)
Async XLA Ops:
  3.5 11.6 %copy-start.8 = (f32[2,1,6,16]{3,1,2,0:T(1,128)S(1)}, f32[2,1,6,16]{3,1,2,0:T(1,128)}, u32[]{:S(2)}) copy-start(f32[2,1,6,16]{3,1,2,0:T(1,128)} %param.17) | copy-start | bytes 2308
  3.5 11.6 %copy-start.7 = (f32[2,1,16,12]{2,1,3,0:T(1,128)S(1)}, f32[2,1,16,12]{2,1,3,0:T(1,128)}, u32[]{:S(2)}) copy-start(f32[2,1,16,12]{2,1,3,0:T(1,128)} %param.15) | copy-start | bytes 4612
  3.5 11.7 %copy-start.1 = (s32[2,32,8]{1,2,0:T(8,128)S(1)}, s32[2,32,8]{1,2,0:T(8,128)}, u32[]{:S(2)}) copy-start(s32[2,32,8]{1,2,0:T(8,128)} %param.11) | copy-start | bytes 6148
  3.5 11.7 %copy-start.3 = (f32[2,32,8]{1,2,0:T(8,128)S(1)}, f32[2,32,8]{1,2,0:T(8,128)}, u32[]{:S(2)}) copy-start(f32[2,32,8]{1,2,0:T(8,128)} %param.12) | copy-start | bytes 6148
  3.5 11.7 %copy-start.4 = (s32[2,128]{1,0:T(2,128)S(1)}, s32[2,128]{1,0:T(2,128)}, u32[]{:S(2)}) copy-start(s32[2,128]{1,0:T(2,128)} %place_ref.3) | copy-start | bytes 3076
  3.5 35.7 %all-to-all-start = ((bf16[128,24,256]{2,1,0:T(8,128)(2,1)}), bf16[128,24,256]{2,1,0:T(8,128)(2,1)S(1)}, u32[]{:S(2)}, u32[]{:S(2)}) async-start(bf16[128,24,256]{2,1,0:T(8,128)(2,1)} %bitcast.1), calls=%async_computation | async-start | bytes 3145728 | tf_op jit(solution)/shard_map/all_to_all | solution.py:347
  39.2 70.6 %copy-start.6 = (bf16[8,768,256]{2,1,0:T(8,128)(2,1)S(1)}, bf16[8,768,256]{2,1,0:T(8,128)(2,1)}, u32[]{:S(2)}) copy-start(bf16[8,768,256]{2,1,0:T(8,128)(2,1)} %get-tuple-element.36.wout) | copy-start | bytes 9437188
  50.6 28.7 %copy-start = (bf16[32,2048]{1,0:T(8,128)(2,1)S(1)}, bf16[32,2048]{1,0:T(8,128)(2,1)}, u32[]{:S(2)}) copy-start(bf16[32,2048]{1,0:T(8,128)(2,1)} %stream_ref.1) | copy-start | bytes 393220
  50.6 28.7 %copy-start.2 = (f32[2,2048]{1,0:T(2,128)S(1)}, f32[2,2048]{1,0:T(2,128)}, u32[]{:S(2)}) copy-start(f32[2,2048]{1,0:T(2,128)} %gain_ref.1) | copy-start | bytes 49156
  50.6 59.2 %copy-start.5 = (bf16[6,2048,256]{2,1,0:T(8,128)(2,1)S(1)}, bf16[6,2048,256]{2,1,0:T(8,128)(2,1)}, u32[]{:S(2)}) copy-start(bf16[6,2048,256]{2,1,0:T(8,128)(2,1)} %get-tuple-element.35.win) | copy-start | bytes 18874372

commit v3 on v1

--- a/solution.py
+++ b/solution.py
@@ -102,9 +102,8 @@
     return (stream_f * scale * gain).astype(jnp.bfloat16)
 
 
-def send_rows(select, normed, stack_ref, slab_ref):
+def send_rows(pick, normed, stack_ref, slab_ref):
     piece = slab_ref.shape[1]
-    pick = jnp.transpose(select).astype(jnp.bfloat16)
     for p in range(PIECES):
         rows = jnp.dot(
             pick, normed[:, p * piece : (p + 1) * piece], preferred_element_type=jnp.float32
@@ -124,10 +123,31 @@
     return both[:tokens] + both[tokens:]
 
 
-def first_kernel(tokens_ref, gain_ref, routes_ref, place_ref, slab_ref, stack_ref):
+def first_kernel(
+    tokens_hbm, gain_hbm, routes_hbm, place_hbm, slab_ref,
+    tokens_ref, gain_ref, routes_ref, place_ref, stack_ref, sems,
+):
+    loads = [
+        pltpu.make_async_copy(src, dst, sems.at[i])
+        for i, (src, dst) in enumerate(
+            (
+                (routes_hbm, routes_ref),
+                (place_hbm, place_ref),
+                (tokens_hbm, tokens_ref),
+                (gain_hbm, gain_ref),
+            )
+        )
+    ]
+    for load in loads:
+        load.start()
+    loads[0].wait()
+    loads[1].wait()
     select, _ = slot_tables(routes_ref[0], place_ref[0:1, :], None)
+    pick = jnp.transpose(select).astype(jnp.bfloat16)
+    loads[2].wait()
+    loads[3].wait()
     normed = normalise(tokens_ref[...].astype(jnp.float32), gain_ref[0:1, :])
-    send_rows(select, normed, stack_ref, slab_ref)
+    send_rows(pick, normed, stack_ref, slab_ref)
 
 
 def middle_kernel(
@@ -136,11 +156,12 @@
 ):
     _, weight = slot_tables(routes_ref[layer], place_ref[layer : layer + 1, :], gates_ref[layer])
     select, _ = slot_tables(routes_ref[layer + 1], place_ref[layer + 1 : layer + 2, :], None)
+    pick = jnp.transpose(select).astype(jnp.bfloat16)
     mixed = mix(weight, slab_in, rows_ref)
     stream = (stream_ref[...].astype(jnp.float32) + mixed).astype(jnp.bfloat16)
     out_ref[...] = stream
     normed = normalise(stream.astype(jnp.float32), gain_ref[layer + 1 : layer + 2, :])
-    send_rows(select, normed, stack_ref, slab_ref)
+    send_rows(pick, normed, stack_ref, slab_ref)
 
 
 def last_kernel(
@@ -151,118 +172,80 @@
     out_ref[...] = (stream_ref[...].astype(jnp.float32) + mixed).astype(jnp.bfloat16)
 
 
-def dequant_kernel(scale_ref, w_ref, out_ref):
-    layer, step = pl.program_id(0), pl.program_id(1)
-    rows, cols = out_ref.shape[1], out_ref.shape[2]
-    per_step = rows // QBLK
-    for i in range(per_step):
-        for j in range(cols // QBLK):
-            scale = scale_ref[layer, step * per_step + i, j]
-            at = (slice(i * QBLK, (i + 1) * QBLK), slice(j * QBLK, (j + 1) * QBLK))
-            out_ref[(0,) + at] = (w_ref[(0, 0) + at].astype(jnp.float32) * scale).astype(
-                jnp.bfloat16
-            )
-
-
-def dequant(weights, scales):
-    layers, _, height, width = weights.shape
-    block = 256
-    return pl.pallas_call(
-        dequant_kernel,
-        grid=(layers, height // block),
-        in_specs=[
-            pl.BlockSpec(memory_space=pltpu.SMEM),
-            pl.BlockSpec((1, 1, block, width), lambda l, i: (l, 0, i, 0)),
-        ],
-        out_specs=pl.BlockSpec((1, block, width), lambda l, i: (l, i, 0)),
-        out_shape=jax.ShapeDtypeStruct((layers, height, width), jnp.bfloat16),
-        cost_estimate=pl.CostEstimate(
-            flops=weights.size, bytes_accessed=4 * weights.size, transcendentals=0
-        ),
-        name="dequant",
-    )(scales[:, 0], weights)
+def block_weight(w_ref, factor, layer, first, count):
+    lines = []
+    for i in range(w_ref.shape[2] // QBLK):
+        line = [
+            (
+                w_ref[layer, 0, i * QBLK : (i + 1) * QBLK, j * QBLK : (j + 1) * QBLK].astype(
+                    jnp.float32
+                )
+                * factor(i, j)
+            ).astype(jnp.bfloat16)
+            for j in range(first // QBLK, (first + count) // QBLK)
+        ]
+        lines.append(jnp.concatenate(line, axis=1))
+    return jnp.concatenate(lines, axis=0)
 
 
 def expert_kernel(
-    layer, slab_in, win_hbm, wout_hbm, slab_ref, x_ref, win, wout, hid, stack_ref, sems
+    layer, in_scale, out_scale, slab_in, w_in, w_out, slab_ref, x_ref, hid, stack_ref
 ):
-    width, gated = win.shape
-    ff = gated // 2
-    chunk = 256
-    loads = []
+    def into(first, count):
+        return block_weight(w_in, lambda i, j: in_scale[layer, j, 0, i], layer, first, count)
+
+    def out_of(first, count):
+        return block_weight(w_out, lambda i, j: out_scale[layer, i, 0, j], layer, first, count)
+
+    unfold_rows(slab_in, x_ref)
+    ff = w_out.shape[2]
+    chunk = slab_ref.shape[1]
     for n in range(ff // chunk):
-        for half in range(2):
-            cols = pl.ds(half * ff + n * chunk, chunk)
-            loads.append(
-                pltpu.make_async_copy(
-                    win_hbm.at[layer, :, cols], win.at[:, cols], sems.at[len(loads)]
-                )
-            )
-    for m in range(PIECES):
-        cols = pl.ds(m * chunk, chunk)
-        loads.append(
-            pltpu.make_async_copy(
-                wout_hbm.at[layer, :, cols], wout.at[:, cols], sems.at[len(loads)]
-            )
-        )
-    for load in loads:
-        load.start()
-    unfold_rows(slab_in, x_ref)
-    at = 0
-    for n in range(ff // chunk):
-        loads[at].wait()
-        gate = jnp.dot(
-            x_ref[...], win[:, n * chunk : (n + 1) * chunk], preferred_element_type=jnp.float32
-        )
-        loads[at + 1].wait()
-        up = jnp.dot(
-            x_ref[...],
-            win[:, ff + n * chunk : ff + (n + 1) * chunk],
-            preferred_element_type=jnp.float32,
-        )
-        at += 2
+        gate = jnp.dot(x_ref[...], into(n * chunk, chunk), preferred_element_type=jnp.float32)
+        up = jnp.dot(x_ref[...], into(ff + n * chunk, chunk), preferred_element_type=jnp.float32)
         hid[:, n * chunk : (n + 1) * chunk] = (gate / (1.0 + jnp.exp(-gate)) * up).astype(
             jnp.bfloat16
         )
     for m in range(PIECES):
-        loads[at].wait()
-        at += 1
         answer = jnp.dot(
-            hid[...], wout[:, m * chunk : (m + 1) * chunk], preferred_element_type=jnp.float32
+            hid[...], out_of(m * chunk, chunk), preferred_element_type=jnp.float32
         ).astype(jnp.bfloat16)
         stack_piece(stack_ref, answer, m)
     fold_rows(stack_ref, slab_ref)
 
 
 VM = pl.BlockSpec(memory_space=pltpu.VMEM)
-
-
-def expert(layer, slab, in_weight, out_weight):
+SM = pl.BlockSpec(memory_space=pltpu.SMEM)
+HB = pl.BlockSpec(memory_space=pltpu.HBM)
+
+
+def expert(layer, slab, weights):
+    w_in, in_scale, w_out, out_scale = weights
     rows, piece = slab.shape
     slots = rows // PIECES
-    _, width, gated = in_weight.shape
-    ff = gated // 2
+    width, ff = w_in.shape[2], w_out.shape[2]
     return pl.pallas_call(
         functools.partial(expert_kernel, layer),
-        in_specs=[VM, pl.BlockSpec(memory_space=pl.ANY), pl.BlockSpec(memory_space=pl.ANY)],
+        in_specs=[SM, SM, VM, VM, VM],
         out_specs=VM,
         out_shape=jax.ShapeDtypeStruct(slab.shape, jnp.bfloat16),
         scratch_shapes=[
             pltpu.VMEM((slots, width), jnp.bfloat16),
-            pltpu.VMEM((width, gated), jnp.bfloat16),
-            pltpu.VMEM((ff, width), jnp.bfloat16),
             pltpu.VMEM((slots, ff), jnp.bfloat16),
             pltpu.VMEM(slab.shape, jnp.bfloat16),
-            pltpu.SemaphoreType.DMA((2 * (ff // 256) + PIECES,)),
         ],
-        compiler_params=pltpu.CompilerParams(vmem_limit_bytes=40 * MIB),
+        compiler_params=pltpu.CompilerParams(vmem_limit_bytes=20 * MIB),
         cost_estimate=pl.CostEstimate(
             flops=6 * slots * width * ff,
             bytes_accessed=6 * width * ff + 4 * slots * width,
             transcendentals=slots * ff,
         ),
         name="expert",
-    )(slab, in_weight, out_weight)
+    )(in_scale, out_scale, slab, w_in, w_out)
+
+
+def hbm(array):
+    return pltpu.with_memory_space_constraint(array, pltpu.HBM)
 
 
 def exchange(slab, devices):
@@ -282,22 +265,35 @@
     stream_type = jax.ShapeDtypeStruct((count, width), jnp.bfloat16)
     rows = pltpu.VMEM((slots, width), jnp.bfloat16)
     stack = pltpu.VMEM((slots * PIECES, piece), jnp.bfloat16)
-    params = pltpu.CompilerParams(vmem_limit_bytes=24 * MIB)
-
+    params = pltpu.CompilerParams(vmem_limit_bytes=12 * MIB)
+
+    small = (
+        pltpu.VMEM((count, width), jnp.bfloat16),
+        pltpu.VMEM(norm_gain.shape, jnp.float32),
+        pltpu.VMEM(routes_t.shape, jnp.int32),
+        pltpu.VMEM(placement.shape, jnp.int32),
+    )
     slab = pl.pallas_call(
         first_kernel,
-        in_specs=[VM] * 4,
+        in_specs=[HB] * 4,
         out_specs=VM,
         out_shape=slab_type,
-        scratch_shapes=[stack],
+        scratch_shapes=[*small, stack, pltpu.SemaphoreType.DMA((4,))],
         compiler_params=params,
+        cost_estimate=pl.CostEstimate(
+            flops=8 * 10**9, bytes_accessed=8 * 10**6, transcendentals=0
+        ),
         name="first",
-    )(tokens, norm_gain, routes_t, placement)
-    in_weight = dequant(w_in, in_scale)
-    out_weight = dequant(w_out, out_scale)
+    )(*[hbm(a) for a in (tokens, norm_gain, routes_t, placement)])
+    weights = (
+        w_in,
+        jnp.transpose(in_scale, (0, 3, 1, 2)),
+        w_out,
+        jnp.transpose(out_scale, (0, 2, 1, 3)),
+    )
     stream = tokens
     for layer in range(layers):
-        answers = expert(layer, exchange(slab, devices), in_weight, out_weight)
+        answers = expert(layer, exchange(slab, devices), weights)
         back = exchange(answers, devices)
         if layer + 1 < layers:
             slab, stream = pl.pallas_call(

time: 163 us -> 139 us (0.85)
  Pallas kernels: 52.9 us -> 18.1 us
  blocking collectives: 90.6 us -> 121 us
  starting transfers between devices: 11.5 us -> 0 us
  local copies, waits for them, and re-layouts: 7.11 us -> 0.06 us
    pallas_call x5 -> x3, Pallas kernels: 48.7 us -> 13.9 us  [the longest x2 11.5 us: expert(): pl.pallas_call(functools.partial(expert_kernel, layer), in_specs=[SM, SM,...]
    all_to_all x3 -> x4, blocking collectives: 90.6 us -> 121 us  [exchange(): moved = lax.all_to_all(split, AXES, split_axis=0, concat_axis=0, tiled=True)]
    all_to_all x1 -> x0, starting transfers between devices: 11.5 us -> none  [exchange(): moved = lax.all_to_all(split, AXES, split_axis=0, concat_axis=0, tiled=True)]
    unnamed x26 -> x24, local copies, waits for them, and re-layouts: 6.51 us -> 0.06 us
  transfers between devices with their start and end apart: 1 -> 0, of which waited for: 0 -> 0; matrix products, arithmetic and copies ran while one was open for 1% -> 0% of each run, Pallas kernels for 14% -> 0%
where the time goes in v3:
time: 139 us
  blocking collectives  121 us (87%)
  Pallas kernels  18.1 us (13%)
    all_to_all x4, blocking collectives, exchange(): moved = lax.all_to_all(split, AXES, split_axis=0, concat_axis=0, tiled=True)  121 us
    pallas_call x2, Pallas kernels, expert(): pl.pallas_call(functools.partial(expert_kernel, layer), in_specs=[SM, SM,...  11.5 us

profile of v3, /device:TPU:1, one launch (start us, length us, event | category | flops | bytes accessed | tf_op | source)
XLA Modules:
  0.0 139.3 jit_solution(5310510813583442487)
XLA Ops:
  0.0 0.0 slice-start.2
  0.0 0.0 slice-start.4
  0.0 2.4 %first.1 = bf16[3072,256]{1,0:T(8,128)(2,1)S(1)} custom-call(bf16[32,2048]{1,0:T(8,128)(2,1)} %stream_ref.1, f32[2,2048]{1,0:T(2,128)} %gain_ref.1, s32[2,8,32]{2,1,0:T(8,128)} %bitcast.26, s32[2,128]{1,0:T(2,128)} %place_ref.3), custom_call_target="tpu_custom_call" | custom-call | flops 8000000000 | bytes 8000000 | tf_op jit(solution)/shard_map/first/pallas_call | solution.py:276
  2.5 0.0 copy-start.1
  2.5 0.0 copy-start.4
  2.5 35.4 %all_to_all.20 = bf16[128,24,256]{2,1,0:T(8,128)(2,1)S(1)} all-to-all(bf16[128,24,256]{2,1,0:T(8,128)(2,1)S(1)} %bitcast.23), channel_id=1, replica_groups=mesh['dp'=8,'expert'=16] {'dp','expert'}, dimensions={0} | all-to-all | bytes 3145728 | tf_op jit(solution)/shard_map/all_to_all | solution.py:253
  37.9 0.0 slice-done
  37.9 0.0 slice-done.3
  38.0 0.0 slice-done.1
  38.0 0.0 slice-done.2
  38.0 5.8 %expert.2 = bf16[3072,256]{1,0:T(8,128)(2,1)S(1)} custom-call(f32[2,12,1,16]{3,2,1,0:T(1,128)S(1)} %bitcast.24, f32[2,6,1,16]{3,2,1,0:T(1,128)S(1)} %bitcast.31, bf16[3072,256]{1,0:T(8,128)(2,1)S(1)} %bitcast.18, bf16[2,1,2048,1536]{3,2,1,0:T(8,128)(2,1)S(1)} %bitcast.13, bf16[2,1,768,2048]{3,2,1,0:T(8,128)(2,1)S(1)} %bitcast.15), custom_call_target="tpu_custom_call" | custom-call | flops 3623878656 | bytes 12582912 | tf_op jit(solution)/shard_map/expert/pallas_call | solution.py:227
  43.8 0.0 copy-start
  43.8 0.0 copy-start.2
  43.8 0.0 copy-start.3
  43.8 0.0 copy-start.5
  43.8 0.0 copy-start.6
  43.8 28.6 %all_to_all.21 = bf16[128,24,256]{2,1,0:T(8,128)(2,1)S(1)} all-to-all(bf16[128,24,256]{2,1,0:T(8,128)(2,1)S(1)} %bitcast.19), channel_id=1, replica_groups=mesh['dp'=8,'expert'=16] {'dp','expert'}, dimensions={0} | all-to-all | bytes 3145728 | tf_op jit(solution)/shard_map/all_to_all | solution.py:253
  72.4 0.0 copy-done.5
  72.4 0.0 copy-done.6
  72.4 2.4 %middle.1 = (bf16[3072,256]{1,0:T(8,128)(2,1)S(1)}, bf16[32,2048]{1,0:T(8,128)(2,1)S(1)}) custom-call(bf16[3072,256]{1,0:T(8,128)(2,1)S(1)} %bitcast.16, bf16[32,2048]{1,0:T(8,128)(2,1)S(1)} %copy-done, f32[2,2048]{1,0:T(2,128)S(1)} %copy-done.5, s32[2,8,32]{2,1,0:T(8,128)S(1)} %bitcast.27, f32[2,8,32]{2,1,0:T(8,128)S(1)} %bitcast.29, s32[2,128]{1,0:T(2,128)S(1)} %copy-done.6), custom_call_target="tpu_custom_call" | custom-call | tf_op jit(solution)/shard_map/middle/pallas_call | solution.py:299
  74.9 28.5 %all_to_all.22 = bf16[128,24,256]{2,1,0:T(8,128)(2,1)S(1)} all-to-all(bf16[128,24,256]{2,1,0:T(8,128)(2,1)S(1)} %bitcast.22), channel_id=1, replica_groups=mesh['dp'=8,'expert'=16] {'dp','expert'}, dimensions={0} | all-to-all | bytes 3145728 | tf_op jit(solution)/shard_map/all_to_all | solution.py:253
  103.3 5.7 %expert.3 = bf16[3072,256]{1,0:T(8,128)(2,1)S(1)} custom-call(f32[2,12,1,16]{3,2,1,0:T(1,128)S(1)} %bitcast.25, f32[2,6,1,16]{3,2,1,0:T(1,128)S(1)} %bitcast.32, bf16[3072,256]{1,0:T(8,128)(2,1)S(1)} %bitcast.20, bf16[2,1,2048,1536]{3,2,1,0:T(8,128)(2,1)S(1)} %bitcast.13, bf16[2,1,768,2048]{3,2,1,0:T(8,128)(2,1)S(1)} %bitcast.15), custom_call_target="tpu_custom_call" | custom-call | flops 3623878656 | bytes 12582912 | tf_op jit(solution)/shard_map/expert/pallas_call | solution.py:227
  109.1 28.5 %all_to_all.23 = bf16[128,24,256]{2,1,0:T(8,128)(2,1)S(1)} all-to-all(bf16[128,24,256]{2,1,0:T(8,128)(2,1)S(1)} %bitcast.21), channel_id=1, replica_groups=mesh['dp'=8,'expert'=16] {'dp','expert'}, dimensions={0} | all-to-all | bytes 3145728 | tf_op jit(solution)/shard_map/all_to_all | solution.py:253
  137.5 1.8 %last.1 = bf16[32,2048]{1,0:T(8,128)(2,1)} custom-call(bf16[3072,256]{1,0:T(8,128)(2,1)S(1)} %bitcast.17, bf16[32,2048]{1,0:T(8,128)(2,1)S(1)} %get-tuple-element.8.stream_ref, s32[2,8,32]{2,1,0:T(8,128)S(1)} %bitcast.28, f32[2,8,32]{2,1,0:T(8,128)S(1)} %bitcast.30, s32[2,128]{1,0:T(2,128)S(1)} %copy-done.6), custom_call_target="tpu_custom_call" | custom-call | tf_op jit(solution)/shard_map/last/pallas_call | solution.py:309
  (11 shorter events, 0.0 us)
Async XLA Ops:
  0.0 37.9 %slice-start = ((s8[12582912]{0:T(1024)(128)(4,1)}), s8[4194304]{0:T(1024)(128)(4,1)S(1)}, s32[]{:S(2)}) async-start(s8[12582912]{0:T(1024)(128)(4,1)} %bitcast.12), calls=%async_computation.4 | async-start | bytes 8388608
  0.0 37.9 %slice-start.3 = ((s8[6291456]{0:T(1024)(128)(4,1)}), s8[4194304]{0:T(1024)(128)(4,1)S(1)}, s32[]{:S(2)}) async-start(s8[6291456]{0:T(1024)(128)(4,1)} %bitcast.14), calls=%async_computation.7 | async-start | bytes 8388608
  0.0 37.9 %slice-start.1 = ((s8[12582912]{0:T(1024)(128)(4,1)}), s8[4194304]{0:T(1024)(128)(4,1)S(1)}, s32[]{:S(2)}) async-start(s8[12582912]{0:T(1024)(128)(4,1)} %bitcast.12), calls=%async_computation.5 | async-start | bytes 8388608
  0.0 37.9 %slice-start.2 = ((s8[12582912]{0:T(1024)(128)(4,1)}), s8[4194304]{0:T(1024)(128)(4,1)S(1)}, s32[]{:S(2)}) async-start(s8[12582912]{0:T(1024)(128)(4,1)} %bitcast.12), calls=%async_computation.6 | async-start | bytes 8388608
  0.0 37.9 %slice-start.4 = ((s8[6291456]{0:T(1024)(128)(4,1)}), s8[2097152]{0:T(1024)(128)(4,1)S(1)}, s32[]{:S(2)}) async-start(s8[6291456]{0:T(1024)(128)(4,1)} %bitcast.14), calls=%async_computation.8 | async-start | bytes 4194304
  2.5 35.5 %copy-start.1 = (f32[2,1,16,12]{2,1,3,0:T(1,128)S(1)}, f32[2,1,16,12]{2,1,3,0:T(1,128)}, u32[]{:S(2)}) copy-start(f32[2,1,16,12]{2,1,3,0:T(1,128)} %param.15) | copy-start | bytes 4612
  2.5 35.5 %copy-start.4 = (f32[2,1,6,16]{3,1,2,0:T(1,128)S(1)}, f32[2,1,6,16]{3,1,2,0:T(1,128)}, u32[]{:S(2)}) copy-start(f32[2,1,6,16]{3,1,2,0:T(1,128)} %param.17) | copy-start | bytes 2308
  43.8 28.6 %copy-start = (bf16[32,2048]{1,0:T(8,128)(2,1)S(1)}, bf16[32,2048]{1,0:T(8,128)(2,1)}, u32[]{:S(2)}) copy-start(bf16[32,2048]{1,0:T(8,128)(2,1)} %stream_ref.1) | copy-start | bytes 393220
  43.8 28.6 %copy-start.2 = (s32[2,32,8]{1,2,0:T(8,128)S(1)}, s32[2,32,8]{1,2,0:T(8,128)}, u32[]{:S(2)}) copy-start(s32[2,32,8]{1,2,0:T(8,128)} %param.11) | copy-start | bytes 6148
  43.8 28.6 %copy-start.3 = (f32[2,32,8]{1,2,0:T(8,128)S(1)}, f32[2,32,8]{1,2,0:T(8,128)}, u32[]{:S(2)}) copy-start(f32[2,32,8]{1,2,0:T(8,128)} %param.12) | copy-start | bytes 6148
  43.8 28.6 %copy-start.5 = (f32[2,2048]{1,0:T(2,128)S(1)}, f32[2,2048]{1,0:T(2,128)}, u32[]{:S(2)}) copy-start(f32[2,2048]{1,0:T(2,128)} %gain_ref.1) | copy-start | bytes 49156
  43.8 28.6 %copy-start.6 = (s32[2,128]{1,0:T(2,128)S(1)}, s32[2,128]{1,0:T(2,128)}, u32[]{:S(2)}) copy-start(s32[2,128]{1,0:T(2,128)} %place_ref.3) | copy-start | bytes 3076

commit v4 on v3

--- a/solution.py
+++ b/solution.py
@@ -102,30 +102,57 @@
     return (stream_f * scale * gain).astype(jnp.bfloat16)
 
 
-def send_rows(pick, normed, stack_ref, slab_ref):
+def build_spread(select, wide_ref, spread_ref):
+    tokens, slots = select.shape
+    lanes = tokens * PIECES
+    token = lax.broadcasted_iota(jnp.int32, (tokens, lanes), 0)
+    lane = lax.broadcasted_iota(jnp.int32, (tokens, lanes), 1)
+    tile = jnp.where((lane & (tokens - 1)) == token, 1.0, 0.0).astype(jnp.bfloat16)
+    wide_ref[...] = jnp.dot(
+        jnp.transpose(select).astype(jnp.bfloat16), tile, preferred_element_type=jnp.float32
+    )
+    own = lax.broadcasted_iota(jnp.int32, (PIECES, lanes), 0)
+    piece = lax.broadcasted_iota(jnp.int32, (PIECES, lanes), 1) // tokens
+    mine = own == piece
+    for s in range(0, slots, 2):
+        pair = [
+            jnp.where(mine, jnp.broadcast_to(wide_ref[i : i + 1, :], (PIECES, lanes)), 0.0)
+            for i in (s, s + 1)
+        ]
+        spread_ref[s * PIECES : (s + 2) * PIECES, :] = jnp.concatenate(pair, axis=0).astype(
+            jnp.bfloat16
+        )
+
+
+def send_rows(spread_ref, normed, slab_ref):
     piece = slab_ref.shape[1]
-    for p in range(PIECES):
-        rows = jnp.dot(
-            pick, normed[:, p * piece : (p + 1) * piece], preferred_element_type=jnp.float32
+    stacked = jnp.concatenate(
+        [normed[:, p * piece : (p + 1) * piece] for p in range(PIECES)], axis=0
+    )
+    span = GROUP * PIECES
+    for b in range(slab_ref.shape[0] // span):
+        at = slice(b * span, (b + 1) * span)
+        slab_ref[at, :] = jnp.dot(
+            spread_ref[at, :], stacked, preferred_element_type=jnp.float32
         ).astype(jnp.bfloat16)
-        stack_piece(stack_ref, rows, p)
-    fold_rows(stack_ref, slab_ref)
+
+
+def split_weight(weight):
+    high = weight.astype(jnp.bfloat16)
+    low = (weight - high.astype(jnp.float32)).astype(jnp.bfloat16)
+    return jnp.concatenate([high, low], axis=0)
 
 
 def mix(weight, slab_ref, rows_ref):
     unfold_rows(slab_ref, rows_ref)
-    high = weight.astype(jnp.bfloat16)
-    low = (weight - high.astype(jnp.float32)).astype(jnp.bfloat16)
-    both = jnp.dot(
-        jnp.concatenate([high, low], axis=0), rows_ref[...], preferred_element_type=jnp.float32
-    )
-    tokens = weight.shape[0]
+    both = jnp.dot(weight, rows_ref[...], preferred_element_type=jnp.float32)
+    tokens = weight.shape[0] // 2
     return both[:tokens] + both[tokens:]
 
 
 def first_kernel(
     tokens_hbm, gain_hbm, routes_hbm, place_hbm, slab_ref,
-    tokens_ref, gain_ref, routes_ref, place_ref, stack_ref, sems,
+    tokens_ref, gain_ref, routes_ref, place_ref, wide_ref, spread_ref, sems,
 ):
     loads = [
         pltpu.make_async_copy(src, dst, sems.at[i])
@@ -143,32 +170,25 @@
     loads[0].wait()
     loads[1].wait()
     select, _ = slot_tables(routes_ref[0], place_ref[0:1, :], None)
-    pick = jnp.transpose(select).astype(jnp.bfloat16)
+    build_spread(select, wide_ref, spread_ref)
     loads[2].wait()
     loads[3].wait()
     normed = normalise(tokens_ref[...].astype(jnp.float32), gain_ref[0:1, :])
-    send_rows(pick, normed, stack_ref, slab_ref)
+    send_rows(spread_ref, normed, slab_ref)
 
 
 def middle_kernel(
-    layer, slab_in, stream_ref, gain_ref, routes_ref, gates_ref, place_ref,
-    slab_ref, out_ref, rows_ref, stack_ref,
+    layer, slab_in, stream_ref, gain_ref, weight_ref, spread_ref, slab_ref, out_ref, rows_ref
 ):
-    _, weight = slot_tables(routes_ref[layer], place_ref[layer : layer + 1, :], gates_ref[layer])
-    select, _ = slot_tables(routes_ref[layer + 1], place_ref[layer + 1 : layer + 2, :], None)
-    pick = jnp.transpose(select).astype(jnp.bfloat16)
-    mixed = mix(weight, slab_in, rows_ref)
+    mixed = mix(weight_ref[...], slab_in, rows_ref)
     stream = (stream_ref[...].astype(jnp.float32) + mixed).astype(jnp.bfloat16)
     out_ref[...] = stream
     normed = normalise(stream.astype(jnp.float32), gain_ref[layer + 1 : layer + 2, :])
-    send_rows(pick, normed, stack_ref, slab_ref)
-
-
-def last_kernel(
-    layer, slab_in, stream_ref, routes_ref, gates_ref, place_ref, out_ref, rows_ref
-):
-    _, weight = slot_tables(routes_ref[layer], place_ref[layer : layer + 1, :], gates_ref[layer])
-    mixed = mix(weight, slab_in, rows_ref)
+    send_rows(spread_ref, normed, slab_ref)
+
+
+def last_kernel(slab_in, stream_ref, weight_ref, out_ref, rows_ref):
+    mixed = mix(weight_ref[...], slab_in, rows_ref)
     out_ref[...] = (stream_ref[...].astype(jnp.float32) + mixed).astype(jnp.bfloat16)
 
 
@@ -189,7 +209,8 @@
 
 
 def expert_kernel(
-    layer, in_scale, out_scale, slab_in, w_in, w_out, slab_ref, x_ref, hid, stack_ref
+    layer, in_scale, out_scale, slab_in, w_in, w_out, routes_ref, gates_ref, place_ref,
+    slab_ref, weight_ref, *rest,
 ):
     def into(first, count):
         return block_weight(w_in, lambda i, j: in_scale[layer, j, 0, i], layer, first, count)
@@ -197,7 +218,16 @@
     def out_of(first, count):
         return block_weight(w_out, lambda i, j: out_scale[layer, i, 0, j], layer, first, count)
 
+    x_ref, hid, stack_ref = rest[-3:]
     unfold_rows(slab_in, x_ref)
+    _, weight = slot_tables(routes_ref[layer], place_ref[layer : layer + 1, :], gates_ref[layer])
+    weight_ref[...] = split_weight(weight)
+    if len(rest) > 3:
+        spread_ref, wide_ref = rest[:2]
+        select, _ = slot_tables(
+            routes_ref[layer + 1], place_ref[layer + 1 : layer + 2, :], None
+        )
+        build_spread(select, wide_ref, spread_ref)
     ff = w_out.shape[2]
     chunk = slab_ref.shape[1]
     for n in range(ff // chunk):
@@ -219,21 +249,30 @@
 HB = pl.BlockSpec(memory_space=pltpu.HBM)
 
 
-def expert(layer, slab, weights):
+def expert(layer, layers, slab, weights, tables):
     w_in, in_scale, w_out, out_scale = weights
     rows, piece = slab.shape
     slots = rows // PIECES
     width, ff = w_in.shape[2], w_out.shape[2]
+    tokens = tables[0].shape[2]
+    outs = [
+        jax.ShapeDtypeStruct(slab.shape, jnp.bfloat16),
+        jax.ShapeDtypeStruct((2 * tokens, slots), jnp.bfloat16),
+    ]
+    scratch = [
+        pltpu.VMEM((slots, width), jnp.bfloat16),
+        pltpu.VMEM((slots, ff), jnp.bfloat16),
+        pltpu.VMEM(slab.shape, jnp.bfloat16),
+    ]
+    if layer + 1 < layers:
+        outs.append(jax.ShapeDtypeStruct((rows, tokens * PIECES), jnp.bfloat16))
+        scratch.insert(0, pltpu.VMEM((slots, tokens * PIECES), jnp.float32))
     return pl.pallas_call(
         functools.partial(expert_kernel, layer),
-        in_specs=[SM, SM, VM, VM, VM],
-        out_specs=VM,
-        out_shape=jax.ShapeDtypeStruct(slab.shape, jnp.bfloat16),
-        scratch_shapes=[
-            pltpu.VMEM((slots, width), jnp.bfloat16),
-            pltpu.VMEM((slots, ff), jnp.bfloat16),
-            pltpu.VMEM(slab.shape, jnp.bfloat16),
-        ],
+        in_specs=[SM, SM] + [VM] * 6,
+        out_specs=[VM] * len(outs),
+        out_shape=outs,
+        scratch_shapes=scratch,
         compiler_params=pltpu.CompilerParams(vmem_limit_bytes=20 * MIB),
         cost_estimate=pl.CostEstimate(
             flops=6 * slots * width * ff,
@@ -241,7 +280,7 @@
             transcendentals=slots * ff,
         ),
         name="expert",
-    )(in_scale, out_scale, slab, w_in, w_out)
+    )(in_scale, out_scale, slab, w_in, w_out, *tables)
 
 
 def hbm(array):
@@ -264,7 +303,8 @@
     slab_type = jax.ShapeDtypeStruct((slots * PIECES, piece), jnp.bfloat16)
     stream_type = jax.ShapeDtypeStruct((count, width), jnp.bfloat16)
     rows = pltpu.VMEM((slots, width), jnp.bfloat16)
-    stack = pltpu.VMEM((slots * PIECES, piece), jnp.bfloat16)
+    wide = pltpu.VMEM((slots, count * PIECES), jnp.float32)
+    spread = pltpu.VMEM((slots * PIECES, count * PIECES), jnp.bfloat16)
     params = pltpu.CompilerParams(vmem_limit_bytes=12 * MIB)
 
     small = (
@@ -278,7 +318,7 @@
         in_specs=[HB] * 4,
         out_specs=VM,
         out_shape=slab_type,
-        scratch_shapes=[*small, stack, pltpu.SemaphoreType.DMA((4,))],
+        scratch_shapes=[*small, wide, spread, pltpu.SemaphoreType.DMA((4,))],
         compiler_params=params,
         cost_estimate=pl.CostEstimate(
             flops=8 * 10**9, bytes_accessed=8 * 10**6, transcendentals=0
@@ -293,28 +333,30 @@
     )
     stream = tokens
     for layer in range(layers):
-        answers = expert(layer, exchange(slab, devices), weights)
+        answers, weight, *spreads = expert(
+            layer, layers, exchange(slab, devices), weights, (routes_t, gates_t, placement)
+        )
         back = exchange(answers, devices)
         if layer + 1 < layers:
             slab, stream = pl.pallas_call(
                 functools.partial(middle_kernel, layer),
-                in_specs=[VM] * 6,
+                in_specs=[VM] * 5,
                 out_specs=(VM, VM),
                 out_shape=(slab_type, stream_type),
-                scratch_shapes=[rows, stack],
+                scratch_shapes=[rows],
                 compiler_params=params,
                 name="middle",
-            )(back, stream, norm_gain, routes_t, gates_t, placement)
+            )(back, stream, norm_gain, weight, spreads[0])
         else:
             stream = pl.pallas_call(
-                functools.partial(last_kernel, layer),
-                in_specs=[VM] * 5,
+                last_kernel,
+                in_specs=[VM] * 3,
                 out_specs=VM,
                 out_shape=stream_type,
                 scratch_shapes=[rows],
                 compiler_params=params,
                 name="last",
-            )(back, stream, routes_t, gates_t, placement)
+            )(back, stream, weight)
     return stream
 
 

time: 139 us -> 139 us (level)
  no operation moved by 1% of the time
where the time goes in v4:
time: 139 us
  blocking collectives  121 us (87%)
  Pallas kernels  18 us (13%)
    all_to_all x4, blocking collectives, exchange(): moved = lax.all_to_all(split, AXES, split_axis=0, concat_axis=0, tiled=True)  121 us
    pallas_call x2, Pallas kernels, expert(): pl.pallas_call(functools.partial(expert_kernel, layer), in_specs=[SM, SM]...  12.5 us

profile of v4, /device:TPU:1, one launch (start us, length us, event | category | flops | bytes accessed | tf_op | source)
XLA Modules:
  0.0 139.1 jit_solution(17783323473333706663)
XLA Ops:
  0.0 0.0 slice-start.2
  0.0 0.0 slice-start.4
  0.0 2.4 %first.1 = bf16[3072,256]{1,0:T(8,128)(2,1)S(1)} custom-call(bf16[32,2048]{1,0:T(8,128)(2,1)} %stream_ref.1, f32[2,2048]{1,0:T(2,128)} %gain_ref.1, s32[2,8,32]{2,1,0:T(8,128)} %bitcast.26, s32[2,128]{1,0:T(2,128)} %place_ref.3), custom_call_target="tpu_custom_call" | custom-call | flops 8000000000 | bytes 8000000 | tf_op jit(solution)/shard_map/first/pallas_call | solution.py:316
  2.4 0.0 copy-start.1
  2.4 0.0 copy-start.2
  2.4 0.0 copy-start.3
  2.4 0.0 copy-start.4
  2.5 0.0 copy-start.6
  2.5 35.4 %all_to_all.20 = bf16[128,24,256]{2,1,0:T(8,128)(2,1)S(1)} all-to-all(bf16[128,24,256]{2,1,0:T(8,128)(2,1)S(1)} %bitcast.23), channel_id=1, replica_groups=mesh['dp'=8,'expert'=16] {'dp','expert'}, dimensions={0} | all-to-all | bytes 3145728 | tf_op jit(solution)/shard_map/all_to_all | solution.py:292
  37.9 0.0 slice-done
  37.9 0.0 slice-done.3
  37.9 0.0 slice-done.1
  37.9 0.0 slice-done.2
  37.9 0.0 slice-done.4
  38.0 6.5 %expert.2 = (bf16[3072,256]{1,0:T(8,128)(2,1)S(1)}, bf16[64,384]{1,0:T(8,128)(2,1)S(1)}, bf16[3072,256]{1,0:T(8,128)(2,1)S(1)}) custom-call(f32[2,12,1,16]{3,2,1,0:T(1,128)S(1)} %bitcast.24, f32[2,6,1,16]{3,2,1,0:T(1,128)S(1)} %bitcast.31, bf16[3072,256]{1,0:T(8,128)(2,1)S(1)} %bitcast.18, bf16[2,1,2048,1536]{3,2,1,0:T(8,128)(2,1)S(1)} %bitcast.13, ...), custom_call_target="tpu_custom_call" | custom-call | flops 3623878656 | bytes 12582912 | tf_op jit(solution)/shard_map/expert/pallas_call | solution.py:270
  44.5 0.0 copy-start
  44.5 0.0 copy-start.5
  44.6 28.6 %all_to_all.21 = bf16[128,24,256]{2,1,0:T(8,128)(2,1)S(1)} all-to-all(bf16[128,24,256]{2,1,0:T(8,128)(2,1)S(1)} %bitcast.21), channel_id=1, replica_groups=mesh['dp'=8,'expert'=16] {'dp','expert'}, dimensions={0} | all-to-all | bytes 3145728 | tf_op jit(solution)/shard_map/all_to_all | solution.py:292
  73.1 0.0 copy-done
  73.1 1.5 %middle.1 = (bf16[3072,256]{1,0:T(8,128)(2,1)S(1)}, bf16[32,2048]{1,0:T(8,128)(2,1)S(1)}) custom-call(bf16[3072,256]{1,0:T(8,128)(2,1)S(1)} %bitcast.16, bf16[32,2048]{1,0:T(8,128)(2,1)S(1)} %copy-done, f32[2,2048]{1,0:T(2,128)S(1)} %copy-done.5, bf16[64,384]{1,0:T(8,128)(2,1)S(1)} %get-tuple-element.13.weight_ref, ...), custom_call_target="tpu_custom_call" | custom-call | tf_op jit(solution)/shard_map/middle/pallas_call | solution.py:341
  74.7 28.5 %all_to_all.22 = bf16[128,24,256]{2,1,0:T(8,128)(2,1)S(1)} all-to-all(bf16[128,24,256]{2,1,0:T(8,128)(2,1)S(1)} %bitcast.20), channel_id=1, replica_groups=mesh['dp'=8,'expert'=16] {'dp','expert'}, dimensions={0} | all-to-all | bytes 3145728 | tf_op jit(solution)/shard_map/all_to_all | solution.py:292
  103.1 6.0 %expert.3 = (bf16[3072,256]{1,0:T(8,128)(2,1)S(1)}, bf16[64,384]{1,0:T(8,128)(2,1)S(1)}) custom-call(f32[2,12,1,16]{3,2,1,0:T(1,128)S(1)} %bitcast.25, f32[2,6,1,16]{3,2,1,0:T(1,128)S(1)} %bitcast.32, bf16[3072,256]{1,0:T(8,128)(2,1)S(1)} %bitcast.19, bf16[2,1,2048,1536]{3,2,1,0:T(8,128)(2,1)S(1)} %bitcast.13, bf16[2,1,768,2048]{3,2,1,0:T(8,128)(2,1)S(1)} %bitcast.15, ...), custom_call_target="tpu_custom_call" | custom-call | flops 3623878656 | bytes 12582912 | tf_op jit(solution)/shard_map/expert/pallas_call | solution.py:270
  109.1 28.5 %all_to_all.23 = bf16[128,24,256]{2,1,0:T(8,128)(2,1)S(1)} all-to-all(bf16[128,24,256]{2,1,0:T(8,128)(2,1)S(1)} %bitcast.22), channel_id=1, replica_groups=mesh['dp'=8,'expert'=16] {'dp','expert'}, dimensions={0} | all-to-all | bytes 3145728 | tf_op jit(solution)/shard_map/all_to_all | solution.py:292
  137.6 1.5 %last.1 = bf16[32,2048]{1,0:T(8,128)(2,1)} custom-call(bf16[3072,256]{1,0:T(8,128)(2,1)S(1)} %bitcast.17, bf16[32,2048]{1,0:T(8,128)(2,1)S(1)} %get-tuple-element.17.stream_ref, bf16[64,384]{1,0:T(8,128)(2,1)S(1)} %get-tuple-element.18.weight_ref), custom_call_target="tpu_custom_call" | custom-call | tf_op jit(solution)/shard_map/last/pallas_call | solution.py:351
  (11 shorter events, 0.0 us)
Async XLA Ops:
  0.0 37.9 %slice-start = ((s8[12582912]{0:T(1024)(128)(4,1)}), s8[4194304]{0:T(1024)(128)(4,1)S(1)}, s32[]{:S(2)}) async-start(s8[12582912]{0:T(1024)(128)(4,1)} %bitcast.12), calls=%async_computation.4 | async-start | bytes 8388608
  0.0 37.9 %slice-start.3 = ((s8[6291456]{0:T(1024)(128)(4,1)}), s8[4194304]{0:T(1024)(128)(4,1)S(1)}, s32[]{:S(2)}) async-start(s8[6291456]{0:T(1024)(128)(4,1)} %bitcast.14), calls=%async_computation.7 | async-start | bytes 8388608
  0.0 37.9 %slice-start.1 = ((s8[12582912]{0:T(1024)(128)(4,1)}), s8[4194304]{0:T(1024)(128)(4,1)S(1)}, s32[]{:S(2)}) async-start(s8[12582912]{0:T(1024)(128)(4,1)} %bitcast.12), calls=%async_computation.5 | async-start | bytes 8388608
  0.0 37.9 %slice-start.2 = ((s8[12582912]{0:T(1024)(128)(4,1)}), s8[4194304]{0:T(1024)(128)(4,1)S(1)}, s32[]{:S(2)}) async-start(s8[12582912]{0:T(1024)(128)(4,1)} %bitcast.12), calls=%async_computation.6 | async-start | bytes 8388608
  0.0 37.9 %slice-start.4 = ((s8[6291456]{0:T(1024)(128)(4,1)}), s8[2097152]{0:T(1024)(128)(4,1)S(1)}, s32[]{:S(2)}) async-start(s8[6291456]{0:T(1024)(128)(4,1)} %bitcast.14), calls=%async_computation.8 | async-start | bytes 4194304
  2.4 35.5 %copy-start.1 = (f32[2,1,16,12]{2,1,3,0:T(1,128)S(1)}, f32[2,1,16,12]{2,1,3,0:T(1,128)}, u32[]{:S(2)}) copy-start(f32[2,1,16,12]{2,1,3,0:T(1,128)} %param.15) | copy-start | bytes 4612
  2.4 35.5 %copy-start.2 = (s32[2,32,8]{1,2,0:T(8,128)S(1)}, s32[2,32,8]{1,2,0:T(8,128)}, u32[]{:S(2)}) copy-start(s32[2,32,8]{1,2,0:T(8,128)} %param.11) | copy-start | bytes 6148
  2.4 35.5 %copy-start.3 = (f32[2,32,8]{1,2,0:T(8,128)S(1)}, f32[2,32,8]{1,2,0:T(8,128)}, u32[]{:S(2)}) copy-start(f32[2,32,8]{1,2,0:T(8,128)} %param.12) | copy-start | bytes 6148
  2.4 35.5 %copy-start.4 = (f32[2,1,6,16]{3,1,2,0:T(1,128)S(1)}, f32[2,1,6,16]{3,1,2,0:T(1,128)}, u32[]{:S(2)}) copy-start(f32[2,1,6,16]{3,1,2,0:T(1,128)} %param.17) | copy-start | bytes 2308
  2.5 35.5 %copy-start.6 = (s32[2,128]{1,0:T(2,128)S(1)}, s32[2,128]{1,0:T(2,128)}, u32[]{:S(2)}) copy-start(s32[2,128]{1,0:T(2,128)} %place_ref.3) | copy-start | bytes 3076
  44.5 28.6 %copy-start = (bf16[32,2048]{1,0:T(8,128)(2,1)S(1)}, bf16[32,2048]{1,0:T(8,128)(2,1)}, u32[]{:S(2)}) copy-start(bf16[32,2048]{1,0:T(8,128)(2,1)} %stream_ref.1) | copy-start | bytes 393220
  44.5 28.6 %copy-start.5 = (f32[2,2048]{1,0:T(2,128)S(1)}, f32[2,2048]{1,0:T(2,128)}, u32[]{:S(2)}) copy-start(f32[2,2048]{1,0:T(2,128)} %gain_ref.1) | copy-start | bytes 49156

commit v5 on v4

--- a/solution.py
+++ b/solution.py
@@ -143,8 +143,7 @@
     return jnp.concatenate([high, low], axis=0)
 
 
-def mix(weight, slab_ref, rows_ref):
-    unfold_rows(slab_ref, rows_ref)
+def mix(weight, rows_ref):
     both = jnp.dot(weight, rows_ref[...], preferred_element_type=jnp.float32)
     tokens = weight.shape[0] // 2
     return both[:tokens] + both[tokens:]
@@ -178,17 +177,37 @@
 
 
 def middle_kernel(
-    layer, slab_in, stream_ref, gain_ref, weight_ref, spread_ref, slab_ref, out_ref, rows_ref
+    layer, slab_in, stream_hbm, gain_hbm, weight_hbm, spread_hbm, slab_ref, out_ref,
+    rows_ref, stream_ref, gain_ref, weight_ref, spread_ref, sems,
 ):
-    mixed = mix(weight_ref[...], slab_in, rows_ref)
+    loads = [
+        pltpu.make_async_copy(src, dst, sems.at[i])
+        for i, (src, dst) in enumerate(
+            (
+                (weight_hbm, weight_ref),
+                (stream_hbm, stream_ref),
+                (gain_hbm, gain_ref),
+                (spread_hbm, spread_ref),
+            )
+        )
+    ]
+    for load in loads:
+        load.start()
+    unfold_rows(slab_in, rows_ref)
+    loads[0].wait()
+    mixed = mix(weight_ref[...], rows_ref)
+    loads[1].wait()
+    loads[2].wait()
     stream = (stream_ref[...].astype(jnp.float32) + mixed).astype(jnp.bfloat16)
     out_ref[...] = stream
     normed = normalise(stream.astype(jnp.float32), gain_ref[layer + 1 : layer + 2, :])
+    loads[3].wait()
     send_rows(spread_ref, normed, slab_ref)
 
 
 def last_kernel(slab_in, stream_ref, weight_ref, out_ref, rows_ref):
-    mixed = mix(weight_ref[...], slab_in, rows_ref)
+    unfold_rows(slab_in, rows_ref)
+    mixed = mix(weight_ref[...], rows_ref)
     out_ref[...] = (stream_ref[...].astype(jnp.float32) + mixed).astype(jnp.bfloat16)
 
 
@@ -208,40 +227,116 @@
     return jnp.concatenate(lines, axis=0)
 
 
-def expert_kernel(
-    layer, in_scale, out_scale, slab_in, w_in, w_out, routes_ref, gates_ref, place_ref,
-    slab_ref, weight_ref, *rest,
-):
-    def into(first, count):
-        return block_weight(w_in, lambda i, j: in_scale[layer, j, 0, i], layer, first, count)
-
-    def out_of(first, count):
-        return block_weight(w_out, lambda i, j: out_scale[layer, i, 0, j], layer, first, count)
-
-    x_ref, hid, stack_ref = rest[-3:]
+def expert_steps(slab_in, x_ref, hid, stack_ref, in_chunk, out_chunk):
     unfold_rows(slab_in, x_ref)
-    _, weight = slot_tables(routes_ref[layer], place_ref[layer : layer + 1, :], gates_ref[layer])
-    weight_ref[...] = split_weight(weight)
-    if len(rest) > 3:
-        spread_ref, wide_ref = rest[:2]
-        select, _ = slot_tables(
-            routes_ref[layer + 1], place_ref[layer + 1 : layer + 2, :], None
-        )
-        build_spread(select, wide_ref, spread_ref)
-    ff = w_out.shape[2]
-    chunk = slab_ref.shape[1]
-    for n in range(ff // chunk):
-        gate = jnp.dot(x_ref[...], into(n * chunk, chunk), preferred_element_type=jnp.float32)
-        up = jnp.dot(x_ref[...], into(ff + n * chunk, chunk), preferred_element_type=jnp.float32)
+    chunk = slab_in.shape[1]
+    chunks = hid.shape[1] // chunk
+    for n in range(chunks):
+        gate = jnp.dot(x_ref[...], in_chunk(n), preferred_element_type=jnp.float32)
+        up = jnp.dot(x_ref[...], in_chunk(chunks + n), preferred_element_type=jnp.float32)
         hid[:, n * chunk : (n + 1) * chunk] = (gate / (1.0 + jnp.exp(-gate)) * up).astype(
             jnp.bfloat16
         )
     for m in range(PIECES):
-        answer = jnp.dot(
-            hid[...], out_of(m * chunk, chunk), preferred_element_type=jnp.float32
+        answer = jnp.dot(hid[...], out_chunk(m), preferred_element_type=jnp.float32).astype(
+            jnp.bfloat16
+        )
+        stack_piece(stack_ref, answer, m)
+
+
+def first_expert_kernel(
+    layer, in_scale, out_scale, slab_in, w_in, w_out, slab_hbm,
+    x_ref, hid, stack_ref, slab_ref, sems,
+):
+    chunk = slab_in.shape[1]
+    expert_steps(
+        slab_in, x_ref, hid, stack_ref,
+        lambda n: block_weight(
+            w_in, lambda i, j: in_scale[layer, j, 0, i], layer, n * chunk, chunk
+        ),
+        lambda m: block_weight(
+            w_out, lambda i, j: out_scale[layer, i, 0, j], layer, m * chunk, chunk
+        ),
+    )
+    span = GROUP * PIECES
+    fold = fold_matrix()
+    stores = []
+    blocks = slab_ref.shape[0] // span
+    for b in range(blocks):
+        at = slice(b * span, (b + 1) * span)
+        slab_ref[at, :] = jnp.dot(
+            fold, stack_ref[at, :], preferred_element_type=jnp.float32
         ).astype(jnp.bfloat16)
-        stack_piece(stack_ref, answer, m)
+        if b % 3 == 2:
+            rows = pl.ds((b - 2) * span, 3 * span)
+            store = pltpu.make_async_copy(
+                slab_ref.at[rows, :], slab_hbm.at[rows, :], sems.at[b // 3]
+            )
+            store.start()
+            stores.append(store)
+    for store in stores:
+        store.wait()
+
+
+def expert_kernel(slab_in, win, wout, slab_ref, x_ref, hid, stack_ref):
+    expert_steps(
+        slab_in, x_ref, hid, stack_ref, lambda c: win[c], lambda c: wout[c]
+    )
     fold_rows(stack_ref, slab_ref)
+
+
+def prepare_kernel(
+    layer, in_scale, out_scale, w_in, w_out, routes_ref, gates_ref, place_ref, after,
+    win_hbm, wout_hbm, weight_ref, spread_hbm, next_ref,
+    win, wout, wide_ref, spread_ref, load_sems, in_sems, out_sems, spread_sem,
+):
+    del after
+    rows = 2 * QBLK
+    chunk = win_hbm.shape[2]
+    loads = []
+    for src, buf, dst, sems, inner in (
+        (w_in, win, win_hbm, in_sems, True),
+        (w_out, wout, wout_hbm, out_sems, False),
+    ):
+        for r in range(buf.shape[0] // rows):
+            span = pl.ds(r * rows, rows)
+            load = pltpu.make_async_copy(
+                src.at[layer, 0, span, :], buf.at[span, :], load_sems.at[len(loads)]
+            )
+            load.start()
+            loads.append((load, buf, dst, sems, inner, r))
+    select, weight = slot_tables(
+        routes_ref[layer], place_ref[layer : layer + 1, :], gates_ref[layer]
+    )
+    next_ref[...] = split_weight(weight)
+    _, weight = slot_tables(
+        routes_ref[layer - 1], place_ref[layer - 1 : layer, :], gates_ref[layer - 1]
+    )
+    weight_ref[...] = split_weight(weight)
+    build_spread(select, wide_ref, spread_ref)
+    stores = [pltpu.make_async_copy(spread_ref, spread_hbm, spread_sem)]
+    stores[0].start()
+    for load, buf, dst, sems, inner, r in loads:
+        load.wait()
+        for i in range(rows // QBLK):
+            for j in range(buf.shape[1] // QBLK):
+                at = (
+                    slice(r * rows + i * QBLK, r * rows + (i + 1) * QBLK),
+                    slice(j * QBLK, (j + 1) * QBLK),
+                )
+                block = r * (rows // QBLK) + i
+                factor = in_scale[layer, j, 0, block] if inner else out_scale[layer, block, 0, j]
+                buf[at] = (buf[at].astype(jnp.float32) * factor).astype(jnp.bfloat16)
+        for c in range(dst.shape[0]):
+            store = pltpu.make_async_copy(
+                buf.at[pl.ds(r * rows, rows), pl.ds(c * chunk, chunk)],
+                dst.at[c, pl.ds(r * rows, rows), :],
+                sems.at[r, c],
+            )
+            store.start()
+            stores.append(store)
+    for store in stores:
+        store.wait()
 
 
 VM = pl.BlockSpec(memory_space=pltpu.VMEM)
@@ -249,38 +344,90 @@
 HB = pl.BlockSpec(memory_space=pltpu.HBM)
 
 
-def expert(layer, layers, slab, weights, tables):
+def expert_cost(slots, width, ff):
+    return pl.CostEstimate(
+        flops=6 * slots * width * ff,
+        bytes_accessed=6 * width * ff + 4 * slots * width,
+        transcendentals=slots * ff,
+    )
+
+
+def first_expert(slab, weights):
     w_in, in_scale, w_out, out_scale = weights
     rows, piece = slab.shape
     slots = rows // PIECES
     width, ff = w_in.shape[2], w_out.shape[2]
+    return pl.pallas_call(
+        functools.partial(first_expert_kernel, 0),
+        in_specs=[SM, SM, VM, VM, VM],
+        out_specs=HB,
+        out_shape=pltpu.HBM(slab.shape, jnp.bfloat16),
+        scratch_shapes=[
+            pltpu.VMEM((slots, width), jnp.bfloat16),
+            pltpu.VMEM((slots, ff), jnp.bfloat16),
+            pltpu.VMEM(slab.shape, jnp.bfloat16),
+            pltpu.VMEM(slab.shape, jnp.bfloat16),
+            pltpu.SemaphoreType.DMA((rows // (3 * GROUP * PIECES),)),
+        ],
+        compiler_params=pltpu.CompilerParams(vmem_limit_bytes=20 * MIB),
+        cost_estimate=expert_cost(slots, width, ff),
+        name="first_expert",
+    )(in_scale, out_scale, slab, w_in, w_out)
+
+
+def expert(slab, win, wout):
+    rows, piece = slab.shape
+    slots = rows // PIECES
+    width, ff = win.shape[1], wout.shape[1]
+    return pl.pallas_call(
+        expert_kernel,
+        in_specs=[VM] * 3,
+        out_specs=VM,
+        out_shape=jax.ShapeDtypeStruct(slab.shape, jnp.bfloat16),
+        scratch_shapes=[
+            pltpu.VMEM((slots, width), jnp.bfloat16),
+            pltpu.VMEM((slots, ff), jnp.bfloat16),
+            pltpu.VMEM(slab.shape, jnp.bfloat16),
+        ],
+        compiler_params=pltpu.CompilerParams(vmem_limit_bytes=20 * MIB),
+        cost_estimate=expert_cost(slots, width, ff),
+        name="expert",
+    )(slab, win, wout)
+
+
+def prepare(layer, weights, tables, slots, chunk, after):
+    w_in, in_scale, w_out, out_scale = weights
     tokens = tables[0].shape[2]
-    outs = [
-        jax.ShapeDtypeStruct(slab.shape, jnp.bfloat16),
-        jax.ShapeDtypeStruct((2 * tokens, slots), jnp.bfloat16),
-    ]
-    scratch = [
-        pltpu.VMEM((slots, width), jnp.bfloat16),
-        pltpu.VMEM((slots, ff), jnp.bfloat16),
-        pltpu.VMEM(slab.shape, jnp.bfloat16),
-    ]
-    if layer + 1 < layers:
-        outs.append(jax.ShapeDtypeStruct((rows, tokens * PIECES), jnp.bfloat16))
-        scratch.insert(0, pltpu.VMEM((slots, tokens * PIECES), jnp.float32))
+    width, gated = w_in.shape[2:]
+    ff = w_out.shape[2]
+    rows = 2 * QBLK
+    size = width * gated + ff * width
+    spread = (slots * PIECES, tokens * PIECES)
     return pl.pallas_call(
-        functools.partial(expert_kernel, layer),
-        in_specs=[SM, SM] + [VM] * 6,
-        out_specs=[VM] * len(outs),
-        out_shape=outs,
-        scratch_shapes=scratch,
-        compiler_params=pltpu.CompilerParams(vmem_limit_bytes=20 * MIB),
-        cost_estimate=pl.CostEstimate(
-            flops=6 * slots * width * ff,
-            bytes_accessed=6 * width * ff + 4 * slots * width,
-            transcendentals=slots * ff,
-        ),
-        name="expert",
-    )(in_scale, out_scale, slab, w_in, w_out, *tables)
+        functools.partial(prepare_kernel, layer),
+        in_specs=[SM, SM, HB, HB, VM, VM, VM, HB],
+        out_specs=[HB, HB, VM, HB, VM],
+        out_shape=[
+            pltpu.HBM((gated // chunk, width, chunk), jnp.bfloat16),
+            pltpu.HBM((width // chunk, ff, chunk), jnp.bfloat16),
+            jax.ShapeDtypeStruct((2 * tokens, slots), jnp.bfloat16),
+            pltpu.HBM(spread, jnp.bfloat16),
+            jax.ShapeDtypeStruct((2 * tokens, slots), jnp.bfloat16),
+        ],
+        scratch_shapes=[
+            pltpu.VMEM((width, gated), jnp.bfloat16),
+            pltpu.VMEM((ff, width), jnp.bfloat16),
+            pltpu.VMEM((slots, tokens * PIECES), jnp.float32),
+            pltpu.VMEM(spread, jnp.bfloat16),
+            pltpu.SemaphoreType.DMA(((width + ff) // rows,)),
+            pltpu.SemaphoreType.DMA((width // rows, gated // chunk)),
+            pltpu.SemaphoreType.DMA((ff // rows, width // chunk)),
+            pltpu.SemaphoreType.DMA,
+        ],
+        compiler_params=pltpu.CompilerParams(vmem_limit_bytes=24 * MIB),
+        cost_estimate=pl.CostEstimate(flops=size, bytes_accessed=4 * size, transcendentals=0),
+        name="prepare",
+    )(in_scale, out_scale, hbm(w_in), hbm(w_out), *tables, after)
 
 
 def hbm(array):
@@ -304,7 +451,7 @@
     stream_type = jax.ShapeDtypeStruct((count, width), jnp.bfloat16)
     rows = pltpu.VMEM((slots, width), jnp.bfloat16)
     wide = pltpu.VMEM((slots, count * PIECES), jnp.float32)
-    spread = pltpu.VMEM((slots * PIECES, count * PIECES), jnp.bfloat16)
+    scatter = pltpu.VMEM((slots * PIECES, count * PIECES), jnp.bfloat16)
     params = pltpu.CompilerParams(vmem_limit_bytes=12 * MIB)
 
     small = (
@@ -318,7 +465,7 @@
         in_specs=[HB] * 4,
         out_specs=VM,
         out_shape=slab_type,
-        scratch_shapes=[*small, wide, spread, pltpu.SemaphoreType.DMA((4,))],
+        scratch_shapes=[*small, wide, scatter, pltpu.SemaphoreType.DMA((4,))],
         compiler_params=params,
         cost_estimate=pl.CostEstimate(
             flops=8 * 10**9, bytes_accessed=8 * 10**6, transcendentals=0
@@ -332,21 +479,35 @@
         jnp.transpose(out_scale, (0, 2, 1, 3)),
     )
     stream = tokens
+    tables = (routes_t, gates_t, placement)
     for layer in range(layers):
-        answers, weight, *spreads = expert(
-            layer, layers, exchange(slab, devices), weights, (routes_t, gates_t, placement)
-        )
+        arrived = exchange(slab, devices)
+        answers = first_expert(arrived, weights) if layer == 0 else expert(arrived, win, wout)
+        if layer + 1 < layers:
+            win, wout, weight, spread, next_weight = prepare(
+                layer + 1, weights, tables, slots, piece, answers
+            )
         back = exchange(answers, devices)
         if layer + 1 < layers:
             slab, stream = pl.pallas_call(
                 functools.partial(middle_kernel, layer),
-                in_specs=[VM] * 5,
+                in_specs=[VM] + [HB] * 4,
                 out_specs=(VM, VM),
                 out_shape=(slab_type, stream_type),
-                scratch_shapes=[rows],
+                scratch_shapes=[
+                    rows,
+                    pltpu.VMEM((count, width), jnp.bfloat16),
+                    pltpu.VMEM(norm_gain.shape, jnp.float32),
+                    pltpu.VMEM(weight.shape, jnp.bfloat16),
+                    pltpu.VMEM(spread.shape, jnp.bfloat16),
+                    pltpu.SemaphoreType.DMA((4,)),
+                ],
                 compiler_params=params,
+                cost_estimate=pl.CostEstimate(
+                    flops=8 * 10**9, bytes_accessed=8 * 10**6, transcendentals=0
+                ),
                 name="middle",
-            )(back, stream, norm_gain, weight, spreads[0])
+            )(back, hbm(stream), hbm(norm_gain), hbm(weight), hbm(spread))
         else:
             stream = pl.pallas_call(
                 last_kernel,
@@ -356,7 +517,7 @@
                 scratch_shapes=[rows],
                 compiler_params=params,
                 name="last",
-            )(back, stream, weight)
+            )(back, stream, next_weight)
     return stream
 
 

time: 139 us -> 140 us (level)
  blocking collectives: 121 us -> 92.6 us
  waiting for transfers between devices: 0 us -> 13.6 us
  Pallas kernels: 18 us -> 27.8 us
  starting transfers between devices: 0 us -> 4.94 us
    all_to_all x4 -> x3, blocking collectives: 121 us -> 92.6 us  [exchange(): moved = lax.all_to_all(split, AXES, split_axis=0, concat_axis=0, tiled=True)]
    all_to_all x0 -> x1, waiting for transfers between devices: none -> 13.6 us  [exchange(): moved = lax.all_to_all(split, AXES, split_axis=0, concat_axis=0, tiled=True)]
    pallas_call x3 -> x4, Pallas kernels: 14.1 us -> 23.9 us  [the longest x1 9.97 us: prepare(): pl.pallas_call(functools.partial(prepare_kernel, layer), in_specs=[SM, SM...]
    all_to_all x0 -> x1, starting transfers between devices: none -> 4.94 us  [exchange(): moved = lax.all_to_all(split, AXES, split_axis=0, concat_axis=0, tiled=True)]
  transfers between devices with their start and end apart: 0 -> 1, of which waited for: 0 -> 1; matrix products, arithmetic and copies ran while one was open for 0% -> 0% of each run, Pallas kernels for 0% -> 7%
where the time goes in v5:
time: 140 us
  blocking collectives  92.6 us (66%)
  Pallas kernels  27.8 us (20%)
  waiting for transfers between devices  13.6 us (10%)
  starting transfers between devices  4.94 us (4%)
    all_to_all x3, blocking collectives, exchange(): moved = lax.all_to_all(split, AXES, split_axis=0, concat_axis=0, tiled=True)  92.6 us
    all_to_all x1, waiting for transfers between devices, exchange(): moved = lax.all_to_all(split, AXES, split_axis=0, concat_axis=0, tiled=True)  13.6 us
    pallas_call x1, Pallas kernels, prepare(): pl.pallas_call(functools.partial(prepare_kernel, layer), in_specs=[SM, SM...  9.97 us
    pallas_call x1, Pallas kernels, first_expert(): pl.pallas_call(functools.partial(first_expert_kernel, 0), in_specs=[SM, S...  6.58 us
    all_to_all x1, starting transfers between devices, exchange(): moved = lax.all_to_all(split, AXES, split_axis=0, concat_axis=0, tiled=True)  4.94 us
    pallas_call x1, Pallas kernels, expert(): pl.pallas_call(expert_kernel, in_specs=[VM] * 3, out_specs=VM, out_shape=...  4.7 us
  transfers between devices with their start and end apart: 1, of which 1 were waited for; matrix products, arithmetic and copies ran while one was open for 0% of the time, Pallas kernels for 7%

profile of v5, /device:TPU:1, one launch (start us, length us, event | category | flops | bytes accessed | tf_op | source)
XLA Modules:
  0.0 139.9 jit_solution(1085755065660370240)
XLA Ops:
  0.0 0.0 slice-start.2
  0.0 0.0 slice-start.4
  0.0 2.4 %first.1 = bf16[3072,256]{1,0:T(8,128)(2,1)S(1)} custom-call(bf16[32,2048]{1,0:T(8,128)(2,1)} %stream_hbm.1, f32[2,2048]{1,0:T(2,128)} %gain_hbm.3, s32[2,8,32]{2,1,0:T(8,128)} %bitcast.28, s32[2,128]{1,0:T(2,128)} %place_ref.1), custom_call_target="tpu_custom_call" | custom-call | flops 8000000000 | bytes 8000000 | tf_op jit(solution)/shard_map/first/pallas_call | solution.py:463
  2.4 0.0 copy-start.1
  2.4 0.0 copy-start.2
  2.4 35.4 %all_to_all.20 = bf16[128,24,256]{2,1,0:T(8,128)(2,1)S(1)} all-to-all(bf16[128,24,256]{2,1,0:T(8,128)(2,1)S(1)} %bitcast.23), channel_id=1, replica_groups=mesh['dp'=8,'expert'=16] {'dp','expert'}, dimensions={0} | all-to-all | bytes 3145728 | tf_op jit(solution)/shard_map/all_to_all | solution.py:439
  37.9 0.0 slice-done
  37.9 0.0 slice-done.1
  37.9 6.6 %first_expert.1.after = bf16[3072,256]{1,0:T(8,128)(2,1)} custom-call(f32[2,12,1,16]{3,2,1,0:T(1,128)S(1)} %bitcast.24, f32[2,6,1,16]{3,2,1,0:T(1,128)S(1)} %bitcast.26, bf16[3072,256]{1,0:T(8,128)(2,1)S(1)} %bitcast.18, bf16[2,1,2048,1536]{3,2,1,0:T(8,128)(2,1)S(1)} %bitcast.13, bf16[2,1,768,2048]{3,2,1,0:T(8,128)(2,1)S(1)} %bitcast.15), custom_call_target="tpu_custom_call" | custom-call | flops 3623878656 | bytes 12582912 | tf_op jit(solution)/shard_map/first_expert/pallas_call | solution.py:360
  44.5 0.0 copy-start
  44.5 0.0 copy-start.3
  44.5 0.0 copy-start.4
  44.6 0.0 copy-start.5
  44.6 4.9 %all-to-all-start.1 = ((bf16[128,24,256]{2,1,0:T(8,128)(2,1)}), bf16[128,24,256]{2,1,0:T(8,128)(2,1)S(1)}, u32[]{:S(2)}, u32[]{:S(2)}) async-start(bf16[128,24,256]{2,1,0:T(8,128)(2,1)} %bitcast.16), calls=%async_computation.1 | async-start | bytes 3145728 | tf_op jit(solution)/shard_map/all_to_all | solution.py:439
  49.6 10.0 %prepare.1 = (bf16[6,2048,256]{2,1,0:T(8,128)(2,1)}, bf16[8,768,256]{2,1,0:T(8,128)(2,1)}, bf16[64,384]{1,0:T(8,128)(2,1)S(1)}, bf16[3072,256]{1,0:T(8,128)(2,1)}, bf16[64,384]{1,0:T(8,128)(2,1)S(1)}) custom-call(f32[2,12,1,16]{3,2,1,0:T(1,128)S(1)} %bitcast.25, f32[2,6,1,16]{3,2,1,0:T(1,128)S(1)} %bitcast.27, bf16[2,1,2048,1536]{3,2,1,0:T(8,128)(2,1)} %w_in.3, ...), custom_call_target="tpu_custom_call" | custom-call | flops 4718592 | bytes 18874368 | tf_op jit(solution)/shard_map/prepare/pallas_call | solution.py:406
  59.5 0.0 copy-start.8
  59.6 0.6 copy-done.8
  60.2 13.6 %all-to-all-done.1 = bf16[128,24,256]{2,1,0:T(8,128)(2,1)S(1)} async-done(((bf16[128,24,256]{2,1,0:T(8,128)(2,1)}), bf16[128,24,256]{2,1,0:T(8,128)(2,1)S(1)}, u32[]{:S(2)}, u32[]{:S(2)}) %all-to-all-start.1) | async-done | bytes 1572896 | tf_op jit(solution)/shard_map/all_to_all | solution.py:439
  73.8 2.6 %middle.1 = (bf16[3072,256]{1,0:T(8,128)(2,1)S(1)}, bf16[32,2048]{1,0:T(8,128)(2,1)S(1)}) custom-call(bf16[3072,256]{1,0:T(8,128)(2,1)S(1)} %bitcast.19, bf16[32,2048]{1,0:T(8,128)(2,1)} %stream_hbm.1, f32[2,2048]{1,0:T(2,128)} %gain_hbm.3, bf16[64,384]{1,0:T(8,128)(2,1)} %copy-done.8, bf16[3072,256]{1,0:T(8,128)(2,1)} %get-tuple-element.13.spread_hbm), custom_call_target="tpu_custom_call" | custom-call | flops 8000000000 | bytes 8000000 | tf_op jit(solution)/shard_map/middle/pallas_call | solution.py:492
  76.5 28.7 %all_to_all.21 = bf16[128,24,256]{2,1,0:T(8,128)(2,1)S(1)} all-to-all(bf16[128,24,256]{2,1,0:T(8,128)(2,1)S(1)} %bitcast.20), channel_id=1, replica_groups=mesh['dp'=8,'expert'=16] {'dp','expert'}, dimensions={0} | all-to-all | bytes 3145728 | tf_op jit(solution)/shard_map/all_to_all | solution.py:439
  105.2 0.0 copy-done.6
  105.2 4.7 %expert.1 = bf16[3072,256]{1,0:T(8,128)(2,1)S(1)} custom-call(bf16[3072,256]{1,0:T(8,128)(2,1)S(1)} %bitcast.21, bf16[6,2048,256]{2,1,0:T(8,128)(2,1)S(1)} %copy-done.6, bf16[8,768,256]{2,1,0:T(8,128)(2,1)S(1)} %copy-done.7), custom_call_target="tpu_custom_call" | custom-call | flops 3623878656 | bytes 12582912 | tf_op jit(solution)/shard_map/expert/pallas_call | solution.py:382
  109.9 28.5 %all_to_all.22 = bf16[128,24,256]{2,1,0:T(8,128)(2,1)S(1)} all-to-all(bf16[128,24,256]{2,1,0:T(8,128)(2,1)S(1)} %bitcast.22), channel_id=1, replica_groups=mesh['dp'=8,'expert'=16] {'dp','expert'}, dimensions={0} | all-to-all | bytes 3145728 | tf_op jit(solution)/shard_map/all_to_all | solution.py:439
  138.3 1.5 %last.1 = bf16[32,2048]{1,0:T(8,128)(2,1)} custom-call(bf16[3072,256]{1,0:T(8,128)(2,1)S(1)} %bitcast.17, bf16[32,2048]{1,0:T(8,128)(2,1)S(1)} %get-tuple-element.17.stream_ref, bf16[64,384]{1,0:T(8,128)(2,1)S(1)} %get-tuple-element.18.weight_ref), custom_call_target="tpu_custom_call" | custom-call | tf_op jit(solution)/shard_map/last/pallas_call | solution.py:512
  (17 shorter events, 0.0 us)
Async XLA Ops:
  0.0 37.9 %slice-start = ((s8[12582912]{0:T(1024)(128)(4,1)}), s8[4194304]{0:T(1024)(128)(4,1)S(1)}, s32[]{:S(2)}) async-start(s8[12582912]{0:T(1024)(128)(4,1)} %bitcast.12), calls=%async_computation.4 | async-start | bytes 8388608
  0.0 37.9 %slice-start.3 = ((s8[6291456]{0:T(1024)(128)(4,1)}), s8[4194304]{0:T(1024)(128)(4,1)S(1)}, s32[]{:S(2)}) async-start(s8[6291456]{0:T(1024)(128)(4,1)} %bitcast.14), calls=%async_computation.7 | async-start | bytes 8388608
  0.0 37.9 %slice-start.1 = ((s8[12582912]{0:T(1024)(128)(4,1)}), s8[4194304]{0:T(1024)(128)(4,1)S(1)}, s32[]{:S(2)}) async-start(s8[12582912]{0:T(1024)(128)(4,1)} %bitcast.12), calls=%async_computation.5 | async-start | bytes 8388608
  0.0 37.9 %slice-start.2 = ((s8[12582912]{0:T(1024)(128)(4,1)}), s8[4194304]{0:T(1024)(128)(4,1)S(1)}, s32[]{:S(2)}) async-start(s8[12582912]{0:T(1024)(128)(4,1)} %bitcast.12), calls=%async_computation.6 | async-start | bytes 8388608
  0.0 37.9 %slice-start.4 = ((s8[6291456]{0:T(1024)(128)(4,1)}), s8[2097152]{0:T(1024)(128)(4,1)S(1)}, s32[]{:S(2)}) async-start(s8[6291456]{0:T(1024)(128)(4,1)} %bitcast.14), calls=%async_computation.8 | async-start | bytes 4194304
  2.4 35.5 %copy-start.1 = (f32[2,1,16,12]{2,1,3,0:T(1,128)S(1)}, f32[2,1,16,12]{2,1,3,0:T(1,128)}, u32[]{:S(2)}) copy-start(f32[2,1,16,12]{2,1,3,0:T(1,128)} %param.15) | copy-start | bytes 4612
  2.4 35.5 %copy-start.2 = (f32[2,1,6,16]{3,1,2,0:T(1,128)S(1)}, f32[2,1,6,16]{3,1,2,0:T(1,128)}, u32[]{:S(2)}) copy-start(f32[2,1,6,16]{3,1,2,0:T(1,128)} %param.17) | copy-start | bytes 2308
  44.5 5.0 %copy-start = (bf16[3072,256]{1,0:T(8,128)(2,1)S(1)}, bf16[3072,256]{1,0:T(8,128)(2,1)}, u32[]{:S(2)}) copy-start(bf16[3072,256]{1,0:T(8,128)(2,1)} %first_expert.1.after) | copy-start | bytes 4718596
  44.5 5.0 %copy-start.3 = (s32[2,32,8]{1,2,0:T(8,128)S(1)}, s32[2,32,8]{1,2,0:T(8,128)}, u32[]{:S(2)}) copy-start(s32[2,32,8]{1,2,0:T(8,128)} %param.11) | copy-start | bytes 6148
  44.5 5.0 %copy-start.4 = (f32[2,32,8]{1,2,0:T(8,128)S(1)}, f32[2,32,8]{1,2,0:T(8,128)}, u32[]{:S(2)}) copy-start(f32[2,32,8]{1,2,0:T(8,128)} %param.12) | copy-start | bytes 6148
  44.6 5.0 %copy-start.5 = (s32[2,128]{1,0:T(2,128)S(1)}, s32[2,128]{1,0:T(2,128)}, u32[]{:S(2)}) copy-start(s32[2,128]{1,0:T(2,128)} %place_ref.1) | copy-start | bytes 3076
  44.6 29.2 %all-to-all-start.1 = ((bf16[128,24,256]{2,1,0:T(8,128)(2,1)}), bf16[128,24,256]{2,1,0:T(8,128)(2,1)S(1)}, u32[]{:S(2)}, u32[]{:S(2)}) async-start(bf16[128,24,256]{2,1,0:T(8,128)(2,1)} %bitcast.16), calls=%async_computation.1 | async-start | bytes 3145728 | tf_op jit(solution)/shard_map/all_to_all | solution.py:439
  59.5 0.6 copy-start.8
  73.8 31.4 %copy-start.6 = (bf16[6,2048,256]{2,1,0:T(8,128)(2,1)S(1)}, bf16[6,2048,256]{2,1,0:T(8,128)(2,1)}, u32[]{:S(2)}) copy-start(bf16[6,2048,256]{2,1,0:T(8,128)(2,1)} %get-tuple-element.15.win) | copy-start | bytes 18874372
  76.5 28.7 %copy-start.7 = (bf16[8,768,256]{2,1,0:T(8,128)(2,1)S(1)}, bf16[8,768,256]{2,1,0:T(8,128)(2,1)}, u32[]{:S(2)}) copy-start(bf16[8,768,256]{2,1,0:T(8,128)(2,1)} %get-tuple-element.16.wout) | copy-start | bytes 9437188

commit v6 on v3

--- a/solution.py
+++ b/solution.py
@@ -112,19 +112,40 @@
     fold_rows(stack_ref, slab_ref)
 
 
-def mix(weight, slab_ref, rows_ref):
-    unfold_rows(slab_ref, rows_ref)
-    high = weight.astype(jnp.bfloat16)
-    low = (weight - high.astype(jnp.float32)).astype(jnp.bfloat16)
-    both = jnp.dot(
-        jnp.concatenate([high, low], axis=0), rows_ref[...], preferred_element_type=jnp.float32
-    )
-    tokens = weight.shape[0]
-    return both[:tokens] + both[tokens:]
+def slot_numbers(routes_t, place_row):
+    choices, tokens = routes_t.shape
+    devices = place_row.shape[1]
+    place = place_row.astype(jnp.float32)
+    chosen = jnp.transpose(routes_t.astype(jnp.float32))
+    same = [chosen[:, k : k + 1] == place for k in range(choices)]
+    taken = jnp.zeros((tokens, devices), jnp.float32)
+    for k in range(choices):
+        taken = jnp.where(same[k], 1.0, taken)
+    later = lax.broadcasted_iota(jnp.int32, (tokens, tokens), 0)
+    earlier = lax.broadcasted_iota(jnp.int32, (tokens, tokens), 1)
+    before = jnp.where(earlier < later, 1.0, 0.0).astype(jnp.bfloat16)
+    ranks = jnp.dot(before, taken.astype(jnp.bfloat16), preferred_element_type=jnp.float32)
+    home = lax.broadcasted_iota(jnp.int32, (tokens, devices), 1).astype(jnp.float32)
+    number = home * CAP + ranks
+    column = lax.broadcasted_iota(jnp.int32, (tokens, choices), 1)
+    slots = jnp.zeros((tokens, choices), jnp.float32)
+    for k in range(choices):
+        found = jnp.sum(jnp.where(same[k], number, 0.0), axis=1, keepdims=True)
+        slots = jnp.where(column == k, found, slots)
+    return jnp.transpose(slots).astype(jnp.int32)
+
+
+def mix_blocks(layer, slots_ref, gates_ref, back_ref, mixed_ref):
+    for t in range(mixed_ref.shape[0]):
+        total = None
+        for k in range(gates_ref.shape[1]):
+            block = back_ref[slots_ref[layer, k, t]].astype(jnp.float32) * gates_ref[layer, k, t]
+            total = block if total is None else total + block
+        mixed_ref[t] = total
 
 
 def first_kernel(
-    tokens_hbm, gain_hbm, routes_hbm, place_hbm, slab_ref,
+    tokens_hbm, gain_hbm, routes_hbm, place_hbm, slab_ref, slots_ref,
     tokens_ref, gain_ref, routes_ref, place_ref, stack_ref, sems,
 ):
     loads = [
@@ -148,28 +169,57 @@
     loads[3].wait()
     normed = normalise(tokens_ref[...].astype(jnp.float32), gain_ref[0:1, :])
     send_rows(pick, normed, stack_ref, slab_ref)
+    for layer in range(routes_ref.shape[0]):
+        slots_ref[layer] = slot_numbers(routes_ref[layer], place_ref[layer : layer + 1, :])
+
+
+def blocks_of(stream_ref, stack_ref):
+    piece = stack_ref.shape[1]
+    for p in range(PIECES):
+        stack_ref[p * GROUP : (p + 1) * GROUP, :] = stream_ref[:, p * piece : (p + 1) * piece]
+    return jnp.dot(fold_matrix(), stack_ref[...], preferred_element_type=jnp.float32)
 
 
 def middle_kernel(
-    layer, slab_in, stream_ref, gain_ref, routes_ref, gates_ref, place_ref,
-    slab_ref, out_ref, rows_ref, stack_ref,
+    layer, first, slots_ref, gates_ref, back_ref, stream_ref, gain_ref,
+    slab_ref, out_ref, mixed_ref, gain_rows, stack_ref,
 ):
-    _, weight = slot_tables(routes_ref[layer], place_ref[layer : layer + 1, :], gates_ref[layer])
-    select, _ = slot_tables(routes_ref[layer + 1], place_ref[layer + 1 : layer + 2, :], None)
-    pick = jnp.transpose(select).astype(jnp.bfloat16)
-    mixed = mix(weight, slab_in, rows_ref)
-    stream = (stream_ref[...].astype(jnp.float32) + mixed).astype(jnp.bfloat16)
+    slab_ref[...] = jnp.zeros(slab_ref.shape, jnp.bfloat16)
+    tokens, pieces, piece = mixed_ref.shape
+    if first:
+        blocks = blocks_of(stream_ref, stack_ref)
+    else:
+        blocks = stream_ref[...].astype(jnp.float32)
+    for p in range(pieces):
+        gain_rows[p : p + 1, :] = gain_ref[
+            layer + 1 : layer + 2, p * piece : (p + 1) * piece
+        ]
+    mix_blocks(layer, slots_ref, gates_ref, back_ref, mixed_ref)
+    stream = (blocks + mixed_ref[...].reshape(tokens * pieces, piece)).astype(jnp.bfloat16)
     out_ref[...] = stream
-    normed = normalise(stream.astype(jnp.float32), gain_ref[layer + 1 : layer + 2, :])
-    send_rows(pick, normed, stack_ref, slab_ref)
+    wide = stream.astype(jnp.float32).reshape(tokens, pieces, piece)
+    total = jnp.sum(jnp.sum(wide * wide, axis=2, keepdims=True), axis=1, keepdims=True)
+    scale = lax.rsqrt(total / (pieces * piece) + EPS)
+    mixed_ref[...] = wide * scale * gain_rows[...][None]
+    for t in range(tokens):
+        row = mixed_ref[t].astype(jnp.bfloat16)
+        for k in range(slots_ref.shape[1]):
+            slab_ref[slots_ref[layer + 1, k, t]] = row
 
 
 def last_kernel(
-    layer, slab_in, stream_ref, routes_ref, gates_ref, place_ref, out_ref, rows_ref
+    layer, slots_ref, gates_ref, back_ref, stream_ref, out_ref, mixed_ref
 ):
-    _, weight = slot_tables(routes_ref[layer], place_ref[layer : layer + 1, :], gates_ref[layer])
-    mixed = mix(weight, slab_in, rows_ref)
-    out_ref[...] = (stream_ref[...].astype(jnp.float32) + mixed).astype(jnp.bfloat16)
+    tokens, pieces, piece = mixed_ref.shape
+    mix_blocks(layer, slots_ref, gates_ref, back_ref, mixed_ref)
+    stream = (
+        stream_ref[...].astype(jnp.float32) + mixed_ref[...].reshape(tokens * pieces, piece)
+    ).astype(jnp.bfloat16)
+    rows = jnp.dot(unfold_matrix(), stream, preferred_element_type=jnp.float32).astype(
+        jnp.bfloat16
+    )
+    for p in range(pieces):
+        out_ref[:, p * piece : (p + 1) * piece] = rows[p * tokens : (p + 1) * tokens]
 
 
 def block_weight(w_ref, factor, layer, first, count):
@@ -262,8 +312,9 @@
     routes_t = jnp.swapaxes(routes, 1, 2)
     gates_t = jnp.swapaxes(gates, 1, 2)
     slab_type = jax.ShapeDtypeStruct((slots * PIECES, piece), jnp.bfloat16)
+    slots_type = jax.ShapeDtypeStruct(routes_t.shape, jnp.int32)
     stream_type = jax.ShapeDtypeStruct((count, width), jnp.bfloat16)
-    rows = pltpu.VMEM((slots, width), jnp.bfloat16)
+    mixed = pltpu.VMEM((count, PIECES, piece), jnp.float32)
     stack = pltpu.VMEM((slots * PIECES, piece), jnp.bfloat16)
     params = pltpu.CompilerParams(vmem_limit_bytes=12 * MIB)
 
@@ -273,11 +324,11 @@
         pltpu.VMEM(routes_t.shape, jnp.int32),
         pltpu.VMEM(placement.shape, jnp.int32),
     )
-    slab = pl.pallas_call(
+    slab, numbers = pl.pallas_call(
         first_kernel,
         in_specs=[HB] * 4,
-        out_specs=VM,
-        out_shape=slab_type,
+        out_specs=(VM, VM),
+        out_shape=(slab_type, slots_type),
         scratch_shapes=[*small, stack, pltpu.SemaphoreType.DMA((4,))],
         compiler_params=params,
         cost_estimate=pl.CostEstimate(
@@ -294,27 +345,35 @@
     stream = tokens
     for layer in range(layers):
         answers = expert(layer, exchange(slab, devices), weights)
-        back = exchange(answers, devices)
+        back = exchange(answers, devices).reshape(slots, PIECES, piece)
         if layer + 1 < layers:
             slab, stream = pl.pallas_call(
-                functools.partial(middle_kernel, layer),
-                in_specs=[VM] * 6,
+                functools.partial(middle_kernel, layer, layer == 0),
+                in_specs=[SM, SM, VM, VM, VM],
                 out_specs=(VM, VM),
-                out_shape=(slab_type, stream_type),
-                scratch_shapes=[rows, stack],
+                out_shape=(
+                    jax.ShapeDtypeStruct(back.shape, jnp.bfloat16),
+                    jax.ShapeDtypeStruct((count * PIECES, piece), jnp.bfloat16),
+                ),
+                scratch_shapes=[
+                    mixed,
+                    pltpu.VMEM((PIECES, piece), jnp.float32),
+                    pltpu.VMEM((count * PIECES, piece), jnp.bfloat16),
+                ],
                 compiler_params=params,
                 name="middle",
-            )(back, stream, norm_gain, routes_t, gates_t, placement)
+            )(numbers, gates_t, back, stream, norm_gain)
+            slab = slab.reshape(slots * PIECES, piece)
         else:
             stream = pl.pallas_call(
                 functools.partial(last_kernel, layer),
-                in_specs=[VM] * 5,
+                in_specs=[SM, SM, VM, VM],
                 out_specs=VM,
                 out_shape=stream_type,
-                scratch_shapes=[rows],
+                scratch_shapes=[mixed],
                 compiler_params=params,
                 name="last",
-            )(back, stream, routes_t, gates_t, placement)
+            )(numbers, gates_t, back, stream)
     return stream
 
 

time: 139 us -> 139 us (level)
  no operation moved by 1% of the time
where the time goes in v6:
time: 139 us
  blocking collectives  121 us (87%)
  Pallas kernels  17.5 us (13%)
    all_to_all x4, blocking collectives, exchange(): moved = lax.all_to_all(split, AXES, split_axis=0, concat_axis=0, tiled=True)  121 us
    pallas_call x2, Pallas kernels, expert(): pl.pallas_call(functools.partial(expert_kernel, layer), in_specs=[SM, SM,...  11.5 us

profile of v6, /device:TPU:1, one launch (start us, length us, event | category | flops | bytes accessed | tf_op | source)
XLA Modules:
  0.0 138.6 jit_solution(8829033986267166447)
XLA Ops:
  0.0 0.0 slice-start.2
  0.0 0.0 slice-start.4
  0.0 2.6 %first.1 = (bf16[3072,256]{1,0:T(8,128)(2,1)S(1)}, s32[2,8,32]{2,1,0:T(8,128)S(1)}) custom-call(bf16[32,2048]{1,0:T(8,128)(2,1)} %stream_ref.1, f32[2,2048]{1,0:T(2,128)} %gain_ref.1, s32[2,8,32]{2,1,0:T(8,128)} %bitcast.30, s32[2,128]{1,0:T(2,128)} %place_hbm.1), custom_call_target="tpu_custom_call" | custom-call | flops 8000000000 | bytes 8000000 | tf_op jit(solution)/shard_map/first/pallas_call | solution.py:327
  2.7 0.0 copy-start.1
  2.7 0.0 copy-start.3
  2.7 35.4 %all_to_all.20 = bf16[128,24,256]{2,1,0:T(8,128)(2,1)S(1)} all-to-all(bf16[128,24,256]{2,1,0:T(8,128)(2,1)S(1)} %bitcast.23), channel_id=1, replica_groups=mesh['dp'=8,'expert'=16] {'dp','expert'}, dimensions={0} | all-to-all | bytes 3145728 | tf_op jit(solution)/shard_map/all_to_all | solution.py:303
  38.1 0.0 slice-done
  38.1 0.0 slice-done.3
  38.2 0.0 slice-done.1
  38.2 0.0 slice-done.2
  38.2 0.0 slice-done.4
  38.2 0.0 copy-done.1
  38.2 0.0 copy-done.3
  38.2 5.8 %expert.2 = bf16[3072,256]{1,0:T(8,128)(2,1)S(1)} custom-call(f32[2,12,1,16]{3,2,1,0:T(1,128)S(1)} %bitcast.24, f32[2,6,1,16]{3,2,1,0:T(1,128)S(1)} %bitcast.28, bf16[3072,256]{1,0:T(8,128)(2,1)S(1)} %bitcast.18, bf16[2,1,2048,1536]{3,2,1,0:T(8,128)(2,1)S(1)} %bitcast.13, bf16[2,1,768,2048]{3,2,1,0:T(8,128)(2,1)S(1)} %bitcast.15), custom_call_target="tpu_custom_call" | custom-call | flops 3623878656 | bytes 12582912 | tf_op jit(solution)/shard_map/expert/pallas_call | solution.py:277
  44.0 0.0 copy-start
  44.0 0.0 copy-start.2
  44.0 0.0 copy-start.4
  44.0 28.6 %all_to_all.21 = bf16[128,24,256]{2,1,0:T(8,128)(2,1)S(1)} all-to-all(bf16[128,24,256]{2,1,0:T(8,128)(2,1)S(1)} %bitcast.19), channel_id=1, replica_groups=mesh['dp'=8,'expert'=16] {'dp','expert'}, dimensions={0} | all-to-all | bytes 3145728 | tf_op jit(solution)/shard_map/all_to_all | solution.py:303
  72.6 0.0 copy-done.2
  72.6 1.5 %middle.1 = (bf16[384,8,256]{2,1,0:T(8,128)(2,1)S(1)}, bf16[256,256]{1,0:T(8,128)(2,1)S(1)}) custom-call(s32[2,8,32]{2,1,0:T(8,128)S(1)} %get-tuple-element.9.slots_ref, f32[2,8,32]{2,1,0:T(8,128)S(1)} %bitcast.26, bf16[384,8,256]{2,1,0:T(8,128)(2,1)S(1)} %bitcast.16, bf16[32,2048]{1,0:T(8,128)(2,1)S(1)} %copy-done, f32[2,2048]{1,0:T(2,128)S(1)} %copy-done.4), custom_call_target="tpu_custom_call" | custom-call | tf_op jit(solution)/shard_map/middle/pallas_call | solution.py:350
  74.1 28.5 %all_to_all.22 = bf16[128,24,256]{2,1,0:T(8,128)(2,1)S(1)} all-to-all(bf16[128,24,256]{2,1,0:T(8,128)(2,1)S(1)} %bitcast.22), channel_id=1, replica_groups=mesh['dp'=8,'expert'=16] {'dp','expert'}, dimensions={0} | all-to-all | bytes 3145728 | tf_op jit(solution)/shard_map/all_to_all | solution.py:303
  102.5 5.8 %expert.3 = bf16[3072,256]{1,0:T(8,128)(2,1)S(1)} custom-call(f32[2,12,1,16]{3,2,1,0:T(1,128)S(1)} %bitcast.25, f32[2,6,1,16]{3,2,1,0:T(1,128)S(1)} %bitcast.29, bf16[3072,256]{1,0:T(8,128)(2,1)S(1)} %bitcast.20, bf16[2,1,2048,1536]{3,2,1,0:T(8,128)(2,1)S(1)} %bitcast.13, bf16[2,1,768,2048]{3,2,1,0:T(8,128)(2,1)S(1)} %bitcast.15), custom_call_target="tpu_custom_call" | custom-call | flops 3623878656 | bytes 12582912 | tf_op jit(solution)/shard_map/expert/pallas_call | solution.py:277
  108.3 28.5 %all_to_all.23 = bf16[128,24,256]{2,1,0:T(8,128)(2,1)S(1)} all-to-all(bf16[128,24,256]{2,1,0:T(8,128)(2,1)S(1)} %bitcast.21), channel_id=1, replica_groups=mesh['dp'=8,'expert'=16] {'dp','expert'}, dimensions={0} | all-to-all | bytes 3145728 | tf_op jit(solution)/shard_map/all_to_all | solution.py:303
  136.7 1.9 %last.1 = bf16[32,2048]{1,0:T(8,128)(2,1)} custom-call(s32[2,8,32]{2,1,0:T(8,128)S(1)} %get-tuple-element.9.slots_ref, f32[2,8,32]{2,1,0:T(8,128)S(1)} %bitcast.27, bf16[384,8,256]{2,1,0:T(8,128)(2,1)S(1)} %bitcast.17, bf16[256,256]{1,0:T(8,128)(2,1)S(1)} %get-tuple-element.12.stream_ref), custom_call_target="tpu_custom_call" | custom-call | tf_op jit(solution)/shard_map/last/pallas_call | solution.py:368
  (7 shorter events, 0.0 us)
Async XLA Ops:
  0.0 38.1 %slice-start = ((s8[12582912]{0:T(1024)(128)(4,1)}), s8[4194304]{0:T(1024)(128)(4,1)S(1)}, s32[]{:S(2)}) async-start(s8[12582912]{0:T(1024)(128)(4,1)} %bitcast.12), calls=%async_computation.4 | async-start | bytes 8388608
  0.0 38.1 %slice-start.3 = ((s8[6291456]{0:T(1024)(128)(4,1)}), s8[4194304]{0:T(1024)(128)(4,1)S(1)}, s32[]{:S(2)}) async-start(s8[6291456]{0:T(1024)(128)(4,1)} %bitcast.14), calls=%async_computation.7 | async-start | bytes 8388608
  0.0 38.1 %slice-start.1 = ((s8[12582912]{0:T(1024)(128)(4,1)}), s8[4194304]{0:T(1024)(128)(4,1)S(1)}, s32[]{:S(2)}) async-start(s8[12582912]{0:T(1024)(128)(4,1)} %bitcast.12), calls=%async_computation.5 | async-start | bytes 8388608
  0.0 38.1 %slice-start.2 = ((s8[12582912]{0:T(1024)(128)(4,1)}), s8[4194304]{0:T(1024)(128)(4,1)S(1)}, s32[]{:S(2)}) async-start(s8[12582912]{0:T(1024)(128)(4,1)} %bitcast.12), calls=%async_computation.6 | async-start | bytes 8388608
  0.0 38.1 %slice-start.4 = ((s8[6291456]{0:T(1024)(128)(4,1)}), s8[2097152]{0:T(1024)(128)(4,1)S(1)}, s32[]{:S(2)}) async-start(s8[6291456]{0:T(1024)(128)(4,1)} %bitcast.14), calls=%async_computation.8 | async-start | bytes 4194304
  2.7 35.5 %copy-start.1 = (f32[2,1,16,12]{2,1,3,0:T(1,128)S(1)}, f32[2,1,16,12]{2,1,3,0:T(1,128)}, u32[]{:S(2)}) copy-start(f32[2,1,16,12]{2,1,3,0:T(1,128)} %param.15) | copy-start | bytes 4612
  2.7 35.5 %copy-start.3 = (f32[2,1,6,16]{3,1,2,0:T(1,128)S(1)}, f32[2,1,6,16]{3,1,2,0:T(1,128)}, u32[]{:S(2)}) copy-start(f32[2,1,6,16]{3,1,2,0:T(1,128)} %param.17) | copy-start | bytes 2308
  44.0 28.6 %copy-start = (bf16[32,2048]{1,0:T(8,128)(2,1)S(1)}, bf16[32,2048]{1,0:T(8,128)(2,1)}, u32[]{:S(2)}) copy-start(bf16[32,2048]{1,0:T(8,128)(2,1)} %stream_ref.1) | copy-start | bytes 393220
  44.0 28.6 %copy-start.2 = (f32[2,32,8]{1,2,0:T(8,128)S(1)}, f32[2,32,8]{1,2,0:T(8,128)}, u32[]{:S(2)}) copy-start(f32[2,32,8]{1,2,0:T(8,128)} %param.12) | copy-start | bytes 6148
  44.0 28.6 %copy-start.4 = (f32[2,2048]{1,0:T(2,128)S(1)}, f32[2,2048]{1,0:T(2,128)}, u32[]{:S(2)}) copy-start(f32[2,2048]{1,0:T(2,128)} %gain_ref.1) | copy-start | bytes 49156

commit v7 on v6

--- a/solution.py
+++ b/solution.py
@@ -181,9 +181,15 @@
 
 
 def middle_kernel(
-    layer, first, slots_ref, gates_ref, back_ref, stream_ref, gain_ref,
-    slab_ref, out_ref, mixed_ref, gain_rows, stack_ref,
+    layer, first, slots_in, gates_in, back_ref, stream_ref, gain_ref,
+    slab_ref, out_ref, mixed_ref, gain_rows, stack_ref, slots_ref, gates_ref, sems,
 ):
+    loads = [
+        pltpu.make_async_copy(slots_in, slots_ref, sems.at[0]),
+        pltpu.make_async_copy(gates_in, gates_ref, sems.at[1]),
+    ]
+    for load in loads:
+        load.start()
     slab_ref[...] = jnp.zeros(slab_ref.shape, jnp.bfloat16)
     tokens, pieces, piece = mixed_ref.shape
     if first:
@@ -194,6 +200,8 @@
         gain_rows[p : p + 1, :] = gain_ref[
             layer + 1 : layer + 2, p * piece : (p + 1) * piece
         ]
+    for load in loads:
+        load.wait()
     mix_blocks(layer, slots_ref, gates_ref, back_ref, mixed_ref)
     stream = (blocks + mixed_ref[...].reshape(tokens * pieces, piece)).astype(jnp.bfloat16)
     out_ref[...] = stream
@@ -208,18 +216,23 @@
 
 
 def last_kernel(
-    layer, slots_ref, gates_ref, back_ref, stream_ref, out_ref, mixed_ref
+    layer, slab_in, stream_ref, routes_ref, gates_ref, place_ref, out_ref, rows_ref
 ):
-    tokens, pieces, piece = mixed_ref.shape
-    mix_blocks(layer, slots_ref, gates_ref, back_ref, mixed_ref)
-    stream = (
-        stream_ref[...].astype(jnp.float32) + mixed_ref[...].reshape(tokens * pieces, piece)
-    ).astype(jnp.bfloat16)
-    rows = jnp.dot(unfold_matrix(), stream, preferred_element_type=jnp.float32).astype(
-        jnp.bfloat16
+    _, weight = slot_tables(routes_ref[layer], place_ref[layer : layer + 1, :], gates_ref[layer])
+    tokens, piece = weight.shape[0], slab_in.shape[1]
+    stream = jnp.dot(unfold_matrix(), stream_ref[...], preferred_element_type=jnp.float32)
+    unfold_rows(slab_in, rows_ref)
+    high = weight.astype(jnp.bfloat16)
+    low = (weight - high.astype(jnp.float32)).astype(jnp.bfloat16)
+    both = jnp.dot(
+        jnp.concatenate([high, low], axis=0), rows_ref[...], preferred_element_type=jnp.float32
     )
-    for p in range(pieces):
-        out_ref[:, p * piece : (p + 1) * piece] = rows[p * tokens : (p + 1) * tokens]
+    mixed = both[:tokens] + both[tokens:]
+    for p in range(PIECES):
+        cols = slice(p * piece, (p + 1) * piece)
+        out_ref[:, cols] = (stream[p * tokens : (p + 1) * tokens] + mixed[:, cols]).astype(
+            jnp.bfloat16
+        )
 
 
 def block_weight(w_ref, factor, layer, first, count):
@@ -239,15 +252,25 @@
 
 
 def expert_kernel(
-    layer, in_scale, out_scale, slab_in, w_in, w_out, slab_ref, x_ref, hid, stack_ref
+    layer, in_factors, out_factors, slab_in, w_in, w_out,
+    slab_ref, x_ref, hid, stack_ref, in_scale, out_scale, sems,
 ):
+    loads = [
+        pltpu.make_async_copy(in_factors.at[layer : layer + 1], in_scale, sems.at[0]),
+        pltpu.make_async_copy(out_factors.at[layer : layer + 1], out_scale, sems.at[1]),
+    ]
+    for load in loads:
+        load.start()
+
     def into(first, count):
-        return block_weight(w_in, lambda i, j: in_scale[layer, j, 0, i], layer, first, count)
+        return block_weight(w_in, lambda i, j: in_scale[0, j, 0, i], layer, first, count)
 
     def out_of(first, count):
-        return block_weight(w_out, lambda i, j: out_scale[layer, i, 0, j], layer, first, count)
+        return block_weight(w_out, lambda i, j: out_scale[0, i, 0, j], layer, first, count)
 
     unfold_rows(slab_in, x_ref)
+    for load in loads:
+        load.wait()
     ff = w_out.shape[2]
     chunk = slab_ref.shape[1]
     for n in range(ff // chunk):
@@ -265,7 +288,6 @@
 
 
 VM = pl.BlockSpec(memory_space=pltpu.VMEM)
-SM = pl.BlockSpec(memory_space=pltpu.SMEM)
 HB = pl.BlockSpec(memory_space=pltpu.HBM)
 
 
@@ -276,13 +298,16 @@
     width, ff = w_in.shape[2], w_out.shape[2]
     return pl.pallas_call(
         functools.partial(expert_kernel, layer),
-        in_specs=[SM, SM, VM, VM, VM],
+        in_specs=[VM] * 5,
         out_specs=VM,
         out_shape=jax.ShapeDtypeStruct(slab.shape, jnp.bfloat16),
         scratch_shapes=[
             pltpu.VMEM((slots, width), jnp.bfloat16),
             pltpu.VMEM((slots, ff), jnp.bfloat16),
             pltpu.VMEM(slab.shape, jnp.bfloat16),
+            pltpu.SMEM((1, *in_scale.shape[1:]), jnp.float32),
+            pltpu.SMEM((1, *out_scale.shape[1:]), jnp.float32),
+            pltpu.SemaphoreType.DMA((2,)),
         ],
         compiler_params=pltpu.CompilerParams(vmem_limit_bytes=20 * MIB),
         cost_estimate=pl.CostEstimate(
@@ -345,35 +370,38 @@
     stream = tokens
     for layer in range(layers):
         answers = expert(layer, exchange(slab, devices), weights)
-        back = exchange(answers, devices).reshape(slots, PIECES, piece)
+        back = exchange(answers, devices)
         if layer + 1 < layers:
             slab, stream = pl.pallas_call(
                 functools.partial(middle_kernel, layer, layer == 0),
-                in_specs=[SM, SM, VM, VM, VM],
+                in_specs=[VM] * 5,
                 out_specs=(VM, VM),
                 out_shape=(
-                    jax.ShapeDtypeStruct(back.shape, jnp.bfloat16),
+                    jax.ShapeDtypeStruct((slots, PIECES, piece), jnp.bfloat16),
                     jax.ShapeDtypeStruct((count * PIECES, piece), jnp.bfloat16),
                 ),
                 scratch_shapes=[
                     mixed,
                     pltpu.VMEM((PIECES, piece), jnp.float32),
                     pltpu.VMEM((count * PIECES, piece), jnp.bfloat16),
+                    pltpu.SMEM(numbers.shape, jnp.int32),
+                    pltpu.SMEM(gates_t.shape, jnp.float32),
+                    pltpu.SemaphoreType.DMA((2,)),
                 ],
                 compiler_params=params,
                 name="middle",
-            )(numbers, gates_t, back, stream, norm_gain)
+            )(numbers, gates_t, back.reshape(slots, PIECES, piece), stream, norm_gain)
             slab = slab.reshape(slots * PIECES, piece)
         else:
             stream = pl.pallas_call(
                 functools.partial(last_kernel, layer),
-                in_specs=[SM, SM, VM, VM],
+                in_specs=[VM] * 5,
                 out_specs=VM,
                 out_shape=stream_type,
-                scratch_shapes=[mixed],
+                scratch_shapes=[pltpu.VMEM((slots, width), jnp.bfloat16)],
                 compiler_params=params,
                 name="last",
-            )(numbers, gates_t, back, stream)
+            )(back, stream, routes_t, gates_t, placement)
     return stream
 
 

time: 139 us -> 138 us (level)
  no operation moved by 1% of the time
where the time goes in v7:
time: 138 us
  blocking collectives  121 us (88%)
  Pallas kernels  16.6 us (12%)
    all_to_all x4, blocking collectives, exchange(): moved = lax.all_to_all(split, AXES, split_axis=0, concat_axis=0, tiled=True)  121 us
    pallas_call x2, Pallas kernels, expert(): pl.pallas_call(functools.partial(expert_kernel, layer), in_specs=[VM] * 5...  10.5 us

profile of v7, /device:TPU:1, one launch (start us, length us, event | category | flops | bytes accessed | tf_op | source)
XLA Modules:
  0.0 137.8 jit_solution(2173441203567193054)
XLA Ops:
  0.0 0.0 slice-start.2
  0.0 0.0 slice-start.4
  0.0 2.6 %first.1 = (bf16[3072,256]{1,0:T(8,128)(2,1)S(1)}, s32[2,8,32]{2,1,0:T(8,128)S(1)}) custom-call(bf16[32,2048]{1,0:T(8,128)(2,1)} %stream_ref.1, f32[2,2048]{1,0:T(2,128)} %gain_ref.1, s32[2,8,32]{2,1,0:T(8,128)} %bitcast.30, s32[2,128]{1,0:T(2,128)} %place_ref.1), custom_call_target="tpu_custom_call" | custom-call | flops 8000000000 | bytes 8000000 | tf_op jit(solution)/shard_map/first/pallas_call | solution.py:352
  2.7 0.0 copy-start.1
  2.7 0.0 copy-start.3
  2.7 35.5 %all_to_all.20 = bf16[128,24,256]{2,1,0:T(8,128)(2,1)S(1)} all-to-all(bf16[128,24,256]{2,1,0:T(8,128)(2,1)S(1)} %bitcast.23), channel_id=1, replica_groups=mesh['dp'=8,'expert'=16] {'dp','expert'}, dimensions={0} | all-to-all | bytes 3145728 | tf_op jit(solution)/shard_map/all_to_all | solution.py:328
  38.2 0.0 slice-done.2
  38.2 0.0 slice-done.4
  38.2 0.0 copy-done.1
  38.2 0.0 copy-done.3
  38.2 5.2 %expert.2 = bf16[3072,256]{1,0:T(8,128)(2,1)S(1)} custom-call(f32[2,12,1,16]{3,2,1,0:T(1,128)S(1)} %bitcast.24, f32[2,6,1,16]{3,2,1,0:T(1,128)S(1)} %bitcast.28, bf16[3072,256]{1,0:T(8,128)(2,1)S(1)} %bitcast.18, bf16[2,1,2048,1536]{3,2,1,0:T(8,128)(2,1)S(1)} %bitcast.13, bf16[2,1,768,2048]{3,2,1,0:T(8,128)(2,1)S(1)} %bitcast.15), custom_call_target="tpu_custom_call" | custom-call | flops 3623878656 | bytes 12582912 | tf_op jit(solution)/shard_map/expert/pallas_call | solution.py:299
  43.5 0.0 copy-start
  43.5 0.0 copy-start.2
  43.5 0.0 copy-start.4
  43.5 28.6 %all_to_all.21 = bf16[128,24,256]{2,1,0:T(8,128)(2,1)S(1)} all-to-all(bf16[128,24,256]{2,1,0:T(8,128)(2,1)S(1)} %bitcast.19), channel_id=1, replica_groups=mesh['dp'=8,'expert'=16] {'dp','expert'}, dimensions={0} | all-to-all | bytes 3145728 | tf_op jit(solution)/shard_map/all_to_all | solution.py:328
  72.1 0.0 copy-done
  72.1 1.4 %middle.1 = (bf16[384,8,256]{2,1,0:T(8,128)(2,1)S(1)}, bf16[256,256]{1,0:T(8,128)(2,1)S(1)}) custom-call(s32[2,8,32]{2,1,0:T(8,128)S(1)} %get-tuple-element.9.slots_in, f32[2,8,32]{2,1,0:T(8,128)S(1)} %bitcast.26, bf16[384,8,256]{2,1,0:T(8,128)(2,1)S(1)} %bitcast.16, bf16[32,2048]{1,0:T(8,128)(2,1)S(1)} %copy-done, f32[2,2048]{1,0:T(2,128)S(1)} %copy-done.4), custom_call_target="tpu_custom_call" | custom-call | tf_op jit(solution)/shard_map/middle/pallas_call | solution.py:375
  73.5 28.5 %all_to_all.22 = bf16[128,24,256]{2,1,0:T(8,128)(2,1)S(1)} all-to-all(bf16[128,24,256]{2,1,0:T(8,128)(2,1)S(1)} %bitcast.22), channel_id=1, replica_groups=mesh['dp'=8,'expert'=16] {'dp','expert'}, dimensions={0} | all-to-all | bytes 3145728 | tf_op jit(solution)/shard_map/all_to_all | solution.py:328
  101.9 5.2 %expert.3 = bf16[3072,256]{1,0:T(8,128)(2,1)S(1)} custom-call(f32[2,12,1,16]{3,2,1,0:T(1,128)S(1)} %bitcast.25, f32[2,6,1,16]{3,2,1,0:T(1,128)S(1)} %bitcast.29, bf16[3072,256]{1,0:T(8,128)(2,1)S(1)} %bitcast.20, bf16[2,1,2048,1536]{3,2,1,0:T(8,128)(2,1)S(1)} %bitcast.13, bf16[2,1,768,2048]{3,2,1,0:T(8,128)(2,1)S(1)} %bitcast.15), custom_call_target="tpu_custom_call" | custom-call | flops 3623878656 | bytes 12582912 | tf_op jit(solution)/shard_map/expert/pallas_call | solution.py:299
  107.2 0.0 copy-start.5
  107.2 0.0 copy-start.6
  107.2 28.5 %all_to_all.23 = bf16[128,24,256]{2,1,0:T(8,128)(2,1)S(1)} all-to-all(bf16[128,24,256]{2,1,0:T(8,128)(2,1)S(1)} %bitcast.21), channel_id=1, replica_groups=mesh['dp'=8,'expert'=16] {'dp','expert'}, dimensions={0} | all-to-all | bytes 3145728 | tf_op jit(solution)/shard_map/all_to_all | solution.py:328
  135.7 0.0 copy-done.5
  135.7 2.1 %last.1 = bf16[32,2048]{1,0:T(8,128)(2,1)} custom-call(bf16[3072,256]{1,0:T(8,128)(2,1)S(1)} %bitcast.17, bf16[256,256]{1,0:T(8,128)(2,1)S(1)} %get-tuple-element.12.stream_ref, s32[2,8,32]{2,1,0:T(8,128)S(1)} %bitcast.31, f32[2,8,32]{2,1,0:T(8,128)S(1)} %bitcast.27, s32[2,128]{1,0:T(2,128)S(1)} %copy-done.6), custom_call_target="tpu_custom_call" | custom-call | tf_op jit(solution)/shard_map/last/pallas_call | solution.py:396
  (11 shorter events, 0.0 us)
Async XLA Ops:
  0.0 38.2 %slice-start = ((s8[12582912]{0:T(1024)(128)(4,1)}), s8[4194304]{0:T(1024)(128)(4,1)S(1)}, s32[]{:S(2)}) async-start(s8[12582912]{0:T(1024)(128)(4,1)} %bitcast.12), calls=%async_computation.4 | async-start | bytes 8388608
  0.0 38.2 %slice-start.3 = ((s8[6291456]{0:T(1024)(128)(4,1)}), s8[4194304]{0:T(1024)(128)(4,1)S(1)}, s32[]{:S(2)}) async-start(s8[6291456]{0:T(1024)(128)(4,1)} %bitcast.14), calls=%async_computation.7 | async-start | bytes 8388608
  0.0 38.2 %slice-start.1 = ((s8[12582912]{0:T(1024)(128)(4,1)}), s8[4194304]{0:T(1024)(128)(4,1)S(1)}, s32[]{:S(2)}) async-start(s8[12582912]{0:T(1024)(128)(4,1)} %bitcast.12), calls=%async_computation.5 | async-start | bytes 8388608
  0.0 38.2 %slice-start.2 = ((s8[12582912]{0:T(1024)(128)(4,1)}), s8[4194304]{0:T(1024)(128)(4,1)S(1)}, s32[]{:S(2)}) async-start(s8[12582912]{0:T(1024)(128)(4,1)} %bitcast.12), calls=%async_computation.6 | async-start | bytes 8388608
  0.0 38.2 %slice-start.4 = ((s8[6291456]{0:T(1024)(128)(4,1)}), s8[2097152]{0:T(1024)(128)(4,1)S(1)}, s32[]{:S(2)}) async-start(s8[6291456]{0:T(1024)(128)(4,1)} %bitcast.14), calls=%async_computation.8 | async-start | bytes 4194304
  2.7 35.5 %copy-start.1 = (f32[2,1,16,12]{2,1,3,0:T(1,128)S(1)}, f32[2,1,16,12]{2,1,3,0:T(1,128)}, u32[]{:S(2)}) copy-start(f32[2,1,16,12]{2,1,3,0:T(1,128)} %param.15) | copy-start | bytes 4612
  2.7 35.5 %copy-start.3 = (f32[2,1,6,16]{3,1,2,0:T(1,128)S(1)}, f32[2,1,6,16]{3,1,2,0:T(1,128)}, u32[]{:S(2)}) copy-start(f32[2,1,6,16]{3,1,2,0:T(1,128)} %param.17) | copy-start | bytes 2308
  43.5 28.6 %copy-start = (bf16[32,2048]{1,0:T(8,128)(2,1)S(1)}, bf16[32,2048]{1,0:T(8,128)(2,1)}, u32[]{:S(2)}) copy-start(bf16[32,2048]{1,0:T(8,128)(2,1)} %stream_ref.1) | copy-start | bytes 393220
  43.5 28.6 %copy-start.2 = (f32[2,32,8]{1,2,0:T(8,128)S(1)}, f32[2,32,8]{1,2,0:T(8,128)}, u32[]{:S(2)}) copy-start(f32[2,32,8]{1,2,0:T(8,128)} %param.12) | copy-start | bytes 6148
  43.5 28.6 %copy-start.4 = (f32[2,2048]{1,0:T(2,128)S(1)}, f32[2,2048]{1,0:T(2,128)}, u32[]{:S(2)}) copy-start(f32[2,2048]{1,0:T(2,128)} %gain_ref.1) | copy-start | bytes 49156
  107.2 28.5 %copy-start.5 = (s32[2,32,8]{1,2,0:T(8,128)S(1)}, s32[2,32,8]{1,2,0:T(8,128)}, u32[]{:S(2)}) copy-start(s32[2,32,8]{1,2,0:T(8,128)} %param.11) | copy-start | bytes 6148
  107.2 28.5 %copy-start.6 = (s32[2,128]{1,0:T(2,128)S(1)}, s32[2,128]{1,0:T(2,128)}, u32[]{:S(2)}) copy-start(s32[2,128]{1,0:T(2,128)} %place_ref.1) | copy-start | bytes 3076

commit v8 on v7

--- a/solution.py
+++ b/solution.py
@@ -135,11 +135,11 @@
     return jnp.transpose(slots).astype(jnp.int32)
 
 
-def mix_blocks(layer, slots_ref, gates_ref, back_ref, mixed_ref):
+def mix_blocks(slots_ref, gates_ref, back_ref, mixed_ref):
     for t in range(mixed_ref.shape[0]):
         total = None
         for k in range(gates_ref.shape[1]):
-            block = back_ref[slots_ref[layer, k, t]].astype(jnp.float32) * gates_ref[layer, k, t]
+            block = back_ref[slots_ref[0, k, t]].astype(jnp.float32) * gates_ref[0, k, t]
             total = block if total is None else total + block
         mixed_ref[t] = total
 
@@ -185,8 +185,13 @@
     slab_ref, out_ref, mixed_ref, gain_rows, stack_ref, slots_ref, gates_ref, sems,
 ):
     loads = [
-        pltpu.make_async_copy(slots_in, slots_ref, sems.at[0]),
-        pltpu.make_async_copy(gates_in, gates_ref, sems.at[1]),
+        pltpu.make_async_copy(
+            slots_in.at[layer : layer + 1], slots_ref.at[0:1], sems.at[0]
+        ),
+        pltpu.make_async_copy(gates_in.at[layer : layer + 1], gates_ref, sems.at[1]),
+        pltpu.make_async_copy(
+            slots_in.at[layer + 1 : layer + 2], slots_ref.at[1:2], sems.at[2]
+        ),
     ]
     for load in loads:
         load.start()
@@ -200,39 +205,36 @@
         gain_rows[p : p + 1, :] = gain_ref[
             layer + 1 : layer + 2, p * piece : (p + 1) * piece
         ]
-    for load in loads:
-        load.wait()
-    mix_blocks(layer, slots_ref, gates_ref, back_ref, mixed_ref)
+    loads[0].wait()
+    loads[1].wait()
+    mix_blocks(slots_ref, gates_ref, back_ref, mixed_ref)
     stream = (blocks + mixed_ref[...].reshape(tokens * pieces, piece)).astype(jnp.bfloat16)
     out_ref[...] = stream
     wide = stream.astype(jnp.float32).reshape(tokens, pieces, piece)
     total = jnp.sum(jnp.sum(wide * wide, axis=2, keepdims=True), axis=1, keepdims=True)
     scale = lax.rsqrt(total / (pieces * piece) + EPS)
     mixed_ref[...] = wide * scale * gain_rows[...][None]
+    loads[2].wait()
     for t in range(tokens):
         row = mixed_ref[t].astype(jnp.bfloat16)
         for k in range(slots_ref.shape[1]):
-            slab_ref[slots_ref[layer + 1, k, t]] = row
+            slab_ref[slots_ref[1, k, t]] = row
 
 
 def last_kernel(
-    layer, slab_in, stream_ref, routes_ref, gates_ref, place_ref, out_ref, rows_ref
+    layer, slab_in, blocks_ref, routes_ref, gates_ref, place_ref, out_ref, rows_ref, stream_ref
 ):
     _, weight = slot_tables(routes_ref[layer], place_ref[layer : layer + 1, :], gates_ref[layer])
-    tokens, piece = weight.shape[0], slab_in.shape[1]
-    stream = jnp.dot(unfold_matrix(), stream_ref[...], preferred_element_type=jnp.float32)
+    unfold_rows(blocks_ref, stream_ref)
     unfold_rows(slab_in, rows_ref)
     high = weight.astype(jnp.bfloat16)
     low = (weight - high.astype(jnp.float32)).astype(jnp.bfloat16)
     both = jnp.dot(
         jnp.concatenate([high, low], axis=0), rows_ref[...], preferred_element_type=jnp.float32
     )
+    tokens = weight.shape[0]
     mixed = both[:tokens] + both[tokens:]
-    for p in range(PIECES):
-        cols = slice(p * piece, (p + 1) * piece)
-        out_ref[:, cols] = (stream[p * tokens : (p + 1) * tokens] + mixed[:, cols]).astype(
-            jnp.bfloat16
-        )
+    out_ref[...] = (stream_ref[...].astype(jnp.float32) + mixed).astype(jnp.bfloat16)
 
 
 def block_weight(w_ref, factor, layer, first, count):
@@ -384,9 +386,9 @@
                     mixed,
                     pltpu.VMEM((PIECES, piece), jnp.float32),
                     pltpu.VMEM((count * PIECES, piece), jnp.bfloat16),
-                    pltpu.SMEM(numbers.shape, jnp.int32),
-                    pltpu.SMEM(gates_t.shape, jnp.float32),
-                    pltpu.SemaphoreType.DMA((2,)),
+                    pltpu.SMEM((2, *numbers.shape[1:]), jnp.int32),
+                    pltpu.SMEM((1, *gates_t.shape[1:]), jnp.float32),
+                    pltpu.SemaphoreType.DMA((3,)),
                 ],
                 compiler_params=params,
                 name="middle",
@@ -398,7 +400,10 @@
                 in_specs=[VM] * 5,
                 out_specs=VM,
                 out_shape=stream_type,
-                scratch_shapes=[pltpu.VMEM((slots, width), jnp.bfloat16)],
+                scratch_shapes=[
+                    pltpu.VMEM((slots, width), jnp.bfloat16),
+                    pltpu.VMEM((count, width), jnp.bfloat16),
+                ],
                 compiler_params=params,
                 name="last",
             )(back, stream, routes_t, gates_t, placement)

time: 138 us -> 138 us (level)
  no operation moved by 1% of the time
where the time goes in v8:
time: 138 us; the launch traced here: 137 us
  blocking collectives  121 us (88%)
  Pallas kernels  16.3 us (12%)
    all_to_all x4, blocking collectives, exchange(): moved = lax.all_to_all(split, AXES, split_axis=0, concat_axis=0, tiled=True)  121 us
    pallas_call x2, Pallas kernels, expert(): pl.pallas_call(functools.partial(expert_kernel, layer), in_specs=[VM] * 5...  10.5 us

profile of v8, /device:TPU:1, one launch (start us, length us, event | category | flops | bytes accessed | tf_op | source)
XLA Modules:
  0.0 137.5 jit_solution(14111602485519925125)
XLA Ops:
  0.0 0.0 slice-start.2
  0.0 0.0 slice-start.4
  0.0 2.6 %first.1 = (bf16[3072,256]{1,0:T(8,128)(2,1)S(1)}, s32[2,8,32]{2,1,0:T(8,128)S(1)}) custom-call(bf16[32,2048]{1,0:T(8,128)(2,1)} %stream_ref.1, f32[2,2048]{1,0:T(2,128)} %gain_ref.1, s32[2,8,32]{2,1,0:T(8,128)} %bitcast.30, s32[2,128]{1,0:T(2,128)} %place_ref.1), custom_call_target="tpu_custom_call" | custom-call | flops 8000000000 | bytes 8000000 | tf_op jit(solution)/shard_map/first/pallas_call | solution.py:354
  2.7 0.0 copy-start.1
  2.7 0.0 copy-start.3
  2.7 35.5 %all_to_all.20 = bf16[128,24,256]{2,1,0:T(8,128)(2,1)S(1)} all-to-all(bf16[128,24,256]{2,1,0:T(8,128)(2,1)S(1)} %bitcast.23), channel_id=1, replica_groups=mesh['dp'=8,'expert'=16] {'dp','expert'}, dimensions={0} | all-to-all | bytes 3145728 | tf_op jit(solution)/shard_map/all_to_all | solution.py:330
  38.2 0.0 slice-done.2
  38.2 0.0 slice-done.4
  38.2 0.0 copy-done.1
  38.2 0.0 copy-done.3
  38.2 5.2 %expert.2 = bf16[3072,256]{1,0:T(8,128)(2,1)S(1)} custom-call(f32[2,12,1,16]{3,2,1,0:T(1,128)S(1)} %bitcast.24, f32[2,6,1,16]{3,2,1,0:T(1,128)S(1)} %bitcast.28, bf16[3072,256]{1,0:T(8,128)(2,1)S(1)} %bitcast.18, bf16[2,1,2048,1536]{3,2,1,0:T(8,128)(2,1)S(1)} %bitcast.13, bf16[2,1,768,2048]{3,2,1,0:T(8,128)(2,1)S(1)} %bitcast.15), custom_call_target="tpu_custom_call" | custom-call | flops 3623878656 | bytes 12582912 | tf_op jit(solution)/shard_map/expert/pallas_call | solution.py:301
  43.5 0.0 copy-start
  43.5 0.0 copy-start.2
  43.5 0.0 copy-start.4
  43.5 28.6 %all_to_all.21 = bf16[128,24,256]{2,1,0:T(8,128)(2,1)S(1)} all-to-all(bf16[128,24,256]{2,1,0:T(8,128)(2,1)S(1)} %bitcast.19), channel_id=1, replica_groups=mesh['dp'=8,'expert'=16] {'dp','expert'}, dimensions={0} | all-to-all | bytes 3145728 | tf_op jit(solution)/shard_map/all_to_all | solution.py:330
  72.1 0.0 copy-done
  72.1 0.0 copy-done.4
  72.1 1.4 middle.1
  73.5 28.5 %all_to_all.22 = bf16[128,24,256]{2,1,0:T(8,128)(2,1)S(1)} all-to-all(bf16[128,24,256]{2,1,0:T(8,128)(2,1)S(1)} %bitcast.22), channel_id=1, replica_groups=mesh['dp'=8,'expert'=16] {'dp','expert'}, dimensions={0} | all-to-all | bytes 3145728 | tf_op jit(solution)/shard_map/all_to_all | solution.py:330
  101.9 5.2 %expert.3 = bf16[3072,256]{1,0:T(8,128)(2,1)S(1)} custom-call(f32[2,12,1,16]{3,2,1,0:T(1,128)S(1)} %bitcast.25, f32[2,6,1,16]{3,2,1,0:T(1,128)S(1)} %bitcast.29, bf16[3072,256]{1,0:T(8,128)(2,1)S(1)} %bitcast.20, bf16[2,1,2048,1536]{3,2,1,0:T(8,128)(2,1)S(1)} %bitcast.13, bf16[2,1,768,2048]{3,2,1,0:T(8,128)(2,1)S(1)} %bitcast.15), custom_call_target="tpu_custom_call" | custom-call | flops 3623878656 | bytes 12582912 | tf_op jit(solution)/shard_map/expert/pallas_call | solution.py:301
  107.2 0.0 copy-start.5
  107.2 0.0 copy-start.6
  107.2 28.5 %all_to_all.23 = bf16[128,24,256]{2,1,0:T(8,128)(2,1)S(1)} all-to-all(bf16[128,24,256]{2,1,0:T(8,128)(2,1)S(1)} %bitcast.21), channel_id=1, replica_groups=mesh['dp'=8,'expert'=16] {'dp','expert'}, dimensions={0} | all-to-all | bytes 3145728 | tf_op jit(solution)/shard_map/all_to_all | solution.py:330
  135.6 1.8 %last.1 = bf16[32,2048]{1,0:T(8,128)(2,1)} custom-call(bf16[3072,256]{1,0:T(8,128)(2,1)S(1)} %bitcast.17, bf16[256,256]{1,0:T(8,128)(2,1)S(1)} %get-tuple-element.12.blocks_ref, s32[2,8,32]{2,1,0:T(8,128)S(1)} %bitcast.31, f32[2,8,32]{2,1,0:T(8,128)S(1)} %bitcast.27, s32[2,128]{1,0:T(2,128)S(1)} %copy-done.6), custom_call_target="tpu_custom_call" | custom-call | tf_op jit(solution)/shard_map/last/pallas_call | solution.py:398
  (11 shorter events, 0.0 us)
Async XLA Ops:
  0.0 38.2 %slice-start = ((s8[12582912]{0:T(1024)(128)(4,1)}), s8[4194304]{0:T(1024)(128)(4,1)S(1)}, s32[]{:S(2)}) async-start(s8[12582912]{0:T(1024)(128)(4,1)} %bitcast.12), calls=%async_computation.4 | async-start | bytes 8388608
  0.0 38.2 %slice-start.3 = ((s8[6291456]{0:T(1024)(128)(4,1)}), s8[4194304]{0:T(1024)(128)(4,1)S(1)}, s32[]{:S(2)}) async-start(s8[6291456]{0:T(1024)(128)(4,1)} %bitcast.14), calls=%async_computation.7 | async-start | bytes 8388608
  0.0 38.2 %slice-start.1 = ((s8[12582912]{0:T(1024)(128)(4,1)}), s8[4194304]{0:T(1024)(128)(4,1)S(1)}, s32[]{:S(2)}) async-start(s8[12582912]{0:T(1024)(128)(4,1)} %bitcast.12), calls=%async_computation.5 | async-start | bytes 8388608
  0.0 38.2 %slice-start.2 = ((s8[12582912]{0:T(1024)(128)(4,1)}), s8[4194304]{0:T(1024)(128)(4,1)S(1)}, s32[]{:S(2)}) async-start(s8[12582912]{0:T(1024)(128)(4,1)} %bitcast.12), calls=%async_computation.6 | async-start | bytes 8388608
  0.0 38.2 %slice-start.4 = ((s8[6291456]{0:T(1024)(128)(4,1)}), s8[2097152]{0:T(1024)(128)(4,1)S(1)}, s32[]{:S(2)}) async-start(s8[6291456]{0:T(1024)(128)(4,1)} %bitcast.14), calls=%async_computation.8 | async-start | bytes 4194304
  2.7 35.5 %copy-start.1 = (f32[2,1,16,12]{2,1,3,0:T(1,128)S(1)}, f32[2,1,16,12]{2,1,3,0:T(1,128)}, u32[]{:S(2)}) copy-start(f32[2,1,16,12]{2,1,3,0:T(1,128)} %param.15) | copy-start | bytes 4612
  2.7 35.5 %copy-start.3 = (f32[2,1,6,16]{3,1,2,0:T(1,128)S(1)}, f32[2,1,6,16]{3,1,2,0:T(1,128)}, u32[]{:S(2)}) copy-start(f32[2,1,6,16]{3,1,2,0:T(1,128)} %param.17) | copy-start | bytes 2308
  43.5 28.6 %copy-start = (bf16[32,2048]{1,0:T(8,128)(2,1)S(1)}, bf16[32,2048]{1,0:T(8,128)(2,1)}, u32[]{:S(2)}) copy-start(bf16[32,2048]{1,0:T(8,128)(2,1)} %stream_ref.1) | copy-start | bytes 393220
  43.5 28.6 %copy-start.2 = (f32[2,32,8]{1,2,0:T(8,128)S(1)}, f32[2,32,8]{1,2,0:T(8,128)}, u32[]{:S(2)}) copy-start(f32[2,32,8]{1,2,0:T(8,128)} %param.12) | copy-start | bytes 6148
  43.5 28.6 %copy-start.4 = (f32[2,2048]{1,0:T(2,128)S(1)}, f32[2,2048]{1,0:T(2,128)}, u32[]{:S(2)}) copy-start(f32[2,2048]{1,0:T(2,128)} %gain_ref.1) | copy-start | bytes 49156
  107.2 28.5 %copy-start.5 = (s32[2,32,8]{1,2,0:T(8,128)S(1)}, s32[2,32,8]{1,2,0:T(8,128)}, u32[]{:S(2)}) copy-start(s32[2,32,8]{1,2,0:T(8,128)} %param.11) | copy-start | bytes 6148
  107.2 28.5 %copy-start.6 = (s32[2,128]{1,0:T(2,128)S(1)}, s32[2,128]{1,0:T(2,128)}, u32[]{:S(2)}) copy-start(s32[2,128]{1,0:T(2,128)} %place_ref.1) | copy-start | bytes 3076

commit v9 on v8

--- a/solution.py
+++ b/solution.py
@@ -165,12 +165,11 @@
     loads[1].wait()
     select, _ = slot_tables(routes_ref[0], place_ref[0:1, :], None)
     pick = jnp.transpose(select).astype(jnp.bfloat16)
+    slots_ref[0] = slot_numbers(routes_ref[0], place_ref[0:1, :])
     loads[2].wait()
     loads[3].wait()
     normed = normalise(tokens_ref[...].astype(jnp.float32), gain_ref[0:1, :])
     send_rows(pick, normed, stack_ref, slab_ref)
-    for layer in range(routes_ref.shape[0]):
-        slots_ref[layer] = slot_numbers(routes_ref[layer], place_ref[layer : layer + 1, :])
 
 
 def blocks_of(stream_ref, stack_ref):
@@ -181,20 +180,24 @@
 
 
 def middle_kernel(
-    layer, first, slots_in, gates_in, back_ref, stream_ref, gain_ref,
-    slab_ref, out_ref, mixed_ref, gain_rows, stack_ref, slots_ref, gates_ref, sems,
+    layer, first, slots_in, gates_in, back_ref, stream_ref, gain_ref, routes_ref, place_ref,
+    slab_ref, out_ref, next_ref, mixed_ref, gain_rows, stack_ref, numbers_ref,
+    slots_ref, gates_ref, sems,
 ):
     loads = [
-        pltpu.make_async_copy(
-            slots_in.at[layer : layer + 1], slots_ref.at[0:1], sems.at[0]
-        ),
+        pltpu.make_async_copy(slots_in, slots_ref.at[0:1], sems.at[0]),
         pltpu.make_async_copy(gates_in.at[layer : layer + 1], gates_ref, sems.at[1]),
-        pltpu.make_async_copy(
-            slots_in.at[layer + 1 : layer + 2], slots_ref.at[1:2], sems.at[2]
-        ),
+        pltpu.make_async_copy(numbers_ref, slots_ref.at[1:2], sems.at[2]),
     ]
-    for load in loads:
-        load.start()
+    loads[0].start()
+    loads[1].start()
+    later = slice(layer + 1, layer + 2)
+    numbers_ref[0] = slot_numbers(routes_ref[layer + 1], place_ref[later, :])
+    loads[2].start()
+    _, weight = slot_tables(routes_ref[layer + 1], place_ref[later, :], gates_in[layer + 1])
+    high = weight.astype(jnp.bfloat16)
+    low = (weight - high.astype(jnp.float32)).astype(jnp.bfloat16)
+    next_ref[...] = jnp.concatenate([high, low], axis=0)
     slab_ref[...] = jnp.zeros(slab_ref.shape, jnp.bfloat16)
     tokens, pieces, piece = mixed_ref.shape
     if first:
@@ -221,18 +224,11 @@
             slab_ref[slots_ref[1, k, t]] = row
 
 
-def last_kernel(
-    layer, slab_in, blocks_ref, routes_ref, gates_ref, place_ref, out_ref, rows_ref, stream_ref
-):
-    _, weight = slot_tables(routes_ref[layer], place_ref[layer : layer + 1, :], gates_ref[layer])
+def last_kernel(slab_in, blocks_ref, weight_ref, out_ref, rows_ref, stream_ref):
     unfold_rows(blocks_ref, stream_ref)
     unfold_rows(slab_in, rows_ref)
-    high = weight.astype(jnp.bfloat16)
-    low = (weight - high.astype(jnp.float32)).astype(jnp.bfloat16)
-    both = jnp.dot(
-        jnp.concatenate([high, low], axis=0), rows_ref[...], preferred_element_type=jnp.float32
-    )
-    tokens = weight.shape[0]
+    both = jnp.dot(weight_ref[...], rows_ref[...], preferred_element_type=jnp.float32)
+    tokens = weight_ref.shape[0] // 2
     mixed = both[:tokens] + both[tokens:]
     out_ref[...] = (stream_ref[...].astype(jnp.float32) + mixed).astype(jnp.bfloat16)
 
@@ -339,7 +335,7 @@
     routes_t = jnp.swapaxes(routes, 1, 2)
     gates_t = jnp.swapaxes(gates, 1, 2)
     slab_type = jax.ShapeDtypeStruct((slots * PIECES, piece), jnp.bfloat16)
-    slots_type = jax.ShapeDtypeStruct(routes_t.shape, jnp.int32)
+    slots_type = jax.ShapeDtypeStruct((1, *routes_t.shape[1:]), jnp.int32)
     stream_type = jax.ShapeDtypeStruct((count, width), jnp.bfloat16)
     mixed = pltpu.VMEM((count, PIECES, piece), jnp.float32)
     stack = pltpu.VMEM((slots * PIECES, piece), jnp.bfloat16)
@@ -374,30 +370,35 @@
         answers = expert(layer, exchange(slab, devices), weights)
         back = exchange(answers, devices)
         if layer + 1 < layers:
-            slab, stream = pl.pallas_call(
+            slab, stream, weight = pl.pallas_call(
                 functools.partial(middle_kernel, layer, layer == 0),
-                in_specs=[VM] * 5,
-                out_specs=(VM, VM),
+                in_specs=[VM] * 7,
+                out_specs=(VM, VM, VM),
                 out_shape=(
                     jax.ShapeDtypeStruct((slots, PIECES, piece), jnp.bfloat16),
                     jax.ShapeDtypeStruct((count * PIECES, piece), jnp.bfloat16),
+                    jax.ShapeDtypeStruct((2 * count, slots), jnp.bfloat16),
                 ),
                 scratch_shapes=[
                     mixed,
                     pltpu.VMEM((PIECES, piece), jnp.float32),
                     pltpu.VMEM((count * PIECES, piece), jnp.bfloat16),
+                    pltpu.VMEM(numbers.shape, jnp.int32),
                     pltpu.SMEM((2, *numbers.shape[1:]), jnp.int32),
                     pltpu.SMEM((1, *gates_t.shape[1:]), jnp.float32),
                     pltpu.SemaphoreType.DMA((3,)),
                 ],
                 compiler_params=params,
                 name="middle",
-            )(numbers, gates_t, back.reshape(slots, PIECES, piece), stream, norm_gain)
+            )(
+                numbers, gates_t, back.reshape(slots, PIECES, piece), stream, norm_gain,
+                routes_t, placement,
+            )
             slab = slab.reshape(slots * PIECES, piece)
         else:
             stream = pl.pallas_call(
-                functools.partial(last_kernel, layer),
-                in_specs=[VM] * 5,
+                last_kernel,
+                in_specs=[VM] * 3,
                 out_specs=VM,
                 out_shape=stream_type,
                 scratch_shapes=[
@@ -406,7 +407,7 @@
                 ],
                 compiler_params=params,
                 name="last",
-            )(back, stream, routes_t, gates_t, placement)
+            )(back, stream, weight)
     return stream
 
 

time: 138 us -> 137 us (level)
  no operation moved by 1% of the time
where the time goes in v9:
time: 137 us
  blocking collectives  121 us (88%)
  Pallas kernels  16.2 us (12%)
    all_to_all x4, blocking collectives, exchange(): moved = lax.all_to_all(split, AXES, split_axis=0, concat_axis=0, tiled=True)  121 us
    pallas_call x2, Pallas kernels, expert(): pl.pallas_call(functools.partial(expert_kernel, layer), in_specs=[VM] * 5...  10.5 us

profile of v9, /device:TPU:1, one launch (start us, length us, event | category | flops | bytes accessed | tf_op | source)
XLA Modules:
  0.0 137.3 jit_solution(8164925949653098650)
XLA Ops:
  0.0 0.0 slice-start.2
  0.0 0.0 slice-start.4
  0.0 2.6 %first.1 = (bf16[3072,256]{1,0:T(8,128)(2,1)S(1)}, s32[1,8,32]{2,1,0:T(8,128)S(1)}) custom-call(bf16[32,2048]{1,0:T(8,128)(2,1)} %stream_ref.1, f32[2,2048]{1,0:T(2,128)} %gain_ref.1, s32[2,8,32]{2,1,0:T(8,128)} %bitcast.28, s32[2,128]{1,0:T(2,128)} %place_ref.1), custom_call_target="tpu_custom_call" | custom-call | flops 8000000000 | bytes 8000000 | tf_op jit(solution)/shard_map/first/pallas_call | solution.py:350
  2.6 0.0 copy-start.1
  2.6 0.0 copy-start.2
  2.6 35.4 %all_to_all.20 = bf16[128,24,256]{2,1,0:T(8,128)(2,1)S(1)} all-to-all(bf16[128,24,256]{2,1,0:T(8,128)(2,1)S(1)} %bitcast.23), channel_id=1, replica_groups=mesh['dp'=8,'expert'=16] {'dp','expert'}, dimensions={0} | all-to-all | bytes 3145728 | tf_op jit(solution)/shard_map/all_to_all | solution.py:326
  38.1 0.0 slice-done
  38.1 0.0 slice-done.3
  38.1 0.0 slice-done.1
  38.2 5.2 %expert.2 = bf16[3072,256]{1,0:T(8,128)(2,1)S(1)} custom-call(f32[2,12,1,16]{3,2,1,0:T(1,128)S(1)} %bitcast.24, f32[2,6,1,16]{3,2,1,0:T(1,128)S(1)} %bitcast.26, bf16[3072,256]{1,0:T(8,128)(2,1)S(1)} %bitcast.18, bf16[2,1,2048,1536]{3,2,1,0:T(8,128)(2,1)S(1)} %bitcast.13, bf16[2,1,768,2048]{3,2,1,0:T(8,128)(2,1)S(1)} %bitcast.15), custom_call_target="tpu_custom_call" | custom-call | flops 3623878656 | bytes 12582912 | tf_op jit(solution)/shard_map/expert/pallas_call | solution.py:297
  43.4 0.0 copy-start
  43.4 0.0 copy-start.3
  43.4 0.0 copy-start.4
  43.5 0.0 copy-start.5
  43.5 0.0 copy-start.6
  43.5 28.6 %all_to_all.21 = bf16[128,24,256]{2,1,0:T(8,128)(2,1)S(1)} all-to-all(bf16[128,24,256]{2,1,0:T(8,128)(2,1)S(1)} %bitcast.19), channel_id=1, replica_groups=mesh['dp'=8,'expert'=16] {'dp','expert'}, dimensions={0} | all-to-all | bytes 3145728 | tf_op jit(solution)/shard_map/all_to_all | solution.py:326
  72.0 0.0 copy-done.4
  72.0 0.0 copy-done.5
  72.1 0.0 copy-done.6
  72.1 1.5 %middle.1 = (bf16[384,8,256]{2,1,0:T(8,128)(2,1)S(1)}, bf16[256,256]{1,0:T(8,128)(2,1)S(1)}, bf16[64,384]{1,0:T(8,128)(2,1)S(1)}) custom-call(s32[1,8,32]{2,1,0:T(8,128)S(1)} %get-tuple-element.10.slots_in, f32[2,8,32]{2,1,0:T(8,128)S(1)} %bitcast.30, bf16[384,8,256]{2,1,0:T(8,128)(2,1)S(1)} %bitcast.16, bf16[32,2048]{1,0:T(8,128)(2,1)S(1)} %copy-done, ...), custom_call_target="tpu_custom_call" | custom-call | tf_op jit(solution)/shard_map/middle/pallas_call | solution.py:373
  73.6 28.5 %all_to_all.22 = bf16[128,24,256]{2,1,0:T(8,128)(2,1)S(1)} all-to-all(bf16[128,24,256]{2,1,0:T(8,128)(2,1)S(1)} %bitcast.22), channel_id=1, replica_groups=mesh['dp'=8,'expert'=16] {'dp','expert'}, dimensions={0} | all-to-all | bytes 3145728 | tf_op jit(solution)/shard_map/all_to_all | solution.py:326
  102.0 5.2 %expert.3 = bf16[3072,256]{1,0:T(8,128)(2,1)S(1)} custom-call(f32[2,12,1,16]{3,2,1,0:T(1,128)S(1)} %bitcast.25, f32[2,6,1,16]{3,2,1,0:T(1,128)S(1)} %bitcast.27, bf16[3072,256]{1,0:T(8,128)(2,1)S(1)} %bitcast.20, bf16[2,1,2048,1536]{3,2,1,0:T(8,128)(2,1)S(1)} %bitcast.13, bf16[2,1,768,2048]{3,2,1,0:T(8,128)(2,1)S(1)} %bitcast.15), custom_call_target="tpu_custom_call" | custom-call | flops 3623878656 | bytes 12582912 | tf_op jit(solution)/shard_map/expert/pallas_call | solution.py:297
  107.3 28.5 %all_to_all.23 = bf16[128,24,256]{2,1,0:T(8,128)(2,1)S(1)} all-to-all(bf16[128,24,256]{2,1,0:T(8,128)(2,1)S(1)} %bitcast.21), channel_id=1, replica_groups=mesh['dp'=8,'expert'=16] {'dp','expert'}, dimensions={0} | all-to-all | bytes 3145728 | tf_op jit(solution)/shard_map/all_to_all | solution.py:326
  135.7 1.6 %last.1 = bf16[32,2048]{1,0:T(8,128)(2,1)} custom-call(bf16[3072,256]{1,0:T(8,128)(2,1)S(1)} %bitcast.17, bf16[256,256]{1,0:T(8,128)(2,1)S(1)} %get-tuple-element.13.blocks_ref, bf16[64,384]{1,0:T(8,128)(2,1)S(1)} %get-tuple-element.14.weight_ref), custom_call_target="tpu_custom_call" | custom-call | tf_op jit(solution)/shard_map/last/pallas_call | solution.py:399
  (11 shorter events, 0.0 us)
Async XLA Ops:
  0.0 38.1 %slice-start = ((s8[12582912]{0:T(1024)(128)(4,1)}), s8[4194304]{0:T(1024)(128)(4,1)S(1)}, s32[]{:S(2)}) async-start(s8[12582912]{0:T(1024)(128)(4,1)} %bitcast.12), calls=%async_computation.4 | async-start | bytes 8388608
  0.0 38.1 %slice-start.3 = ((s8[6291456]{0:T(1024)(128)(4,1)}), s8[4194304]{0:T(1024)(128)(4,1)S(1)}, s32[]{:S(2)}) async-start(s8[6291456]{0:T(1024)(128)(4,1)} %bitcast.14), calls=%async_computation.7 | async-start | bytes 8388608
  0.0 38.1 %slice-start.1 = ((s8[12582912]{0:T(1024)(128)(4,1)}), s8[4194304]{0:T(1024)(128)(4,1)S(1)}, s32[]{:S(2)}) async-start(s8[12582912]{0:T(1024)(128)(4,1)} %bitcast.12), calls=%async_computation.5 | async-start | bytes 8388608
  0.0 38.1 %slice-start.2 = ((s8[12582912]{0:T(1024)(128)(4,1)}), s8[4194304]{0:T(1024)(128)(4,1)S(1)}, s32[]{:S(2)}) async-start(s8[12582912]{0:T(1024)(128)(4,1)} %bitcast.12), calls=%async_computation.6 | async-start | bytes 8388608
  0.0 38.1 %slice-start.4 = ((s8[6291456]{0:T(1024)(128)(4,1)}), s8[2097152]{0:T(1024)(128)(4,1)S(1)}, s32[]{:S(2)}) async-start(s8[6291456]{0:T(1024)(128)(4,1)} %bitcast.14), calls=%async_computation.8 | async-start | bytes 4194304
  2.6 35.5 %copy-start.1 = (f32[2,1,16,12]{2,1,3,0:T(1,128)S(1)}, f32[2,1,16,12]{2,1,3,0:T(1,128)}, u32[]{:S(2)}) copy-start(f32[2,1,16,12]{2,1,3,0:T(1,128)} %param.15) | copy-start | bytes 4612
  2.6 35.5 %copy-start.2 = (f32[2,1,6,16]{3,1,2,0:T(1,128)S(1)}, f32[2,1,6,16]{3,1,2,0:T(1,128)}, u32[]{:S(2)}) copy-start(f32[2,1,6,16]{3,1,2,0:T(1,128)} %param.17) | copy-start | bytes 2308
  43.4 28.6 %copy-start = (bf16[32,2048]{1,0:T(8,128)(2,1)S(1)}, bf16[32,2048]{1,0:T(8,128)(2,1)}, u32[]{:S(2)}) copy-start(bf16[32,2048]{1,0:T(8,128)(2,1)} %stream_ref.1) | copy-start | bytes 393220
  43.4 28.6 %copy-start.3 = (f32[2,2048]{1,0:T(2,128)S(1)}, f32[2,2048]{1,0:T(2,128)}, u32[]{:S(2)}) copy-start(f32[2,2048]{1,0:T(2,128)} %gain_ref.1) | copy-start | bytes 49156
  43.4 28.6 %copy-start.4 = (s32[2,32,8]{1,2,0:T(8,128)S(1)}, s32[2,32,8]{1,2,0:T(8,128)}, u32[]{:S(2)}) copy-start(s32[2,32,8]{1,2,0:T(8,128)} %param.11) | copy-start | bytes 6148
  43.5 28.6 %copy-start.5 = (f32[2,32,8]{1,2,0:T(8,128)S(1)}, f32[2,32,8]{1,2,0:T(8,128)}, u32[]{:S(2)}) copy-start(f32[2,32,8]{1,2,0:T(8,128)} %param.12) | copy-start | bytes 6148
  43.5 28.6 %copy-start.6 = (s32[2,128]{1,0:T(2,128)S(1)}, s32[2,128]{1,0:T(2,128)}, u32[]{:S(2)}) copy-start(s32[2,128]{1,0:T(2,128)} %place_ref.1) | copy-start | bytes 3076

commit v10 on v9

--- a/solution.py
+++ b/solution.py
@@ -251,24 +251,15 @@
 
 def expert_kernel(
     layer, in_factors, out_factors, slab_in, w_in, w_out,
-    slab_ref, x_ref, hid, stack_ref, in_scale, out_scale, sems,
+    slab_ref, x_ref, hid, stack_ref,
 ):
-    loads = [
-        pltpu.make_async_copy(in_factors.at[layer : layer + 1], in_scale, sems.at[0]),
-        pltpu.make_async_copy(out_factors.at[layer : layer + 1], out_scale, sems.at[1]),
-    ]
-    for load in loads:
-        load.start()
-
     def into(first, count):
-        return block_weight(w_in, lambda i, j: in_scale[0, j, 0, i], layer, first, count)
+        return block_weight(w_in, lambda i, j: in_factors[layer, j, :, i : i + 1], layer, first, count)
 
     def out_of(first, count):
-        return block_weight(w_out, lambda i, j: out_scale[0, i, 0, j], layer, first, count)
+        return block_weight(w_out, lambda i, j: out_factors[layer, i, :, j : j + 1], layer, first, count)
 
     unfold_rows(slab_in, x_ref)
-    for load in loads:
-        load.wait()
     ff = w_out.shape[2]
     chunk = slab_ref.shape[1]
     for n in range(ff // chunk):
@@ -303,9 +294,6 @@
             pltpu.VMEM((slots, width), jnp.bfloat16),
             pltpu.VMEM((slots, ff), jnp.bfloat16),
             pltpu.VMEM(slab.shape, jnp.bfloat16),
-            pltpu.SMEM((1, *in_scale.shape[1:]), jnp.float32),
-            pltpu.SMEM((1, *out_scale.shape[1:]), jnp.float32),
-            pltpu.SemaphoreType.DMA((2,)),
         ],
         compiler_params=pltpu.CompilerParams(vmem_limit_bytes=20 * MIB),
         cost_estimate=pl.CostEstimate(

time: 137 us -> 137 us (level)
  no operation moved by 1% of the time
where the time goes in v10:
time: 137 us
  blocking collectives  121 us (88%)
  Pallas kernels  15.3 us (11%)
    all_to_all x4, blocking collectives, exchange(): moved = lax.all_to_all(split, AXES, split_axis=0, concat_axis=0, tiled=True)  121 us
    pallas_call x2, Pallas kernels, expert(): pl.pallas_call(functools.partial(expert_kernel, layer), in_specs=[VM] * 5...  9.67 us

profile of v10, /device:TPU:1, one launch (start us, length us, event | category | flops | bytes accessed | tf_op | source)
XLA Modules:
  0.0 136.5 jit_solution(5226856420007803742)
XLA Ops:
  0.0 0.0 slice-start.2
  0.0 0.0 slice-start.4
  0.0 2.6 %first.1 = (bf16[3072,256]{1,0:T(8,128)(2,1)S(1)}, s32[1,8,32]{2,1,0:T(8,128)S(1)}) custom-call(bf16[32,2048]{1,0:T(8,128)(2,1)} %stream_ref.1, f32[2,2048]{1,0:T(2,128)} %gain_ref.1, s32[2,8,32]{2,1,0:T(8,128)} %bitcast.28, s32[2,128]{1,0:T(2,128)} %place_ref.1), custom_call_target="tpu_custom_call" | custom-call | flops 8000000000 | bytes 8000000 | tf_op jit(solution)/shard_map/first/pallas_call | solution.py:338
  2.6 0.0 copy-start.1
  2.6 0.0 copy-start.2
  2.6 35.4 %all_to_all.20 = bf16[128,24,256]{2,1,0:T(8,128)(2,1)S(1)} all-to-all(bf16[128,24,256]{2,1,0:T(8,128)(2,1)S(1)} %bitcast.23), channel_id=1, replica_groups=mesh['dp'=8,'expert'=16] {'dp','expert'}, dimensions={0} | all-to-all | bytes 3145728 | tf_op jit(solution)/shard_map/all_to_all | solution.py:314
  38.1 0.0 slice-done
  38.1 0.0 slice-done.3
  38.1 0.0 slice-done.1
  38.1 0.0 slice-done.2
  38.1 0.0 slice-done.4
  38.2 4.8 %expert.2 = bf16[3072,256]{1,0:T(8,128)(2,1)S(1)} custom-call(f32[2,12,1,16]{3,2,1,0:T(1,128)S(1)} %bitcast.24, f32[2,6,1,16]{3,2,1,0:T(1,128)S(1)} %bitcast.26, bf16[3072,256]{1,0:T(8,128)(2,1)S(1)} %bitcast.18, bf16[2,1,2048,1536]{3,2,1,0:T(8,128)(2,1)S(1)} %bitcast.13, bf16[2,1,768,2048]{3,2,1,0:T(8,128)(2,1)S(1)} %bitcast.15), custom_call_target="tpu_custom_call" | custom-call | flops 3623878656 | bytes 12582912 | tf_op jit(solution)/shard_map/expert/pallas_call | solution.py:288
  43.0 0.0 copy-start
  43.0 0.0 copy-start.3
  43.0 0.0 copy-start.4
  43.0 0.0 copy-start.5
  43.0 0.0 copy-start.6
  43.1 28.6 %all_to_all.21 = bf16[128,24,256]{2,1,0:T(8,128)(2,1)S(1)} all-to-all(bf16[128,24,256]{2,1,0:T(8,128)(2,1)S(1)} %bitcast.19), channel_id=1, replica_groups=mesh['dp'=8,'expert'=16] {'dp','expert'}, dimensions={0} | all-to-all | bytes 3145728 | tf_op jit(solution)/shard_map/all_to_all | solution.py:314
  71.6 0.0 copy-done.3
  71.7 1.5 %middle.1 = (bf16[384,8,256]{2,1,0:T(8,128)(2,1)S(1)}, bf16[256,256]{1,0:T(8,128)(2,1)S(1)}, bf16[64,384]{1,0:T(8,128)(2,1)S(1)}) custom-call(s32[1,8,32]{2,1,0:T(8,128)S(1)} %get-tuple-element.10.slots_in, f32[2,8,32]{2,1,0:T(8,128)S(1)} %bitcast.30, bf16[384,8,256]{2,1,0:T(8,128)(2,1)S(1)} %bitcast.16, bf16[32,2048]{1,0:T(8,128)(2,1)S(1)} %copy-done, ...), custom_call_target="tpu_custom_call" | custom-call | tf_op jit(solution)/shard_map/middle/pallas_call | solution.py:361
  73.1 28.5 %all_to_all.22 = bf16[128,24,256]{2,1,0:T(8,128)(2,1)S(1)} all-to-all(bf16[128,24,256]{2,1,0:T(8,128)(2,1)S(1)} %bitcast.22), channel_id=1, replica_groups=mesh['dp'=8,'expert'=16] {'dp','expert'}, dimensions={0} | all-to-all | bytes 3145728 | tf_op jit(solution)/shard_map/all_to_all | solution.py:314
  101.6 4.8 %expert.3 = bf16[3072,256]{1,0:T(8,128)(2,1)S(1)} custom-call(f32[2,12,1,16]{3,2,1,0:T(1,128)S(1)} %bitcast.25, f32[2,6,1,16]{3,2,1,0:T(1,128)S(1)} %bitcast.27, bf16[3072,256]{1,0:T(8,128)(2,1)S(1)} %bitcast.20, bf16[2,1,2048,1536]{3,2,1,0:T(8,128)(2,1)S(1)} %bitcast.13, bf16[2,1,768,2048]{3,2,1,0:T(8,128)(2,1)S(1)} %bitcast.15), custom_call_target="tpu_custom_call" | custom-call | flops 3623878656 | bytes 12582912 | tf_op jit(solution)/shard_map/expert/pallas_call | solution.py:288
  106.4 28.5 %all_to_all.23 = bf16[128,24,256]{2,1,0:T(8,128)(2,1)S(1)} all-to-all(bf16[128,24,256]{2,1,0:T(8,128)(2,1)S(1)} %bitcast.21), channel_id=1, replica_groups=mesh['dp'=8,'expert'=16] {'dp','expert'}, dimensions={0} | all-to-all | bytes 3145728 | tf_op jit(solution)/shard_map/all_to_all | solution.py:314
  134.9 1.6 %last.1 = bf16[32,2048]{1,0:T(8,128)(2,1)} custom-call(bf16[3072,256]{1,0:T(8,128)(2,1)S(1)} %bitcast.17, bf16[256,256]{1,0:T(8,128)(2,1)S(1)} %get-tuple-element.13.blocks_ref, bf16[64,384]{1,0:T(8,128)(2,1)S(1)} %get-tuple-element.14.weight_ref), custom_call_target="tpu_custom_call" | custom-call | tf_op jit(solution)/shard_map/last/pallas_call | solution.py:387
  (11 shorter events, 0.0 us)
Async XLA Ops:
  0.0 38.1 %slice-start = ((s8[12582912]{0:T(1024)(128)(4,1)}), s8[4194304]{0:T(1024)(128)(4,1)S(1)}, s32[]{:S(2)}) async-start(s8[12582912]{0:T(1024)(128)(4,1)} %bitcast.12), calls=%async_computation.4 | async-start | bytes 8388608
  0.0 38.1 %slice-start.3 = ((s8[6291456]{0:T(1024)(128)(4,1)}), s8[4194304]{0:T(1024)(128)(4,1)S(1)}, s32[]{:S(2)}) async-start(s8[6291456]{0:T(1024)(128)(4,1)} %bitcast.14), calls=%async_computation.7 | async-start | bytes 8388608
  0.0 38.1 %slice-start.1 = ((s8[12582912]{0:T(1024)(128)(4,1)}), s8[4194304]{0:T(1024)(128)(4,1)S(1)}, s32[]{:S(2)}) async-start(s8[12582912]{0:T(1024)(128)(4,1)} %bitcast.12), calls=%async_computation.5 | async-start | bytes 8388608
  0.0 38.1 %slice-start.2 = ((s8[12582912]{0:T(1024)(128)(4,1)}), s8[4194304]{0:T(1024)(128)(4,1)S(1)}, s32[]{:S(2)}) async-start(s8[12582912]{0:T(1024)(128)(4,1)} %bitcast.12), calls=%async_computation.6 | async-start | bytes 8388608
  0.0 38.1 %slice-start.4 = ((s8[6291456]{0:T(1024)(128)(4,1)}), s8[2097152]{0:T(1024)(128)(4,1)S(1)}, s32[]{:S(2)}) async-start(s8[6291456]{0:T(1024)(128)(4,1)} %bitcast.14), calls=%async_computation.8 | async-start | bytes 4194304
  2.6 35.5 %copy-start.1 = (f32[2,1,16,12]{2,1,3,0:T(1,128)S(1)}, f32[2,1,16,12]{2,1,3,0:T(1,128)}, u32[]{:S(2)}) copy-start(f32[2,1,16,12]{2,1,3,0:T(1,128)} %param.15) | copy-start | bytes 4612
  2.6 35.5 %copy-start.2 = (f32[2,1,6,16]{3,1,2,0:T(1,128)S(1)}, f32[2,1,6,16]{3,1,2,0:T(1,128)}, u32[]{:S(2)}) copy-start(f32[2,1,6,16]{3,1,2,0:T(1,128)} %param.17) | copy-start | bytes 2308
  43.0 28.6 %copy-start = (bf16[32,2048]{1,0:T(8,128)(2,1)S(1)}, bf16[32,2048]{1,0:T(8,128)(2,1)}, u32[]{:S(2)}) copy-start(bf16[32,2048]{1,0:T(8,128)(2,1)} %stream_ref.1) | copy-start | bytes 393220
  43.0 28.6 %copy-start.3 = (f32[2,2048]{1,0:T(2,128)S(1)}, f32[2,2048]{1,0:T(2,128)}, u32[]{:S(2)}) copy-start(f32[2,2048]{1,0:T(2,128)} %gain_ref.1) | copy-start | bytes 49156
  43.0 28.6 %copy-start.4 = (s32[2,32,8]{1,2,0:T(8,128)S(1)}, s32[2,32,8]{1,2,0:T(8,128)}, u32[]{:S(2)}) copy-start(s32[2,32,8]{1,2,0:T(8,128)} %param.11) | copy-start | bytes 6148
  43.0 28.6 %copy-start.5 = (f32[2,32,8]{1,2,0:T(8,128)S(1)}, f32[2,32,8]{1,2,0:T(8,128)}, u32[]{:S(2)}) copy-start(f32[2,32,8]{1,2,0:T(8,128)} %param.12) | copy-start | bytes 6148
  43.0 28.6 %copy-start.6 = (s32[2,128]{1,0:T(2,128)S(1)}, s32[2,128]{1,0:T(2,128)}, u32[]{:S(2)}) copy-start(s32[2,128]{1,0:T(2,128)} %place_ref.1) | copy-start | bytes 3076

commit v11 on v10

--- a/solution.py
+++ b/solution.py
@@ -224,13 +224,27 @@
             slab_ref[slots_ref[1, k, t]] = row
 
 
-def last_kernel(slab_in, blocks_ref, weight_ref, out_ref, rows_ref, stream_ref):
+def last_kernel(
+    slab_in, blocks_ref, weight_ref, out_hbm, rows_ref, stream_ref, out_ref, sems
+):
     unfold_rows(blocks_ref, stream_ref)
     unfold_rows(slab_in, rows_ref)
-    both = jnp.dot(weight_ref[...], rows_ref[...], preferred_element_type=jnp.float32)
     tokens = weight_ref.shape[0] // 2
-    mixed = both[:tokens] + both[tokens:]
-    out_ref[...] = (stream_ref[...].astype(jnp.float32) + mixed).astype(jnp.bfloat16)
+    span = out_ref.shape[1] // sems.shape[0]
+    stores = []
+    for i in range(sems.shape[0]):
+        cols = slice(i * span, (i + 1) * span)
+        both = jnp.dot(weight_ref[...], rows_ref[:, cols], preferred_element_type=jnp.float32)
+        mixed = both[:tokens] + both[tokens:]
+        out_ref[:, cols] = (stream_ref[:, cols].astype(jnp.float32) + mixed).astype(
+            jnp.bfloat16
+        )
+        at = pl.ds(i * span, span)
+        store = pltpu.make_async_copy(out_ref.at[:, at], out_hbm.at[:, at], sems.at[i])
+        store.start()
+        stores.append(store)
+    for store in stores:
+        store.wait()
 
 
 def block_weight(w_ref, factor, layer, first, count):
@@ -387,11 +401,13 @@
             stream = pl.pallas_call(
                 last_kernel,
                 in_specs=[VM] * 3,
-                out_specs=VM,
-                out_shape=stream_type,
+                out_specs=HB,
+                out_shape=pltpu.HBM((count, width), jnp.bfloat16),
                 scratch_shapes=[
                     pltpu.VMEM((slots, width), jnp.bfloat16),
                     pltpu.VMEM((count, width), jnp.bfloat16),
+                    pltpu.VMEM((count, width), jnp.bfloat16),
+                    pltpu.SemaphoreType.DMA((4,)),
                 ],
                 compiler_params=params,
                 name="last",

time: 137 us -> 137 us (level)
  no operation moved by 1% of the time
where the time goes in v11:
time: 137 us
  blocking collectives  121 us (88%)
  Pallas kernels  15.3 us (11%)
    all_to_all x4, blocking collectives, exchange(): moved = lax.all_to_all(split, AXES, split_axis=0, concat_axis=0, tiled=True)  121 us
    pallas_call x2, Pallas kernels, expert(): pl.pallas_call(functools.partial(expert_kernel, layer), in_specs=[VM] * 5...  9.67 us

profile of v11, /device:TPU:1, one launch (start us, length us, event | category | flops | bytes accessed | tf_op | source)
XLA Modules:
  0.0 136.7 jit_solution(15683291935913258903)
XLA Ops:
  0.0 0.0 slice-start.2
  0.0 0.0 slice-start.4
  0.0 2.6 %first.1 = (bf16[3072,256]{1,0:T(8,128)(2,1)S(1)}, s32[1,8,32]{2,1,0:T(8,128)S(1)}) custom-call(bf16[32,2048]{1,0:T(8,128)(2,1)} %stream_ref.1, f32[2,2048]{1,0:T(2,128)} %gain_ref.1, s32[2,8,32]{2,1,0:T(8,128)} %bitcast.28, s32[2,128]{1,0:T(2,128)} %place_ref.1), custom_call_target="tpu_custom_call" | custom-call | flops 8000000000 | bytes 8000000 | tf_op jit(solution)/shard_map/first/pallas_call | solution.py:352
  2.6 0.0 copy-start.1
  2.6 0.0 copy-start.2
  2.6 35.4 %all_to_all.20 = bf16[128,24,256]{2,1,0:T(8,128)(2,1)S(1)} all-to-all(bf16[128,24,256]{2,1,0:T(8,128)(2,1)S(1)} %bitcast.23), channel_id=1, replica_groups=mesh['dp'=8,'expert'=16] {'dp','expert'}, dimensions={0} | all-to-all | bytes 3145728 | tf_op jit(solution)/shard_map/all_to_all | solution.py:328
  38.1 0.0 slice-done.1
  38.1 0.0 slice-done.2
  38.1 0.0 slice-done.4
  38.1 0.0 copy-done.1
  38.1 0.0 copy-done.2
  38.2 4.8 %expert.2 = bf16[3072,256]{1,0:T(8,128)(2,1)S(1)} custom-call(f32[2,12,1,16]{3,2,1,0:T(1,128)S(1)} %bitcast.24, f32[2,6,1,16]{3,2,1,0:T(1,128)S(1)} %bitcast.26, bf16[3072,256]{1,0:T(8,128)(2,1)S(1)} %bitcast.18, bf16[2,1,2048,1536]{3,2,1,0:T(8,128)(2,1)S(1)} %bitcast.13, bf16[2,1,768,2048]{3,2,1,0:T(8,128)(2,1)S(1)} %bitcast.15), custom_call_target="tpu_custom_call" | custom-call | flops 3623878656 | bytes 12582912 | tf_op jit(solution)/shard_map/expert/pallas_call | solution.py:302
  43.0 0.0 copy-start
  43.0 0.0 copy-start.3
  43.0 0.0 copy-start.4
  43.0 0.0 copy-start.5
  43.0 0.0 copy-start.6
  43.1 28.6 %all_to_all.21 = bf16[128,24,256]{2,1,0:T(8,128)(2,1)S(1)} all-to-all(bf16[128,24,256]{2,1,0:T(8,128)(2,1)S(1)} %bitcast.19), channel_id=1, replica_groups=mesh['dp'=8,'expert'=16] {'dp','expert'}, dimensions={0} | all-to-all | bytes 3145728 | tf_op jit(solution)/shard_map/all_to_all | solution.py:328
  71.6 0.0 copy-done.4
  71.7 1.5 %middle.1 = (bf16[384,8,256]{2,1,0:T(8,128)(2,1)S(1)}, bf16[256,256]{1,0:T(8,128)(2,1)S(1)}, bf16[64,384]{1,0:T(8,128)(2,1)S(1)}) custom-call(s32[1,8,32]{2,1,0:T(8,128)S(1)} %get-tuple-element.10.slots_in, f32[2,8,32]{2,1,0:T(8,128)S(1)} %bitcast.30, bf16[384,8,256]{2,1,0:T(8,128)(2,1)S(1)} %bitcast.16, bf16[32,2048]{1,0:T(8,128)(2,1)S(1)} %copy-done, ...), custom_call_target="tpu_custom_call" | custom-call | tf_op jit(solution)/shard_map/middle/pallas_call | solution.py:375
  73.1 28.5 %all_to_all.22 = bf16[128,24,256]{2,1,0:T(8,128)(2,1)S(1)} all-to-all(bf16[128,24,256]{2,1,0:T(8,128)(2,1)S(1)} %bitcast.22), channel_id=1, replica_groups=mesh['dp'=8,'expert'=16] {'dp','expert'}, dimensions={0} | all-to-all | bytes 3145728 | tf_op jit(solution)/shard_map/all_to_all | solution.py:328
  101.6 4.8 %expert.3 = bf16[3072,256]{1,0:T(8,128)(2,1)S(1)} custom-call(f32[2,12,1,16]{3,2,1,0:T(1,128)S(1)} %bitcast.25, f32[2,6,1,16]{3,2,1,0:T(1,128)S(1)} %bitcast.27, bf16[3072,256]{1,0:T(8,128)(2,1)S(1)} %bitcast.20, bf16[2,1,2048,1536]{3,2,1,0:T(8,128)(2,1)S(1)} %bitcast.13, bf16[2,1,768,2048]{3,2,1,0:T(8,128)(2,1)S(1)} %bitcast.15), custom_call_target="tpu_custom_call" | custom-call | flops 3623878656 | bytes 12582912 | tf_op jit(solution)/shard_map/expert/pallas_call | solution.py:302
  106.4 28.5 %all_to_all.23 = bf16[128,24,256]{2,1,0:T(8,128)(2,1)S(1)} all-to-all(bf16[128,24,256]{2,1,0:T(8,128)(2,1)S(1)} %bitcast.21), channel_id=1, replica_groups=mesh['dp'=8,'expert'=16] {'dp','expert'}, dimensions={0} | all-to-all | bytes 3145728 | tf_op jit(solution)/shard_map/all_to_all | solution.py:328
  134.9 1.6 %last.1 = bf16[32,2048]{1,0:T(8,128)(2,1)} custom-call(bf16[3072,256]{1,0:T(8,128)(2,1)S(1)} %bitcast.17, bf16[256,256]{1,0:T(8,128)(2,1)S(1)} %get-tuple-element.13.blocks_ref, bf16[64,384]{1,0:T(8,128)(2,1)S(1)} %get-tuple-element.14.weight_ref), custom_call_target="tpu_custom_call" | custom-call | tf_op jit(solution)/shard_map/last/pallas_call | solution.py:401
  (11 shorter events, 0.0 us)
Async XLA Ops:
  0.0 38.1 %slice-start = ((s8[12582912]{0:T(1024)(128)(4,1)}), s8[4194304]{0:T(1024)(128)(4,1)S(1)}, s32[]{:S(2)}) async-start(s8[12582912]{0:T(1024)(128)(4,1)} %bitcast.12), calls=%async_computation.4 | async-start | bytes 8388608
  0.0 38.1 %slice-start.3 = ((s8[6291456]{0:T(1024)(128)(4,1)}), s8[4194304]{0:T(1024)(128)(4,1)S(1)}, s32[]{:S(2)}) async-start(s8[6291456]{0:T(1024)(128)(4,1)} %bitcast.14), calls=%async_computation.7 | async-start | bytes 8388608
  0.0 38.1 %slice-start.1 = ((s8[12582912]{0:T(1024)(128)(4,1)}), s8[4194304]{0:T(1024)(128)(4,1)S(1)}, s32[]{:S(2)}) async-start(s8[12582912]{0:T(1024)(128)(4,1)} %bitcast.12), calls=%async_computation.5 | async-start | bytes 8388608
  0.0 38.1 %slice-start.2 = ((s8[12582912]{0:T(1024)(128)(4,1)}), s8[4194304]{0:T(1024)(128)(4,1)S(1)}, s32[]{:S(2)}) async-start(s8[12582912]{0:T(1024)(128)(4,1)} %bitcast.12), calls=%async_computation.6 | async-start | bytes 8388608
  0.0 38.1 %slice-start.4 = ((s8[6291456]{0:T(1024)(128)(4,1)}), s8[2097152]{0:T(1024)(128)(4,1)S(1)}, s32[]{:S(2)}) async-start(s8[6291456]{0:T(1024)(128)(4,1)} %bitcast.14), calls=%async_computation.8 | async-start | bytes 4194304
  2.6 35.5 %copy-start.1 = (f32[2,1,16,12]{2,1,3,0:T(1,128)S(1)}, f32[2,1,16,12]{2,1,3,0:T(1,128)}, u32[]{:S(2)}) copy-start(f32[2,1,16,12]{2,1,3,0:T(1,128)} %param.15) | copy-start | bytes 4612
  2.6 35.5 %copy-start.2 = (f32[2,1,6,16]{3,1,2,0:T(1,128)S(1)}, f32[2,1,6,16]{3,1,2,0:T(1,128)}, u32[]{:S(2)}) copy-start(f32[2,1,6,16]{3,1,2,0:T(1,128)} %param.17) | copy-start | bytes 2308
  43.0 28.6 %copy-start = (bf16[32,2048]{1,0:T(8,128)(2,1)S(1)}, bf16[32,2048]{1,0:T(8,128)(2,1)}, u32[]{:S(2)}) copy-start(bf16[32,2048]{1,0:T(8,128)(2,1)} %stream_ref.1) | copy-start | bytes 393220
  43.0 28.6 %copy-start.3 = (f32[2,2048]{1,0:T(2,128)S(1)}, f32[2,2048]{1,0:T(2,128)}, u32[]{:S(2)}) copy-start(f32[2,2048]{1,0:T(2,128)} %gain_ref.1) | copy-start | bytes 49156
  43.0 28.6 %copy-start.4 = (s32[2,32,8]{1,2,0:T(8,128)S(1)}, s32[2,32,8]{1,2,0:T(8,128)}, u32[]{:S(2)}) copy-start(s32[2,32,8]{1,2,0:T(8,128)} %param.11) | copy-start | bytes 6148
  43.0 28.6 %copy-start.5 = (f32[2,32,8]{1,2,0:T(8,128)S(1)}, f32[2,32,8]{1,2,0:T(8,128)}, u32[]{:S(2)}) copy-start(f32[2,32,8]{1,2,0:T(8,128)} %param.12) | copy-start | bytes 6148
  43.0 28.6 %copy-start.6 = (s32[2,128]{1,0:T(2,128)S(1)}, s32[2,128]{1,0:T(2,128)}, u32[]{:S(2)}) copy-start(s32[2,128]{1,0:T(2,128)} %place_ref.1) | copy-start | bytes 3076

commit v12 on v10

--- a/solution.py
+++ b/solution.py
@@ -145,7 +145,7 @@
 
 
 def first_kernel(
-    tokens_hbm, gain_hbm, routes_hbm, place_hbm, slab_ref, slots_ref,
+    tokens_hbm, gain_hbm, routes_hbm, place_hbm, slab_ref,
     tokens_ref, gain_ref, routes_ref, place_ref, stack_ref, sems,
 ):
     loads = [
@@ -165,7 +165,6 @@
     loads[1].wait()
     select, _ = slot_tables(routes_ref[0], place_ref[0:1, :], None)
     pick = jnp.transpose(select).astype(jnp.bfloat16)
-    slots_ref[0] = slot_numbers(routes_ref[0], place_ref[0:1, :])
     loads[2].wait()
     loads[3].wait()
     normed = normalise(tokens_ref[...].astype(jnp.float32), gain_ref[0:1, :])
@@ -250,8 +249,8 @@
 
 
 def expert_kernel(
-    layer, in_factors, out_factors, slab_in, w_in, w_out,
-    slab_ref, x_ref, hid, stack_ref,
+    layer, in_factors, out_factors, slab_in, w_in, w_out, routes_ref, place_ref,
+    slab_ref, slots_ref, x_ref, hid, stack_ref,
 ):
     def into(first, count):
         return block_weight(w_in, lambda i, j: in_factors[layer, j, :, i : i + 1], layer, first, count)
@@ -259,6 +258,10 @@
     def out_of(first, count):
         return block_weight(w_out, lambda i, j: out_factors[layer, i, :, j : j + 1], layer, first, count)
 
+    if layer + 1 < routes_ref.shape[0]:
+        slots_ref[0] = slot_numbers(routes_ref[layer], place_ref[layer : layer + 1, :])
+    else:
+        slots_ref[...] = jnp.zeros(slots_ref.shape, jnp.int32)
     unfold_rows(slab_in, x_ref)
     ff = w_out.shape[2]
     chunk = slab_ref.shape[1]
@@ -280,16 +283,19 @@
 HB = pl.BlockSpec(memory_space=pltpu.HBM)
 
 
-def expert(layer, slab, weights):
+def expert(layer, slab, weights, routes_t, place):
     w_in, in_scale, w_out, out_scale = weights
     rows, piece = slab.shape
     slots = rows // PIECES
     width, ff = w_in.shape[2], w_out.shape[2]
     return pl.pallas_call(
         functools.partial(expert_kernel, layer),
-        in_specs=[VM] * 5,
-        out_specs=VM,
-        out_shape=jax.ShapeDtypeStruct(slab.shape, jnp.bfloat16),
+        in_specs=[VM] * 7,
+        out_specs=(VM, VM),
+        out_shape=(
+            jax.ShapeDtypeStruct(slab.shape, jnp.bfloat16),
+            jax.ShapeDtypeStruct((1, *routes_t.shape[1:]), jnp.int32),
+        ),
         scratch_shapes=[
             pltpu.VMEM((slots, width), jnp.bfloat16),
             pltpu.VMEM((slots, ff), jnp.bfloat16),
@@ -302,7 +308,7 @@
             transcendentals=slots * ff,
         ),
         name="expert",
-    )(in_scale, out_scale, slab, w_in, w_out)
+    )(in_scale, out_scale, slab, w_in, w_out, routes_t, place)
 
 
 def hbm(array):
@@ -323,7 +329,6 @@
     routes_t = jnp.swapaxes(routes, 1, 2)
     gates_t = jnp.swapaxes(gates, 1, 2)
     slab_type = jax.ShapeDtypeStruct((slots * PIECES, piece), jnp.bfloat16)
-    slots_type = jax.ShapeDtypeStruct((1, *routes_t.shape[1:]), jnp.int32)
     stream_type = jax.ShapeDtypeStruct((count, width), jnp.bfloat16)
     mixed = pltpu.VMEM((count, PIECES, piece), jnp.float32)
     stack = pltpu.VMEM((slots * PIECES, piece), jnp.bfloat16)
@@ -335,11 +340,11 @@
         pltpu.VMEM(routes_t.shape, jnp.int32),
         pltpu.VMEM(placement.shape, jnp.int32),
     )
-    slab, numbers = pl.pallas_call(
+    slab = pl.pallas_call(
         first_kernel,
         in_specs=[HB] * 4,
-        out_specs=(VM, VM),
-        out_shape=(slab_type, slots_type),
+        out_specs=VM,
+        out_shape=slab_type,
         scratch_shapes=[*small, stack, pltpu.SemaphoreType.DMA((4,))],
         compiler_params=params,
         cost_estimate=pl.CostEstimate(
@@ -355,7 +360,9 @@
     )
     stream = tokens
     for layer in range(layers):
-        answers = expert(layer, exchange(slab, devices), weights)
+        answers, numbers = expert(
+            layer, exchange(slab, devices), weights, routes_t, placement
+        )
         back = exchange(answers, devices)
         if layer + 1 < layers:
             slab, stream, weight = pl.pallas_call(

time: 137 us -> 137 us (level)
  no operation moved by 1% of the time
where the time goes in v12:
time: 137 us
  blocking collectives  121 us (88%)
  Pallas kernels  15.8 us (12%)
    all_to_all x4, blocking collectives, exchange(): moved = lax.all_to_all(split, AXES, split_axis=0, concat_axis=0, tiled=True)  121 us
    pallas_call x2, Pallas kernels, expert(): pl.pallas_call(functools.partial(expert_kernel, layer), in_specs=[VM] * 7...  10.3 us

profile of v12, /device:TPU:1, one launch (start us, length us, event | category | flops | bytes accessed | tf_op | source)
XLA Modules:
  0.0 137.0 jit_solution(16901304812362238004)
XLA Ops:
  0.0 0.0 slice-start.2
  0.0 0.0 slice-start.4
  0.0 2.4 %first.1 = bf16[3072,256]{1,0:T(8,128)(2,1)S(1)} custom-call(bf16[32,2048]{1,0:T(8,128)(2,1)} %stream_ref.1, f32[2,2048]{1,0:T(2,128)} %gain_ref.1, s32[2,8,32]{2,1,0:T(8,128)} %bitcast.24, s32[2,128]{1,0:T(2,128)} %place_ref.5), custom_call_target="tpu_custom_call" | custom-call | flops 8000000000 | bytes 8000000 | tf_op jit(solution)/shard_map/first/pallas_call | solution.py:343
  2.5 0.0 copy-start.1
  2.5 0.0 copy-start.2
  2.5 0.0 copy-start.3
  2.5 0.0 copy-start.5
  2.5 35.4 %all_to_all.20 = bf16[128,24,256]{2,1,0:T(8,128)(2,1)S(1)} all-to-all(bf16[128,24,256]{2,1,0:T(8,128)(2,1)S(1)} %bitcast.23), channel_id=1, replica_groups=mesh['dp'=8,'expert'=16] {'dp','expert'}, dimensions={0} | all-to-all | bytes 3145728 | tf_op jit(solution)/shard_map/all_to_all | solution.py:320
  38.0 0.0 slice-done
  38.0 0.0 slice-done.3
  38.0 0.0 slice-done.1
  38.0 0.0 slice-done.2
  38.0 0.0 slice-done.4
  38.0 0.0 copy-done.1
  38.1 5.0 %expert.2 = (bf16[3072,256]{1,0:T(8,128)(2,1)S(1)}, s32[1,8,32]{2,1,0:T(8,128)S(1)}) custom-call(f32[2,12,1,16]{3,2,1,0:T(1,128)S(1)} %bitcast.28, f32[2,6,1,16]{3,2,1,0:T(1,128)S(1)} %bitcast.30, bf16[3072,256]{1,0:T(8,128)(2,1)S(1)} %bitcast.18, bf16[2,1,2048,1536]{3,2,1,0:T(8,128)(2,1)S(1)} %bitcast.13, bf16[2,1,768,2048]{3,2,1,0:T(8,128)(2,1)S(1)} %bitcast.15, ...), custom_call_target="tpu_custom_call" | custom-call | flops 3623878656 | bytes 12582912 | tf_op jit(solution)/shard_map/expert/pallas_call | solution.py:291
  43.0 0.0 copy-start
  43.0 0.0 copy-start.4
  43.1 0.0 copy-start.6
  43.1 28.6 %all_to_all.21 = bf16[128,24,256]{2,1,0:T(8,128)(2,1)S(1)} all-to-all(bf16[128,24,256]{2,1,0:T(8,128)(2,1)S(1)} %bitcast.21), channel_id=1, replica_groups=mesh['dp'=8,'expert'=16] {'dp','expert'}, dimensions={0} | all-to-all | bytes 3145728 | tf_op jit(solution)/shard_map/all_to_all | solution.py:320
  71.6 1.5 %middle.1 = (bf16[384,8,256]{2,1,0:T(8,128)(2,1)S(1)}, bf16[256,256]{1,0:T(8,128)(2,1)S(1)}, bf16[64,384]{1,0:T(8,128)(2,1)S(1)}) custom-call(s32[1,8,32]{2,1,0:T(8,128)S(1)} %get-tuple-element.11.slots_in, f32[2,8,32]{2,1,0:T(8,128)S(1)} %bitcast.32, bf16[384,8,256]{2,1,0:T(8,128)(2,1)S(1)} %bitcast.16, bf16[32,2048]{1,0:T(8,128)(2,1)S(1)} %copy-done, ...), custom_call_target="tpu_custom_call" | custom-call | tf_op jit(solution)/shard_map/middle/pallas_call | solution.py:368
  73.1 28.5 %all_to_all.22 = bf16[128,24,256]{2,1,0:T(8,128)(2,1)S(1)} all-to-all(bf16[128,24,256]{2,1,0:T(8,128)(2,1)S(1)} %bitcast.20), channel_id=1, replica_groups=mesh['dp'=8,'expert'=16] {'dp','expert'}, dimensions={0} | all-to-all | bytes 3145728 | tf_op jit(solution)/shard_map/all_to_all | solution.py:320
  101.6 5.3 %expert.3 = (bf16[3072,256]{1,0:T(8,128)(2,1)S(1)}, s32[1,8,32]{2,1,0:T(8,128)}) custom-call(f32[2,12,1,16]{3,2,1,0:T(1,128)S(1)} %bitcast.29, f32[2,6,1,16]{3,2,1,0:T(1,128)S(1)} %bitcast.31, bf16[3072,256]{1,0:T(8,128)(2,1)S(1)} %bitcast.19, bf16[2,1,2048,1536]{3,2,1,0:T(8,128)(2,1)S(1)} %bitcast.13, bf16[2,1,768,2048]{3,2,1,0:T(8,128)(2,1)S(1)} %bitcast.15, ...), custom_call_target="tpu_custom_call" | custom-call | flops 3623878656 | bytes 12582912 | tf_op jit(solution)/shard_map/expert/pallas_call | solution.py:291
  106.9 28.4 %all_to_all.23 = bf16[128,24,256]{2,1,0:T(8,128)(2,1)S(1)} all-to-all(bf16[128,24,256]{2,1,0:T(8,128)(2,1)S(1)} %bitcast.22), channel_id=1, replica_groups=mesh['dp'=8,'expert'=16] {'dp','expert'}, dimensions={0} | all-to-all | bytes 3145728 | tf_op jit(solution)/shard_map/all_to_all | solution.py:320
  135.4 1.6 %last.1 = bf16[32,2048]{1,0:T(8,128)(2,1)} custom-call(bf16[3072,256]{1,0:T(8,128)(2,1)S(1)} %bitcast.17, bf16[256,256]{1,0:T(8,128)(2,1)S(1)} %get-tuple-element.15.blocks_ref, bf16[64,384]{1,0:T(8,128)(2,1)S(1)} %get-tuple-element.16.weight_ref), custom_call_target="tpu_custom_call" | custom-call | tf_op jit(solution)/shard_map/last/pallas_call | solution.py:394
  (11 shorter events, 0.0 us)
Async XLA Ops:
  0.0 38.0 %slice-start = ((s8[12582912]{0:T(1024)(128)(4,1)}), s8[4194304]{0:T(1024)(128)(4,1)S(1)}, s32[]{:S(2)}) async-start(s8[12582912]{0:T(1024)(128)(4,1)} %bitcast.12), calls=%async_computation.4 | async-start | bytes 8388608
  0.0 38.0 %slice-start.3 = ((s8[6291456]{0:T(1024)(128)(4,1)}), s8[4194304]{0:T(1024)(128)(4,1)S(1)}, s32[]{:S(2)}) async-start(s8[6291456]{0:T(1024)(128)(4,1)} %bitcast.14), calls=%async_computation.7 | async-start | bytes 8388608
  0.0 38.0 %slice-start.1 = ((s8[12582912]{0:T(1024)(128)(4,1)}), s8[4194304]{0:T(1024)(128)(4,1)S(1)}, s32[]{:S(2)}) async-start(s8[12582912]{0:T(1024)(128)(4,1)} %bitcast.12), calls=%async_computation.5 | async-start | bytes 8388608
  0.0 38.0 %slice-start.2 = ((s8[12582912]{0:T(1024)(128)(4,1)}), s8[4194304]{0:T(1024)(128)(4,1)S(1)}, s32[]{:S(2)}) async-start(s8[12582912]{0:T(1024)(128)(4,1)} %bitcast.12), calls=%async_computation.6 | async-start | bytes 8388608
  0.0 38.0 %slice-start.4 = ((s8[6291456]{0:T(1024)(128)(4,1)}), s8[2097152]{0:T(1024)(128)(4,1)S(1)}, s32[]{:S(2)}) async-start(s8[6291456]{0:T(1024)(128)(4,1)} %bitcast.14), calls=%async_computation.8 | async-start | bytes 4194304
  2.5 35.5 %copy-start.1 = (s32[2,32,8]{1,2,0:T(8,128)S(1)}, s32[2,32,8]{1,2,0:T(8,128)}, u32[]{:S(2)}) copy-start(s32[2,32,8]{1,2,0:T(8,128)} %param.11) | copy-start | bytes 6148
  2.5 35.5 %copy-start.2 = (f32[2,1,16,12]{2,1,3,0:T(1,128)S(1)}, f32[2,1,16,12]{2,1,3,0:T(1,128)}, u32[]{:S(2)}) copy-start(f32[2,1,16,12]{2,1,3,0:T(1,128)} %param.15) | copy-start | bytes 4612
  2.5 35.5 %copy-start.3 = (f32[2,1,6,16]{3,1,2,0:T(1,128)S(1)}, f32[2,1,6,16]{3,1,2,0:T(1,128)}, u32[]{:S(2)}) copy-start(f32[2,1,6,16]{3,1,2,0:T(1,128)} %param.17) | copy-start | bytes 2308
  2.5 35.5 %copy-start.5 = (s32[2,128]{1,0:T(2,128)S(1)}, s32[2,128]{1,0:T(2,128)}, u32[]{:S(2)}) copy-start(s32[2,128]{1,0:T(2,128)} %place_ref.5) | copy-start | bytes 3076
  43.0 28.6 %copy-start = (bf16[32,2048]{1,0:T(8,128)(2,1)S(1)}, bf16[32,2048]{1,0:T(8,128)(2,1)}, u32[]{:S(2)}) copy-start(bf16[32,2048]{1,0:T(8,128)(2,1)} %stream_ref.1) | copy-start | bytes 393220
  43.0 28.6 %copy-start.4 = (f32[2,2048]{1,0:T(2,128)S(1)}, f32[2,2048]{1,0:T(2,128)}, u32[]{:S(2)}) copy-start(f32[2,2048]{1,0:T(2,128)} %gain_ref.1) | copy-start | bytes 49156
  43.1 28.6 %copy-start.6 = (f32[2,32,8]{1,2,0:T(8,128)S(1)}, f32[2,32,8]{1,2,0:T(8,128)}, u32[]{:S(2)}) copy-start(f32[2,32,8]{1,2,0:T(8,128)} %param.12) | copy-start | bytes 6148

commit v13 on v12

--- a/solution.py
+++ b/solution.py
@@ -250,7 +250,7 @@
 
 def expert_kernel(
     layer, in_factors, out_factors, slab_in, w_in, w_out, routes_ref, place_ref,
-    slab_ref, slots_ref, x_ref, hid, stack_ref,
+    slab_ref, *rest,
 ):
     def into(first, count):
         return block_weight(w_in, lambda i, j: in_factors[layer, j, :, i : i + 1], layer, first, count)
@@ -258,10 +258,9 @@
     def out_of(first, count):
         return block_weight(w_out, lambda i, j: out_factors[layer, i, :, j : j + 1], layer, first, count)
 
-    if layer + 1 < routes_ref.shape[0]:
-        slots_ref[0] = slot_numbers(routes_ref[layer], place_ref[layer : layer + 1, :])
-    else:
-        slots_ref[...] = jnp.zeros(slots_ref.shape, jnp.int32)
+    x_ref, hid, stack_ref = rest[-3:]
+    if len(rest) > 3:
+        rest[0][0] = slot_numbers(routes_ref[layer], place_ref[layer : layer + 1, :])
     unfold_rows(slab_in, x_ref)
     ff = w_out.shape[2]
     chunk = slab_ref.shape[1]
@@ -288,14 +287,14 @@
     rows, piece = slab.shape
     slots = rows // PIECES
     width, ff = w_in.shape[2], w_out.shape[2]
+    outs = [jax.ShapeDtypeStruct(slab.shape, jnp.bfloat16)]
+    if layer + 1 < routes_t.shape[0]:
+        outs.append(jax.ShapeDtypeStruct((1, *routes_t.shape[1:]), jnp.int32))
     return pl.pallas_call(
         functools.partial(expert_kernel, layer),
         in_specs=[VM] * 7,
-        out_specs=(VM, VM),
-        out_shape=(
-            jax.ShapeDtypeStruct(slab.shape, jnp.bfloat16),
-            jax.ShapeDtypeStruct((1, *routes_t.shape[1:]), jnp.int32),
-        ),
+        out_specs=[VM] * len(outs),
+        out_shape=outs,
         scratch_shapes=[
             pltpu.VMEM((slots, width), jnp.bfloat16),
             pltpu.VMEM((slots, ff), jnp.bfloat16),
@@ -360,7 +359,7 @@
     )
     stream = tokens
     for layer in range(layers):
-        answers, numbers = expert(
+        answers, *numbers = expert(
             layer, exchange(slab, devices), weights, routes_t, placement
         )
         back = exchange(answers, devices)
@@ -378,15 +377,15 @@
                     mixed,
                     pltpu.VMEM((PIECES, piece), jnp.float32),
                     pltpu.VMEM((count * PIECES, piece), jnp.bfloat16),
-                    pltpu.VMEM(numbers.shape, jnp.int32),
-                    pltpu.SMEM((2, *numbers.shape[1:]), jnp.int32),
+                    pltpu.VMEM(numbers[0].shape, jnp.int32),
+                    pltpu.SMEM((2, *numbers[0].shape[1:]), jnp.int32),
                     pltpu.SMEM((1, *gates_t.shape[1:]), jnp.float32),
                     pltpu.SemaphoreType.DMA((3,)),
                 ],
                 compiler_params=params,
                 name="middle",
             )(
-                numbers, gates_t, back.reshape(slots, PIECES, piece), stream, norm_gain,
+                numbers[0], gates_t, back.reshape(slots, PIECES, piece), stream, norm_gain,
                 routes_t, placement,
             )
             slab = slab.reshape(slots * PIECES, piece)

time: 137 us -> 137 us (level)
  no operation moved by 1% of the time
where the time goes in v13:
time: 137 us; the launch traced here: 136 us
  blocking collectives  121 us (88%)
  Pallas kernels  15.3 us (11%)
    all_to_all x4, blocking collectives, exchange(): moved = lax.all_to_all(split, AXES, split_axis=0, concat_axis=0, tiled=True)  121 us
    pallas_call x2, Pallas kernels, expert(): pl.pallas_call(functools.partial(expert_kernel, layer), in_specs=[VM] * 7...  9.78 us

profile of v13, /device:TPU:1, one launch (start us, length us, event | category | flops | bytes accessed | tf_op | source)
XLA Modules:
  0.0 136.5 jit_solution(14921840574106387123)
XLA Ops:
  0.0 0.0 slice-start.2
  0.0 0.0 slice-start.4
  0.0 2.4 %first.1 = bf16[3072,256]{1,0:T(8,128)(2,1)S(1)} custom-call(bf16[32,2048]{1,0:T(8,128)(2,1)} %stream_ref.1, f32[2,2048]{1,0:T(2,128)} %gain_ref.1, s32[2,8,32]{2,1,0:T(8,128)} %bitcast.24, s32[2,128]{1,0:T(2,128)} %place_ref.5), custom_call_target="tpu_custom_call" | custom-call | flops 8000000000 | bytes 8000000 | tf_op jit(solution)/shard_map/first/pallas_call | solution.py:342
  2.5 0.0 copy-start.1
  2.5 0.0 copy-start.2
  2.5 0.0 copy-start.3
  2.5 0.0 copy-start.5
  2.5 35.4 %all_to_all.20 = bf16[128,24,256]{2,1,0:T(8,128)(2,1)S(1)} all-to-all(bf16[128,24,256]{2,1,0:T(8,128)(2,1)S(1)} %bitcast.23), channel_id=1, replica_groups=mesh['dp'=8,'expert'=16] {'dp','expert'}, dimensions={0} | all-to-all | bytes 3145728 | tf_op jit(solution)/shard_map/all_to_all | solution.py:319
  38.0 0.0 slice-done.1
  38.0 0.0 slice-done.2
  38.0 0.0 slice-done.4
  38.0 0.0 copy-done.1
  38.0 0.0 copy-done.2
  38.0 0.0 copy-done.3
  38.1 5.0 %expert.2 = (bf16[3072,256]{1,0:T(8,128)(2,1)S(1)}, s32[1,8,32]{2,1,0:T(8,128)S(1)}) custom-call(f32[2,12,1,16]{3,2,1,0:T(1,128)S(1)} %bitcast.28, f32[2,6,1,16]{3,2,1,0:T(1,128)S(1)} %bitcast.30, bf16[3072,256]{1,0:T(8,128)(2,1)S(1)} %bitcast.18, bf16[2,1,2048,1536]{3,2,1,0:T(8,128)(2,1)S(1)} %bitcast.13, bf16[2,1,768,2048]{3,2,1,0:T(8,128)(2,1)S(1)} %bitcast.15, ...), custom_call_target="tpu_custom_call" | custom-call | flops 3623878656 | bytes 12582912 | tf_op jit(solution)/shard_map/expert/pallas_call | solution.py:293
  43.0 0.0 copy-start
  43.0 0.0 copy-start.4
  43.1 0.0 copy-start.6
  43.1 28.6 %all_to_all.21 = bf16[128,24,256]{2,1,0:T(8,128)(2,1)S(1)} all-to-all(bf16[128,24,256]{2,1,0:T(8,128)(2,1)S(1)} %bitcast.22), channel_id=1, replica_groups=mesh['dp'=8,'expert'=16] {'dp','expert'}, dimensions={0} | all-to-all | bytes 3145728 | tf_op jit(solution)/shard_map/all_to_all | solution.py:319
  71.6 1.5 %middle.1 = (bf16[384,8,256]{2,1,0:T(8,128)(2,1)S(1)}, bf16[256,256]{1,0:T(8,128)(2,1)S(1)}, bf16[64,384]{1,0:T(8,128)(2,1)S(1)}) custom-call(s32[1,8,32]{2,1,0:T(8,128)S(1)} %get-tuple-element.10.slots_in, f32[2,8,32]{2,1,0:T(8,128)S(1)} %bitcast.32, bf16[384,8,256]{2,1,0:T(8,128)(2,1)S(1)} %bitcast.16, bf16[32,2048]{1,0:T(8,128)(2,1)S(1)} %copy-done, ...), custom_call_target="tpu_custom_call" | custom-call | tf_op jit(solution)/shard_map/middle/pallas_call | solution.py:367
  73.1 28.5 %all_to_all.22 = bf16[128,24,256]{2,1,0:T(8,128)(2,1)S(1)} all-to-all(bf16[128,24,256]{2,1,0:T(8,128)(2,1)S(1)} %bitcast.21), channel_id=1, replica_groups=mesh['dp'=8,'expert'=16] {'dp','expert'}, dimensions={0} | all-to-all | bytes 3145728 | tf_op jit(solution)/shard_map/all_to_all | solution.py:319
  101.6 4.8 %expert.3 = bf16[3072,256]{1,0:T(8,128)(2,1)S(1)} custom-call(f32[2,12,1,16]{3,2,1,0:T(1,128)S(1)} %bitcast.29, f32[2,6,1,16]{3,2,1,0:T(1,128)S(1)} %bitcast.31, bf16[3072,256]{1,0:T(8,128)(2,1)S(1)} %bitcast.19, bf16[2,1,2048,1536]{3,2,1,0:T(8,128)(2,1)S(1)} %bitcast.13, bf16[2,1,768,2048]{3,2,1,0:T(8,128)(2,1)S(1)} %bitcast.15, s32[2,8,32]{2,1,0:T(8,128)S(1)} %bitcast.27, ...), custom_call_target="tpu_custom_call" | custom-call | flops 3623878656 | bytes 12582912 | tf_op jit(solution)/shard_map/expert/pallas_call | solution.py:293
  106.4 28.5 %all_to_all.23 = bf16[128,24,256]{2,1,0:T(8,128)(2,1)S(1)} all-to-all(bf16[128,24,256]{2,1,0:T(8,128)(2,1)S(1)} %bitcast.20), channel_id=1, replica_groups=mesh['dp'=8,'expert'=16] {'dp','expert'}, dimensions={0} | all-to-all | bytes 3145728 | tf_op jit(solution)/shard_map/all_to_all | solution.py:319
  134.9 1.6 %last.1 = bf16[32,2048]{1,0:T(8,128)(2,1)} custom-call(bf16[3072,256]{1,0:T(8,128)(2,1)S(1)} %bitcast.17, bf16[256,256]{1,0:T(8,128)(2,1)S(1)} %get-tuple-element.13.blocks_ref, bf16[64,384]{1,0:T(8,128)(2,1)S(1)} %get-tuple-element.14.weight_ref), custom_call_target="tpu_custom_call" | custom-call | tf_op jit(solution)/shard_map/last/pallas_call | solution.py:393
  (11 shorter events, 0.0 us)
Async XLA Ops:
  0.0 38.0 %slice-start = ((s8[12582912]{0:T(1024)(128)(4,1)}), s8[4194304]{0:T(1024)(128)(4,1)S(1)}, s32[]{:S(2)}) async-start(s8[12582912]{0:T(1024)(128)(4,1)} %bitcast.12), calls=%async_computation.4 | async-start | bytes 8388608
  0.0 38.0 %slice-start.3 = ((s8[6291456]{0:T(1024)(128)(4,1)}), s8[4194304]{0:T(1024)(128)(4,1)S(1)}, s32[]{:S(2)}) async-start(s8[6291456]{0:T(1024)(128)(4,1)} %bitcast.14), calls=%async_computation.7 | async-start | bytes 8388608
  0.0 38.0 %slice-start.1 = ((s8[12582912]{0:T(1024)(128)(4,1)}), s8[4194304]{0:T(1024)(128)(4,1)S(1)}, s32[]{:S(2)}) async-start(s8[12582912]{0:T(1024)(128)(4,1)} %bitcast.12), calls=%async_computation.5 | async-start | bytes 8388608
  0.0 38.0 %slice-start.2 = ((s8[12582912]{0:T(1024)(128)(4,1)}), s8[4194304]{0:T(1024)(128)(4,1)S(1)}, s32[]{:S(2)}) async-start(s8[12582912]{0:T(1024)(128)(4,1)} %bitcast.12), calls=%async_computation.6 | async-start | bytes 8388608
  0.0 38.0 %slice-start.4 = ((s8[6291456]{0:T(1024)(128)(4,1)}), s8[2097152]{0:T(1024)(128)(4,1)S(1)}, s32[]{:S(2)}) async-start(s8[6291456]{0:T(1024)(128)(4,1)} %bitcast.14), calls=%async_computation.8 | async-start | bytes 4194304
  2.5 35.5 %copy-start.1 = (s32[2,32,8]{1,2,0:T(8,128)S(1)}, s32[2,32,8]{1,2,0:T(8,128)}, u32[]{:S(2)}) copy-start(s32[2,32,8]{1,2,0:T(8,128)} %param.11) | copy-start | bytes 6148
  2.5 35.5 %copy-start.2 = (f32[2,1,16,12]{2,1,3,0:T(1,128)S(1)}, f32[2,1,16,12]{2,1,3,0:T(1,128)}, u32[]{:S(2)}) copy-start(f32[2,1,16,12]{2,1,3,0:T(1,128)} %param.15) | copy-start | bytes 4612
  2.5 35.5 %copy-start.3 = (f32[2,1,6,16]{3,1,2,0:T(1,128)S(1)}, f32[2,1,6,16]{3,1,2,0:T(1,128)}, u32[]{:S(2)}) copy-start(f32[2,1,6,16]{3,1,2,0:T(1,128)} %param.17) | copy-start | bytes 2308
  2.5 35.5 %copy-start.5 = (s32[2,128]{1,0:T(2,128)S(1)}, s32[2,128]{1,0:T(2,128)}, u32[]{:S(2)}) copy-start(s32[2,128]{1,0:T(2,128)} %place_ref.5) | copy-start | bytes 3076
  43.0 28.6 %copy-start = (bf16[32,2048]{1,0:T(8,128)(2,1)S(1)}, bf16[32,2048]{1,0:T(8,128)(2,1)}, u32[]{:S(2)}) copy-start(bf16[32,2048]{1,0:T(8,128)(2,1)} %stream_ref.1) | copy-start | bytes 393220
  43.0 28.6 %copy-start.4 = (f32[2,2048]{1,0:T(2,128)S(1)}, f32[2,2048]{1,0:T(2,128)}, u32[]{:S(2)}) copy-start(f32[2,2048]{1,0:T(2,128)} %gain_ref.1) | copy-start | bytes 49156
  43.1 28.6 %copy-start.6 = (f32[2,32,8]{1,2,0:T(8,128)S(1)}, f32[2,32,8]{1,2,0:T(8,128)}, u32[]{:S(2)}) copy-start(f32[2,32,8]{1,2,0:T(8,128)} %param.12) | copy-start | bytes 6148
